TPU v7x, 32 devices: a whole 2x2x4 slice. The times are simulated.
32 devices in a mesh: tm: 4 (over y, core), slab: 2 (over x), coarse: 4 (over z).
Axes of the slice: x: 2, y: 2, z: 4, core: 2. Of those that a mesh axis runs over, the one named last changes fastest.
Arguments:
- states: float32 [4, 8, 64, 256], P('tm', 'slab', 'coarse'), may hold values from -6 to 6
- diffusivity: float32 [8, 64, 256], P('slab', 'coarse'), may hold values from 0.25 to 2
- velocity: float32 [3, 8, 64, 256], P(None, 'slab', 'coarse'), may hold values from -0.5 to 0.5
Outputs:
- new_states: float32 [4, 8, 64, 256], P('tm', 'slab', 'coarse')
All inputs are finite; a program needn't handle non-finite values.
Results may differ from a plain program's by a relative error of at most 0.0001.
Values sent between devices are 32-bit elements; how exact they have to be, the bound alone decides.
No kernel may reach another device: no remote copies, remote signals or barrier semaphores. Data moves between devices by JAX's collectives and lax.ppermute only.
A program may use at most 64 MiB of HBM per device.

v0:
```python
import jax
import jax.numpy as jnp
from jax import lax
from jax.sharding import PartitionSpec as P

SECTIONS = 4
FINE_STEPS = 2


fine_step = 1.0
relaxation = 0.8


def extended(block, sides, width):
    for axis, dim in sides:
        count = lax.axis_size(axis)
        forward = [(i, i + 1) for i in range(count - 1)]
        backward = [(target, source) for source, target in forward]
        low = lax.ppermute(
            lax.slice_in_dim(block, block.shape[dim] - width, None, axis=dim), axis, forward
        )
        high = lax.ppermute(lax.slice_in_dim(block, 0, width, axis=dim), axis, backward)
        block = jnp.concatenate([low, block, high], axis=dim)
    return block


def passed_along(block, axis, distance):
    devices = range(lax.axis_size(axis))
    route = [(i - distance, i) for i in devices if i - distance in devices]
    return lax.ppermute(block, axis, route)


def chebyshev_coefficients(sections):
    damping = 0.05
    centre_point = 1.0 + damping / (sections * sections)
    chebyshev = [1.0, centre_point]
    slopes = [0.0, 1.0]
    for degree in range(2, sections + 1):
        chebyshev.append(2.0 * centre_point * chebyshev[degree - 1] - chebyshev[degree - 2])
        slopes.append(
            2.0 * chebyshev[degree - 1]
            + 2.0 * centre_point * slopes[degree - 1]
            - slopes[degree - 2]
        )
    slope_ratio = chebyshev[sections] / slopes[sections]
    weights = [1.0 / entry for entry in chebyshev]
    scales = [0.0, 0.0]
    carries = [0.0, 0.0]
    tildes = [0.0, slope_ratio / centre_point]
    for degree in range(2, sections + 1):
        scales.append(2.0 * weights[degree] * centre_point / weights[degree - 1])
        carries.append(-weights[degree] / weights[degree - 2])
        tildes.append(2.0 * weights[degree] * slope_ratio / weights[degree - 1])
    return (scales, carries, tildes)


def stencil(padded, coeffs, spacing):
    centre = padded[1:-1, 1:-1, 1:-1]
    depth_after = padded[2:, 1:-1, 1:-1]
    depth_before = padded[:-2, 1:-1, 1:-1]
    row_after = padded[1:-1, 2:, 1:-1]
    row_before = padded[1:-1, :-2, 1:-1]
    column_after = padded[1:-1, 1:-1, 2:]
    column_before = padded[1:-1, 1:-1, :-2]
    beside_all = depth_after + depth_before + row_after + row_before + column_after + column_before
    spread = coeffs[0] * (beside_all - 6.0 * centre) / (spacing * spacing)
    drifts = (
        coeffs[1] * (depth_after - depth_before)
        + coeffs[2] * (row_after - row_before)
        + coeffs[3] * (column_after - column_before)
    ) / (2.0 * spacing)
    return spread - drifts


def shrink(values):
    return values.reshape(
        values.shape[0] // 2, 2, values.shape[1] // 2, 2, values.shape[2] // 2, 2
    ).mean(axis=(1, 3, 5))


def expand(values):
    return jnp.repeat(jnp.repeat(jnp.repeat(values, 2, 0), 2, 1), 2, 2)


def pad_columns(values):
    return jnp.pad(values, ((0, 0), (0, 0), (1, 1)))


def trim(values, amount):
    return values[..., amount : values.shape[-3] - amount, amount : values.shape[-2] - amount, :]


def solve_padding(values):
    return pad_columns(extended(values, (("slab", 0), ("coarse", 1)), 1))


def coarse_padding(values):
    return pad_columns(extended(values, (("slab", 0), ("coarse", 1)), 1))


def coarse_step(source, coeffs, coarse_coeffs):
    interval = FINE_STEPS * fine_step
    diagonal = 1.0 + 6.0 * interval * coeffs[0]

    def misfit(trial):
        return source - (trial - interval * stencil(solve_padding(trial), coeffs, 1.0))

    smoothed = source + relaxation * misfit(source) / diagonal
    coarse_source = shrink(misfit(smoothed))
    coarse_diagonal = 1.0 + 6.0 * interval * coarse_coeffs[0] / 4.0
    guess_one = relaxation * coarse_source / coarse_diagonal
    coarse_misfit = coarse_source - (
        guess_one - interval * stencil(coarse_padding(guess_one), coarse_coeffs, 2.0)
    )
    guess_two = guess_one + relaxation * coarse_misfit / coarse_diagonal
    second = smoothed + expand(guess_two)
    return second + relaxation * misfit(second) / diagonal


def fine_deep(start_field, coeffs):
    scales, carries, tildes = chebyshev_coefficients(SECTIONS)
    ghost_width = SECTIONS
    wide_coeffs = extended(coeffs, (("slab", 1), ("coarse", 2)), ghost_width)
    depth_cells = start_field.shape[0]
    row_cells = start_field.shape[1]
    first_depth = lax.axis_index("slab") * depth_cells
    first_row = lax.axis_index("coarse") * row_cells
    total_depth = depth_cells * lax.axis_size("slab")
    total_rows = row_cells * lax.axis_size("coarse")
    for repeat in range(FINE_STEPS):
        widened = extended(start_field, (("slab", 0), ("coarse", 1)), ghost_width)
        before = widened
        current = widened
        for degree in range(1, SECTIONS + 1):
            margin = ghost_width - degree
            change = stencil(pad_columns(current), trim(wide_coeffs, ghost_width - margin), 1.0)
            if degree == 1:
                update = trim(current, 1) + tildes[1] * fine_step * change
            else:
                update = (
                    scales[degree] * trim(current, 1)
                    + carries[degree] * trim(before, 2)
                    + tildes[degree] * fine_step * change
                )
            depth_index = (
                first_depth - margin + jnp.arange(depth_cells + 2 * margin, dtype=jnp.int32)
            )
            row_index = first_row - margin + jnp.arange(row_cells + 2 * margin, dtype=jnp.int32)
            depth_valid = (depth_index >= 0) & (depth_index < total_depth)
            row_valid = (row_index >= 0) & (row_index < total_rows)
            before, current = (
                current,
                update
                * (depth_valid[:, None, None] & row_valid[None, :, None]).astype(jnp.float32),
            )
        start_field = current
    return start_field


def per_device(states, diffusivity, velocity):
    coeffs = jnp.concatenate([diffusivity[None], velocity], 0)
    coarse_coeffs = jnp.stack([shrink(coeffs[number]) for number in range(4)])
    own_start = states[0]
    fine_end = fine_deep(own_start, coeffs)
    coarse_old = coarse_step(own_start, coeffs, coarse_coeffs)
    corrections = fine_end - coarse_old
    position = lax.axis_index("tm")
    window_count = lax.axis_size("tm")
    current = coarse_old + corrections
    result = current
    for turn_number in range(1, window_count):
        incoming = passed_along(current, "tm", 1)
        current = coarse_step(incoming, coeffs, coarse_coeffs) + corrections
        result = jnp.where(position == turn_number, current, result)
    return result[None]


def solution(mesh):
    return jax.shard_map(
        per_device,
        mesh=mesh,
        in_specs=(
            P("tm", "slab", "coarse", None),
            P("slab", "coarse", None),
            P(None, "slab", "coarse", None),
        ),
        out_specs=P("tm", "slab", "coarse", None),
        check_vma=False,
    )
```

profile of v0, /device:TPU:30, one launch (start us, length us, event | category | flops | bytes accessed | tf_op | source)
XLA Modules:
  0.0 367.0 jit_solution(12859345116133894671)
XLA Ops:
  1.4 4.6 %collective-permute-start.17 = (f32[4,16,256]{2,1,0:T(8,128)}, f32[4,16,256]{2,1,0:T(8,128)S(1)}, u32[]{:S(2)}, u32[]{:S(2)}) collective-permute-start(f32[4,16,256]{2,1,0:T(8,128)} %bitcast.430), channel_id=1, source_target_pairs={{4,0},{5,1},{6,2},{7,3},{12,8},{13,9},{14,10},{15,11},{20,16},{21,... | collective-permute-start | bytes 196616 | tf_op jit(solution)/shard_map/ppermute | solution.py:22
  18.2 4.2 %collective-permute-done.3 = f32[6,1,256]{2,1,0:T(1,128)S(1)} collective-permute-done((f32[6,1,256]{2,1,0:T(1,128)S(1)}, f32[6,1,256]{2,1,0:T(1,128)S(1)}, u32[]{:S(2)}, u32[]{:S(2)}) %collective-permute-start.3) | collective-permute-done | bytes 6176 | tf_op jit(solution)/shard_map/ppermute | solution.py:19
  27.8 4.2 %collective-permute-done.5 = f32[1,16,256]{2,1,0:T(8,128)S(1)} collective-permute-done((f32[1,16,256]{2,1,0:T(8,128)S(1)}, f32[1,16,256]{2,1,0:T(8,128)S(1)}, u32[]{:S(2)}, u32[]{:S(2)}) %collective-permute-start.5) | collective-permute-done | bytes 16416 | tf_op jit(solution)/shard_map/ppermute | solution.py:19
  35.7 5.6 %reshape_squeeze_broadcast_in_dim.3 = f32[2,2,8,2,128,2]{5,4,3,2,1,0:T(8,128)} reshape(f32[4,16,256]{2,1,0:T(8,128)S(1)} %copy-done.1) | data formatting | bytes 131072 | tf_op jit(solution)/shard_map/reshape;squeeze;broadcast_in_dim | solution.py:76
  44.1 5.6 %reshape.242 = f32[2,2,8,2,128,2]{5,4,3,2,1,0:T(8,128)} reshape(f32[4,16,256]{2,1,0:T(8,128)S(1)} %fusion.41) | data formatting | bytes 131072 | tf_op jit(solution)/shard_map/reshape | solution.py:76
  59.3 4.5 %collective-permute-start.10 = (f32[4,1,128]{2,1,0:T(1,128)S(1)}, f32[4,1,128]{2,1,0:T(1,128)S(1)}, u32[]{:S(2)}, u32[]{:S(2)}) collective-permute-start(f32[4,1,128]{2,1,0:T(1,128)S(1)} %get-tuple-element.71), channel_id=1, source_target_pairs={{1,0},{2,1},{3,2},{5,4},{6,5},{7,6},{9,8},{10,9},{11,10},{13,12},{... | collective-permute-start | bytes 6152 | tf_op jit(solution)/shard_map/ppermute | solution.py:22
  65.3 5.5 %reshape_squeeze.9 = f32[2,2,8,2,128,2]{5,4,3,2,1,0:T(8,128)} reshape(f32[1,4,16,256]{3,2,1,0:T(8,128)S(1)} %get-tuple-element.13) | data formatting | bytes 131072 | tf_op jit(solution)/shard_map/reshape;squeeze | solution.py:76
  73.3 5.6 %reshape_squeeze.10 = f32[2,2,8,2,128,2]{5,4,3,2,1,0:T(8,128)} reshape(f32[1,4,16,256]{3,2,1,0:T(8,128)S(1)} %get-tuple-element.14) | data formatting | bytes 131072 | tf_op jit(solution)/shard_map/reshape;squeeze | solution.py:76
  81.4 5.6 %reshape_squeeze.11 = f32[2,2,8,2,128,2]{5,4,3,2,1,0:T(8,128)} reshape(f32[1,4,16,256]{3,2,1,0:T(8,128)S(1)} %get-tuple-element.15) | data formatting | bytes 131072 | tf_op jit(solution)/shard_map/reshape;squeeze | solution.py:76
  93.3 5.2 %collective-permute-start.19 = (f32[12,4,256]{2,1,0:T(4,128)S(1)}, f32[12,4,256]{2,1,0:T(4,128)S(1)}, u32[]{:S(2)}, u32[]{:S(2)}) collective-permute-start(f32[12,4,256]{2,1,0:T(4,128)S(1)} %get-tuple-element.12), channel_id=1, source_target_pairs={{1,0},{2,1},{3,2},{5,4},{6,5},{7,6},{9,8},{10,9},{11,10},{13,12},{... | collective-permute-start | bytes 147464 | tf_op jit(solution)/shard_map/ppermute | solution.py:22
  99.9 4.6 %collective-permute-start.23 = (f32[4,12,4,256]{3,2,1,0:T(4,128)S(1)}, f32[4,12,4,256]{3,2,1,0:T(4,128)S(1)}, u32[]{:S(2)}, u32[]{:S(2)}) collective-permute-start(f32[4,12,4,256]{3,2,1,0:T(4,128)S(1)} %get-tuple-element.8), channel_id=1, source_target_pairs={{1,0},{2,1},{3,2},{5,4},{6,5},{7,6},{9,8},{10,9},{11,10},{13,12},{... | collective-permute-start | bytes 589832 | tf_op jit(solution)/shard_map/ppermute | solution.py:22
  110.2 4.5 %collective-permute-start.25 = (f32[4,16,256]{2,1,0:T(8,128)S(1)}, f32[4,16,256]{2,1,0:T(8,128)S(1)}, u32[]{:S(2)}, u32[]{:S(2)}) collective-permute-start(f32[4,16,256]{2,1,0:T(8,128)S(1)} %fusion.31), channel_id=1, source_target_pairs={{4,0},{5,1},{6,2},{7,3},{12,8},{13,9},{14,10},{15,11},{20,16},{21,... | collective-permute-start | bytes 196616 | tf_op jit(solution)/shard_map/ppermute | solution.py:22
  114.8 4.4 %collective-permute-start.14 = (f32[6,1,256]{2,1,0:T(1,128)S(1)}, f32[6,1,256]{2,1,0:T(1,128)S(1)}, u32[]{:S(2)}, u32[]{:S(2)}) collective-permute-start(f32[6,1,256]{2,1,0:T(1,128)S(1)} %get-tuple-element.35), channel_id=1, source_target_pairs={{1,0},{2,1},{3,2},{5,4},{6,5},{7,6},{9,8},{10,9},{11,10},{13,12},{... | collective-permute-start | bytes 18440 | tf_op jit(solution)/shard_map/ppermute | solution.py:22
  121.8 5.2 %collective-permute-start.27 = (f32[12,4,256]{2,1,0:T(4,128)S(1)}, f32[12,4,256]{2,1,0:T(4,128)S(1)}, u32[]{:S(2)}, u32[]{:S(2)}) collective-permute-start(f32[12,4,256]{2,1,0:T(4,128)S(1)} %get-tuple-element.10), channel_id=1, source_target_pairs={{1,0},{2,1},{3,2},{5,4},{6,5},{7,6},{9,8},{10,9},{11,10},{13,12},{... | collective-permute-start | bytes 147464 | tf_op jit(solution)/shard_map/ppermute | solution.py:22
  136.9 4.5 %collective-permute-start.29 = (f32[1,16,256]{2,1,0:T(8,128)S(1)}, f32[1,16,256]{2,1,0:T(8,128)S(1)}, u32[]{:S(2)}, u32[]{:S(2)}) collective-permute-start(f32[1,16,256]{2,1,0:T(8,128)S(1)} %get-tuple-element.56), channel_id=1, source_target_pairs={{4,0},{5,1},{6,2},{7,3},{12,8},{13,9},{14,10},{15,11},{20,16},{21,... | collective-permute-start | bytes 49160 | tf_op jit(solution)/shard_map/ppermute | solution.py:22
  142.8 4.2 %collective-permute-start.31 = (f32[6,1,256]{2,1,0:T(1,128)S(1)}, f32[6,1,256]{2,1,0:T(1,128)S(1)}, u32[]{:S(2)}, u32[]{:S(2)}) collective-permute-start(f32[6,1,256]{2,1,0:T(1,128)S(1)} %get-tuple-element.33), channel_id=1, source_target_pairs={{1,0},{2,1},{3,2},{5,4},{6,5},{7,6},{9,8},{10,9},{11,10},{13,12},{... | collective-permute-start | bytes 18440 | tf_op jit(solution)/shard_map/ppermute | solution.py:22
  148.4 4.2 %collective-permute-done.32 = f32[6,1,256]{2,1,0:T(1,128)S(1)} collective-permute-done((f32[6,1,256]{2,1,0:T(1,128)S(1)}, f32[6,1,256]{2,1,0:T(1,128)S(1)}, u32[]{:S(2)}, u32[]{:S(2)}) %collective-permute-start.32) | collective-permute-done | bytes 6176 | tf_op jit(solution)/shard_map/ppermute | solution.py:19
  152.9 4.2 %collective-permute-start.33 = (f32[1,16,256]{2,1,0:T(8,128)S(1)}, f32[1,16,256]{2,1,0:T(8,128)S(1)}, u32[]{:S(2)}, u32[]{:S(2)}) collective-permute-start(f32[1,16,256]{2,1,0:T(8,128)S(1)} %get-tuple-element.55), channel_id=1, source_target_pairs={{4,0},{5,1},{6,2},{7,3},{12,8},{13,9},{14,10},{15,11},{20,16},{21,... | collective-permute-start | bytes 49160 | tf_op jit(solution)/shard_map/ppermute | solution.py:22
  158.6 4.2 %collective-permute-done.34 = f32[1,16,256]{2,1,0:T(8,128)S(1)} collective-permute-done((f32[1,16,256]{2,1,0:T(8,128)S(1)}, f32[1,16,256]{2,1,0:T(8,128)S(1)}, u32[]{:S(2)}, u32[]{:S(2)}) %collective-permute-start.34) | collective-permute-done | bytes 16416 | tf_op jit(solution)/shard_map/ppermute | solution.py:19
  168.0 4.2 %collective-permute-done.36 = f32[6,1,256]{2,1,0:T(1,128)S(1)} collective-permute-done((f32[6,1,256]{2,1,0:T(1,128)S(1)}, f32[6,1,256]{2,1,0:T(1,128)S(1)}, u32[]{:S(2)}, u32[]{:S(2)}) %collective-permute-start.36) | collective-permute-done | bytes 6176 | tf_op jit(solution)/shard_map/ppermute | solution.py:19
  172.5 5.6 %reshape.246 = f32[2,2,8,2,128,2]{5,4,3,2,1,0:T(8,128)} reshape(f32[4,16,256]{2,1,0:T(8,128)S(1)} %fusion.68) | data formatting | bytes 131072 | tf_op jit(solution)/shard_map/reshape | solution.py:76
  201.0 4.2 %collective-permute-done.42 = f32[1,16,256]{2,1,0:T(8,128)S(1)} collective-permute-done((f32[1,16,256]{2,1,0:T(8,128)S(1)}, f32[1,16,256]{2,1,0:T(8,128)S(1)}, u32[]{:S(2)}, u32[]{:S(2)}) %collective-permute-start.42) | collective-permute-done | bytes 16416 | tf_op jit(solution)/shard_map/ppermute | solution.py:19
  219.9 4.5 %collective-permute-start.46 = (f32[1,16,256]{2,1,0:T(8,128)S(1)}, f32[1,16,256]{2,1,0:T(8,128)S(1)}, u32[]{:S(2)}, u32[]{:S(2)}) collective-permute-start(f32[1,16,256]{2,1,0:T(8,128)S(1)} %get-tuple-element.50), channel_id=1, source_target_pairs={{4,0},{5,1},{6,2},{7,3},{12,8},{13,9},{14,10},{15,11},{20,16},{21,... | collective-permute-start | bytes 49160 | tf_op jit(solution)/shard_map/ppermute | solution.py:22
  233.6 4.2 %collective-permute-start.50 = (f32[1,16,256]{2,1,0:T(8,128)S(1)}, f32[1,16,256]{2,1,0:T(8,128)S(1)}, u32[]{:S(2)}, u32[]{:S(2)}) collective-permute-start(f32[1,16,256]{2,1,0:T(8,128)S(1)} %get-tuple-element.49), channel_id=1, source_target_pairs={{4,0},{5,1},{6,2},{7,3},{12,8},{13,9},{14,10},{15,11},{20,16},{21,... | collective-permute-start | bytes 49160 | tf_op jit(solution)/shard_map/ppermute | solution.py:22
  239.2 4.2 %collective-permute-done.51 = f32[1,16,256]{2,1,0:T(8,128)S(1)} collective-permute-done((f32[1,16,256]{2,1,0:T(8,128)S(1)}, f32[1,16,256]{2,1,0:T(8,128)S(1)}, u32[]{:S(2)}, u32[]{:S(2)}) %collective-permute-start.51) | collective-permute-done | bytes 16416 | tf_op jit(solution)/shard_map/ppermute | solution.py:19
  251.2 5.6 %reshape.250 = f32[2,2,8,2,128,2]{5,4,3,2,1,0:T(8,128)} reshape(f32[4,16,256]{2,1,0:T(8,128)S(1)} %fusion.88) | data formatting | bytes 131072 | tf_op jit(solution)/shard_map/reshape | solution.py:76
  277.7 4.2 %collective-permute-done.59 = f32[1,16,256]{2,1,0:T(8,128)S(1)} collective-permute-done((f32[1,16,256]{2,1,0:T(8,128)S(1)}, f32[1,16,256]{2,1,0:T(8,128)S(1)}, u32[]{:S(2)}, u32[]{:S(2)}) %collective-permute-start.59) | collective-permute-done | bytes 16416 | tf_op jit(solution)/shard_map/ppermute | solution.py:19
  296.5 4.5 %collective-permute-start.63 = (f32[1,16,256]{2,1,0:T(8,128)S(1)}, f32[1,16,256]{2,1,0:T(8,128)S(1)}, u32[]{:S(2)}, u32[]{:S(2)}) collective-permute-start(f32[1,16,256]{2,1,0:T(8,128)S(1)} %get-tuple-element.44), channel_id=1, source_target_pairs={{4,0},{5,1},{6,2},{7,3},{12,8},{13,9},{14,10},{15,11},{20,16},{21,... | collective-permute-start | bytes 49160 | tf_op jit(solution)/shard_map/ppermute | solution.py:22
  310.3 4.2 %collective-permute-start.67 = (f32[1,16,256]{2,1,0:T(8,128)S(1)}, f32[1,16,256]{2,1,0:T(8,128)S(1)}, u32[]{:S(2)}, u32[]{:S(2)}) collective-permute-start(f32[1,16,256]{2,1,0:T(8,128)S(1)} %get-tuple-element.43), channel_id=1, source_target_pairs={{4,0},{5,1},{6,2},{7,3},{12,8},{13,9},{14,10},{15,11},{20,16},{21,... | collective-permute-start | bytes 49160 | tf_op jit(solution)/shard_map/ppermute | solution.py:22
  315.9 4.2 %collective-permute-done.68 = f32[1,16,256]{2,1,0:T(8,128)S(1)} collective-permute-done((f32[1,16,256]{2,1,0:T(8,128)S(1)}, f32[1,16,256]{2,1,0:T(8,128)S(1)}, u32[]{:S(2)}, u32[]{:S(2)}) %collective-permute-start.68) | collective-permute-done | bytes 16416 | tf_op jit(solution)/shard_map/ppermute | solution.py:19
  327.9 5.6 %reshape.254 = f32[2,2,8,2,128,2]{5,4,3,2,1,0:T(8,128)} reshape(f32[4,16,256]{2,1,0:T(8,128)S(1)} %fusion.108) | data formatting | bytes 131072 | tf_op jit(solution)/shard_map/reshape | solution.py:76
  354.4 4.2 %collective-permute-done.76 = f32[1,16,256]{2,1,0:T(8,128)S(1)} collective-permute-done((f32[1,16,256]{2,1,0:T(8,128)S(1)}, f32[1,16,256]{2,1,0:T(8,128)S(1)}, u32[]{:S(2)}, u32[]{:S(2)}) %collective-permute-start.76) | collective-permute-done | bytes 16416 | tf_op jit(solution)/shard_map/ppermute | solution.py:19
  (276 shorter events, 215.6 us)
Async XLA Ops:
  0.0 91.9 %collective-permute-start.16 = (f32[4,16,256]{2,1,0:T(8,128)}, f32[4,16,256]{2,1,0:T(8,128)S(1)}, u32[]{:S(2)}, u32[]{:S(2)}) collective-permute-start(f32[4,16,256]{2,1,0:T(8,128)} %bitcast.429), channel_id=1, source_target_pairs={{0,4},{1,5},{2,6},{3,7},{8,12},{9,13},{10,14},{11,15},{16,20},{17,... | collective-permute-start | bytes 196616 | tf_op jit(solution)/shard_map/ppermute | solution.py:19
  1.4 90.5 %collective-permute-start.17 = (f32[4,16,256]{2,1,0:T(8,128)}, f32[4,16,256]{2,1,0:T(8,128)S(1)}, u32[]{:S(2)}, u32[]{:S(2)}) collective-permute-start(f32[4,16,256]{2,1,0:T(8,128)} %bitcast.430), channel_id=1, source_target_pairs={{4,0},{5,1},{6,2},{7,3},{12,8},{13,9},{14,10},{15,11},{20,16},{21,... | collective-permute-start | bytes 196616 | tf_op jit(solution)/shard_map/ppermute | solution.py:22
  6.8 6.0 %collective-permute-start = (f32[1,16,256]{2,1,0:T(8,128)S(1)}, f32[1,16,256]{2,1,0:T(8,128)S(1)}, u32[]{:S(2)}, u32[]{:S(2)}) collective-permute-start(f32[1,16,256]{2,1,0:T(8,128)S(1)} %get-tuple-element.63), channel_id=1, source_target_pairs={{4,0},{5,1},{6,2},{7,3},{12,8},{13,9},{14,10},{15,11},{20,16},{21,... | collective-permute-start | bytes 49160 | tf_op jit(solution)/shard_map/ppermute | solution.py:22
  10.3 88.2 %collective-permute-start.20 = (f32[4,4,16,256]{3,2,1,0:T(8,128)S(1)}, f32[4,4,16,256]{3,2,1,0:T(8,128)S(1)}, u32[]{:S(2)}, u32[]{:S(2)}) collective-permute-start(f32[4,4,16,256]{3,2,1,0:T(8,128)S(1)} %pad_maximum_fusion.3), channel_id=1, source_target_pairs={{0,4},{1,5},{2,6},{3,7},{8,12},{9,13},{10,14},{11,15},{16,20},{17,... | collective-permute-start | bytes 786440 | tf_op jit(solution)/shard_map/ppermute | solution.py:19
  32.0 11.8 %collective-permute-start.6 = (f32[6,1,256]{2,1,0:T(1,128)S(1)}, f32[6,1,256]{2,1,0:T(1,128)S(1)}, u32[]{:S(2)}, u32[]{:S(2)}) collective-permute-start(f32[6,1,256]{2,1,0:T(1,128)S(1)} %get-tuple-element.37), channel_id=1, source_target_pairs={{1,0},{2,1},{3,2},{5,4},{6,5},{7,6},{9,8},{10,9},{11,10},{13,12},{... | collective-permute-start | bytes 18440 | tf_op jit(solution)/shard_map/ppermute | solution.py:22
  34.4 9.4 %collective-permute-start.7 = (f32[6,1,256]{2,1,0:T(1,128)S(1)}, f32[6,1,256]{2,1,0:T(1,128)S(1)}, u32[]{:S(2)}, u32[]{:S(2)}) collective-permute-start(f32[6,1,256]{2,1,0:T(1,128)S(1)} %get-tuple-element.36), channel_id=1, source_target_pairs={{0,1},{1,2},{2,3},{4,5},{5,6},{6,7},{8,9},{9,10},{10,11},{12,13},{... | collective-permute-start | bytes 18440 | tf_op jit(solution)/shard_map/ppermute | solution.py:19
  59.3 30.2 %collective-permute-start.10 = (f32[4,1,128]{2,1,0:T(1,128)S(1)}, f32[4,1,128]{2,1,0:T(1,128)S(1)}, u32[]{:S(2)}, u32[]{:S(2)}) collective-permute-start(f32[4,1,128]{2,1,0:T(1,128)S(1)} %get-tuple-element.71), channel_id=1, source_target_pairs={{1,0},{2,1},{3,2},{5,4},{6,5},{7,6},{9,8},{10,9},{11,10},{13,12},{... | collective-permute-start | bytes 6152 | tf_op jit(solution)/shard_map/ppermute | solution.py:22
  63.9 27.3 %collective-permute-start.11 = (f32[4,1,128]{2,1,0:T(1,128)S(1)}, f32[4,1,128]{2,1,0:T(1,128)S(1)}, u32[]{:S(2)}, u32[]{:S(2)}) collective-permute-start(f32[4,1,128]{2,1,0:T(1,128)S(1)} %get-tuple-element.70), channel_id=1, source_target_pairs={{0,1},{1,2},{2,3},{4,5},{5,6},{6,7},{8,9},{9,10},{10,11},{12,13},{... | collective-permute-start | bytes 6152 | tf_op jit(solution)/shard_map/ppermute | solution.py:19
  89.5 9.0 %collective-permute-start.21 = (f32[4,4,16,256]{3,2,1,0:T(8,128)S(1)}, f32[4,4,16,256]{3,2,1,0:T(8,128)S(1)}, u32[]{:S(2)}, u32[]{:S(2)}) collective-permute-start(f32[4,4,16,256]{3,2,1,0:T(8,128)S(1)} %pad_maximum_fusion.3), channel_id=1, source_target_pairs={{4,0},{5,1},{6,2},{7,3},{12,8},{13,9},{14,10},{15,11},{20,16},{21,... | collective-permute-start | bytes 786440 | tf_op jit(solution)/shard_map/ppermute | solution.py:22
  92.0 14.0 %collective-permute-start.18 = (f32[12,4,256]{2,1,0:T(4,128)S(1)}, f32[12,4,256]{2,1,0:T(4,128)S(1)}, u32[]{:S(2)}, u32[]{:S(2)}) collective-permute-start(f32[12,4,256]{2,1,0:T(4,128)S(1)} %get-tuple-element.11), channel_id=1, source_target_pairs={{0,1},{1,2},{2,3},{4,5},{5,6},{6,7},{8,9},{9,10},{10,11},{12,13},{... | collective-permute-start | bytes 147464 | tf_op jit(solution)/shard_map/ppermute | solution.py:19
  93.3 14.2 %collective-permute-start.19 = (f32[12,4,256]{2,1,0:T(4,128)S(1)}, f32[12,4,256]{2,1,0:T(4,128)S(1)}, u32[]{:S(2)}, u32[]{:S(2)}) collective-permute-start(f32[12,4,256]{2,1,0:T(4,128)S(1)} %get-tuple-element.12), channel_id=1, source_target_pairs={{1,0},{2,1},{3,2},{5,4},{6,5},{7,6},{9,8},{10,9},{11,10},{13,12},{... | collective-permute-start | bytes 147464 | tf_op jit(solution)/shard_map/ppermute | solution.py:22
  98.6 9.0 %collective-permute-start.22 = (f32[4,12,4,256]{3,2,1,0:T(4,128)S(1)}, f32[4,12,4,256]{3,2,1,0:T(4,128)S(1)}, u32[]{:S(2)}, u32[]{:S(2)}) collective-permute-start(f32[4,12,4,256]{3,2,1,0:T(4,128)S(1)} %get-tuple-element.7), channel_id=1, source_target_pairs={{0,1},{1,2},{2,3},{4,5},{5,6},{6,7},{8,9},{9,10},{10,11},{12,13},{... | collective-permute-start | bytes 589832 | tf_op jit(solution)/shard_map/ppermute | solution.py:19
  99.9 7.7 %collective-permute-start.23 = (f32[4,12,4,256]{3,2,1,0:T(4,128)S(1)}, f32[4,12,4,256]{3,2,1,0:T(4,128)S(1)}, u32[]{:S(2)}, u32[]{:S(2)}) collective-permute-start(f32[4,12,4,256]{3,2,1,0:T(4,128)S(1)} %get-tuple-element.8), channel_id=1, source_target_pairs={{1,0},{2,1},{3,2},{5,4},{6,5},{7,6},{9,8},{10,9},{11,10},{13,12},{... | collective-permute-start | bytes 589832 | tf_op jit(solution)/shard_map/ppermute | solution.py:22
  104.5 10.3 %collective-permute-start.12 = (f32[1,16,256]{2,1,0:T(8,128)S(1)}, f32[1,16,256]{2,1,0:T(8,128)S(1)}, u32[]{:S(2)}, u32[]{:S(2)}) collective-permute-start(f32[1,16,256]{2,1,0:T(8,128)S(1)} %get-tuple-element.59), channel_id=1, source_target_pairs={{4,0},{5,1},{6,2},{7,3},{12,8},{13,9},{14,10},{15,11},{20,16},{21,... | collective-permute-start | bytes 49160 | tf_op jit(solution)/shard_map/ppermute | solution.py:22
  106.1 8.7 %collective-permute-start.13 = (f32[1,16,256]{2,1,0:T(8,128)S(1)}, f32[1,16,256]{2,1,0:T(8,128)S(1)}, u32[]{:S(2)}, u32[]{:S(2)}) collective-permute-start(f32[1,16,256]{2,1,0:T(8,128)S(1)} %get-tuple-element.58), channel_id=1, source_target_pairs={{0,4},{1,5},{2,6},{3,7},{8,12},{9,13},{10,14},{11,15},{16,20},{17,... | collective-permute-start | bytes 49160 | tf_op jit(solution)/shard_map/ppermute | solution.py:19
  108.9 11.6 %collective-permute-start.24 = (f32[4,16,256]{2,1,0:T(8,128)S(1)}, f32[4,16,256]{2,1,0:T(8,128)S(1)}, u32[]{:S(2)}, u32[]{:S(2)}) collective-permute-start(f32[4,16,256]{2,1,0:T(8,128)S(1)} %fusion.31), channel_id=1, source_target_pairs={{0,4},{1,5},{2,6},{3,7},{8,12},{9,13},{10,14},{11,15},{16,20},{17,... | collective-permute-start | bytes 196616 | tf_op jit(solution)/shard_map/ppermute | solution.py:19
  110.2 10.3 %collective-permute-start.25 = (f32[4,16,256]{2,1,0:T(8,128)S(1)}, f32[4,16,256]{2,1,0:T(8,128)S(1)}, u32[]{:S(2)}, u32[]{:S(2)}) collective-permute-start(f32[4,16,256]{2,1,0:T(8,128)S(1)} %fusion.31), channel_id=1, source_target_pairs={{4,0},{5,1},{6,2},{7,3},{12,8},{13,9},{14,10},{15,11},{20,16},{21,... | collective-permute-start | bytes 196616 | tf_op jit(solution)/shard_map/ppermute | solution.py:22
  114.8 12.2 %collective-permute-start.14 = (f32[6,1,256]{2,1,0:T(1,128)S(1)}, f32[6,1,256]{2,1,0:T(1,128)S(1)}, u32[]{:S(2)}, u32[]{:S(2)}) collective-permute-start(f32[6,1,256]{2,1,0:T(1,128)S(1)} %get-tuple-element.35), channel_id=1, source_target_pairs={{1,0},{2,1},{3,2},{5,4},{6,5},{7,6},{9,8},{10,9},{11,10},{13,12},{... | collective-permute-start | bytes 18440 | tf_op jit(solution)/shard_map/ppermute | solution.py:22
  119.2 7.9 %collective-permute-start.15 = (f32[6,1,256]{2,1,0:T(1,128)S(1)}, f32[6,1,256]{2,1,0:T(1,128)S(1)}, u32[]{:S(2)}, u32[]{:S(2)}) collective-permute-start(f32[6,1,256]{2,1,0:T(1,128)S(1)} %get-tuple-element.34), channel_id=1, source_target_pairs={{0,1},{1,2},{2,3},{4,5},{5,6},{6,7},{8,9},{9,10},{10,11},{12,13},{... | collective-permute-start | bytes 18440 | tf_op jit(solution)/shard_map/ppermute | solution.py:19
  120.5 6.7 %collective-permute-start.26 = (f32[12,4,256]{2,1,0:T(4,128)S(1)}, f32[12,4,256]{2,1,0:T(4,128)S(1)}, u32[]{:S(2)}, u32[]{:S(2)}) collective-permute-start(f32[12,4,256]{2,1,0:T(4,128)S(1)} %get-tuple-element.9), channel_id=1, source_target_pairs={{0,1},{1,2},{2,3},{4,5},{5,6},{6,7},{8,9},{9,10},{10,11},{12,13},{... | collective-permute-start | bytes 147464 | tf_op jit(solution)/shard_map/ppermute | solution.py:19
  121.8 6.9 %collective-permute-start.27 = (f32[12,4,256]{2,1,0:T(4,128)S(1)}, f32[12,4,256]{2,1,0:T(4,128)S(1)}, u32[]{:S(2)}, u32[]{:S(2)}) collective-permute-start(f32[12,4,256]{2,1,0:T(4,128)S(1)} %get-tuple-element.10), channel_id=1, source_target_pairs={{1,0},{2,1},{3,2},{5,4},{6,5},{7,6},{9,8},{10,9},{11,10},{13,12},{... | collective-permute-start | bytes 147464 | tf_op jit(solution)/shard_map/ppermute | solution.py:22
  135.6 5.8 %collective-permute-start.30 = (f32[1,16,256]{2,1,0:T(8,128)S(1)}, f32[1,16,256]{2,1,0:T(8,128)S(1)}, u32[]{:S(2)}, u32[]{:S(2)}) collective-permute-start(f32[1,16,256]{2,1,0:T(8,128)S(1)} %get-tuple-element.57), channel_id=1, source_target_pairs={{0,4},{1,5},{2,6},{3,7},{8,12},{9,13},{10,14},{11,15},{16,20},{17,... | collective-permute-start | bytes 49160 | tf_op jit(solution)/shard_map/ppermute | solution.py:19
  136.9 6.0 %collective-permute-start.29 = (f32[1,16,256]{2,1,0:T(8,128)S(1)}, f32[1,16,256]{2,1,0:T(8,128)S(1)}, u32[]{:S(2)}, u32[]{:S(2)}) collective-permute-start(f32[1,16,256]{2,1,0:T(8,128)S(1)} %get-tuple-element.56), channel_id=1, source_target_pairs={{4,0},{5,1},{6,2},{7,3},{12,8},{13,9},{14,10},{15,11},{20,16},{21,... | collective-permute-start | bytes 49160 | tf_op jit(solution)/shard_map/ppermute | solution.py:22
  152.9 5.6 %collective-permute-start.33 = (f32[1,16,256]{2,1,0:T(8,128)S(1)}, f32[1,16,256]{2,1,0:T(8,128)S(1)}, u32[]{:S(2)}, u32[]{:S(2)}) collective-permute-start(f32[1,16,256]{2,1,0:T(8,128)S(1)} %get-tuple-element.55), channel_id=1, source_target_pairs={{4,0},{5,1},{6,2},{7,3},{12,8},{13,9},{14,10},{15,11},{20,16},{21,... | collective-permute-start | bytes 49160 | tf_op jit(solution)/shard_map/ppermute | solution.py:22
  199.6 5.6 %collective-permute-start.42 = (f32[1,16,256]{2,1,0:T(8,128)S(1)}, f32[1,16,256]{2,1,0:T(8,128)S(1)}, u32[]{:S(2)}, u32[]{:S(2)}) collective-permute-start(f32[1,16,256]{2,1,0:T(8,128)S(1)} %get-tuple-element.52), channel_id=1, source_target_pairs={{0,4},{1,5},{2,6},{3,7},{8,12},{9,13},{10,14},{11,15},{16,20},{17,... | collective-permute-start | bytes 49160 | tf_op jit(solution)/shard_map/ppermute | solution.py:19
  218.6 5.8 %collective-permute-start.47 = (f32[1,16,256]{2,1,0:T(8,128)S(1)}, f32[1,16,256]{2,1,0:T(8,128)S(1)}, u32[]{:S(2)}, u32[]{:S(2)}) collective-permute-start(f32[1,16,256]{2,1,0:T(8,128)S(1)} %get-tuple-element.51), channel_id=1, source_target_pairs={{0,4},{1,5},{2,6},{3,7},{8,12},{9,13},{10,14},{11,15},{16,20},{17,... | collective-permute-start | bytes 49160 | tf_op jit(solution)/shard_map/ppermute | solution.py:19
  219.9 6.0 %collective-permute-start.46 = (f32[1,16,256]{2,1,0:T(8,128)S(1)}, f32[1,16,256]{2,1,0:T(8,128)S(1)}, u32[]{:S(2)}, u32[]{:S(2)}) collective-permute-start(f32[1,16,256]{2,1,0:T(8,128)S(1)} %get-tuple-element.50), channel_id=1, source_target_pairs={{4,0},{5,1},{6,2},{7,3},{12,8},{13,9},{14,10},{15,11},{20,16},{21,... | collective-permute-start | bytes 49160 | tf_op jit(solution)/shard_map/ppermute | solution.py:22
  233.6 5.6 %collective-permute-start.50 = (f32[1,16,256]{2,1,0:T(8,128)S(1)}, f32[1,16,256]{2,1,0:T(8,128)S(1)}, u32[]{:S(2)}, u32[]{:S(2)}) collective-permute-start(f32[1,16,256]{2,1,0:T(8,128)S(1)} %get-tuple-element.49), channel_id=1, source_target_pairs={{4,0},{5,1},{6,2},{7,3},{12,8},{13,9},{14,10},{15,11},{20,16},{21,... | collective-permute-start | bytes 49160 | tf_op jit(solution)/shard_map/ppermute | solution.py:22
  276.3 5.6 %collective-permute-start.59 = (f32[1,16,256]{2,1,0:T(8,128)S(1)}, f32[1,16,256]{2,1,0:T(8,128)S(1)}, u32[]{:S(2)}, u32[]{:S(2)}) collective-permute-start(f32[1,16,256]{2,1,0:T(8,128)S(1)} %get-tuple-element.46), channel_id=1, source_target_pairs={{0,4},{1,5},{2,6},{3,7},{8,12},{9,13},{10,14},{11,15},{16,20},{17,... | collective-permute-start | bytes 49160 | tf_op jit(solution)/shard_map/ppermute | solution.py:19
  295.2 5.8 %collective-permute-start.64 = (f32[1,16,256]{2,1,0:T(8,128)S(1)}, f32[1,16,256]{2,1,0:T(8,128)S(1)}, u32[]{:S(2)}, u32[]{:S(2)}) collective-permute-start(f32[1,16,256]{2,1,0:T(8,128)S(1)} %get-tuple-element.45), channel_id=1, source_target_pairs={{0,4},{1,5},{2,6},{3,7},{8,12},{9,13},{10,14},{11,15},{16,20},{17,... | collective-permute-start | bytes 49160 | tf_op jit(solution)/shard_map/ppermute | solution.py:19
  296.5 6.0 %collective-permute-start.63 = (f32[1,16,256]{2,1,0:T(8,128)S(1)}, f32[1,16,256]{2,1,0:T(8,128)S(1)}, u32[]{:S(2)}, u32[]{:S(2)}) collective-permute-start(f32[1,16,256]{2,1,0:T(8,128)S(1)} %get-tuple-element.44), channel_id=1, source_target_pairs={{4,0},{5,1},{6,2},{7,3},{12,8},{13,9},{14,10},{15,11},{20,16},{21,... | collective-permute-start | bytes 49160 | tf_op jit(solution)/shard_map/ppermute | solution.py:22
  310.3 5.6 %collective-permute-start.67 = (f32[1,16,256]{2,1,0:T(8,128)S(1)}, f32[1,16,256]{2,1,0:T(8,128)S(1)}, u32[]{:S(2)}, u32[]{:S(2)}) collective-permute-start(f32[1,16,256]{2,1,0:T(8,128)S(1)} %get-tuple-element.43), channel_id=1, source_target_pairs={{4,0},{5,1},{6,2},{7,3},{12,8},{13,9},{14,10},{15,11},{20,16},{21,... | collective-permute-start | bytes 49160 | tf_op jit(solution)/shard_map/ppermute | solution.py:22
  (50 other events, 287.0 us)
where the time goes:
time: 369 us; the launch traced here: 367 us
  starting transfers between devices  168 us (46%)
  waiting for transfers between devices  119 us (32%)
  local copies, waits for them, and re-layouts  48.2 us (13%)
  other arithmetic  29.9 us (8%)
    ppermute x38, starting transfers between devices, extended(): lax.ppermute(lax.slice_in_dim(block, 0, width, axis=dim), axis, backward)  113 us
    ppermute x38, waiting for transfers between devices, extended(): lax.ppermute(lax.slice_in_dim(block, block.shape[dim] - width, None, axis...  101 us
    ppermute x38, starting transfers between devices, extended(): lax.ppermute(lax.slice_in_dim(block, block.shape[dim] - width, None, axis...  49.6 us
    reshape x4, local copies, waits for them, and re-layouts, shrink(): values.reshape(values.shape[0] // 2, 2, values.shape[1] // 2, 2, values.s...  22.2 us
    another operation x4, local copies, waits for them, and re-layouts, shrink(): values.reshape(values.shape[0] // 2, 2, values.shape[1] // 2, 2, values.s...  22.2 us
    reduce_sum x8, other arithmetic, shrink(): return values.reshape(values.shape[0] // 2, 2, values.shape[1] // 2, 2, v...  20.3 us
    ppermute x3, waiting for transfers between devices, passed_along(): return lax.ppermute(block, axis, route)  11 us
  transfers between devices with their start and end apart: 79, of which 39 were waited for; matrix products, arithmetic and copies ran while one was open for 13% of the time, Pallas kernels for 0%

commit v1 on v0

v1 whole, which is shorter than its diff:
```python
import functools

import jax
import jax.numpy as jnp
from jax import lax
from jax.experimental import pallas as pl
from jax.experimental.pallas import tpu as pltpu
from jax.sharding import PartitionSpec as P

SECTIONS = 4
FINE_STEPS = 2
FINE_STEP = 1.0
RELAX = 0.8
INTERVAL = FINE_STEPS * FINE_STEP
LANES = 128
PAD = 8
COARSE_REACH = 6
FINE_REACH = SECTIONS * FINE_STEPS


def chebyshev_coefficients(sections):
    damping = 0.05
    centre_point = 1.0 + damping / (sections * sections)
    chebyshev = [1.0, centre_point]
    slopes = [0.0, 1.0]
    for degree in range(2, sections + 1):
        chebyshev.append(2.0 * centre_point * chebyshev[degree - 1] - chebyshev[degree - 2])
        slopes.append(
            2.0 * chebyshev[degree - 1]
            + 2.0 * centre_point * slopes[degree - 1]
            - slopes[degree - 2]
        )
    slope_ratio = chebyshev[sections] / slopes[sections]
    weights = [1.0 / entry for entry in chebyshev]
    scales = [0.0, 0.0]
    carries = [0.0, 0.0]
    tildes = [0.0, slope_ratio / centre_point]
    for degree in range(2, sections + 1):
        scales.append(2.0 * weights[degree] * centre_point / weights[degree - 1])
        carries.append(-weights[degree] / weights[degree - 2])
        tildes.append(2.0 * weights[degree] * slope_ratio / weights[degree - 1])
    return (scales, carries, tildes)


def round_up(value, unit):
    return -(-value // unit) * unit


class Box:
    def __init__(self, depth, rows, side, columns):
        self.depth, self.rows, self.side, self.columns = depth, rows, side, columns
        self.height = rows + 2 * side
        self.tiles = columns // LANES

    def scratch(self, depth=None):
        depth = self.depth if depth is None else depth
        return pltpu.VMEM(
            (self.tiles, depth + 4, self.height + 2 * PAD, LANES), jnp.float32
        )

    def span(self, margin):
        first = (self.side - margin) // 8 * 8
        last = round_up(self.side + self.rows + margin, 8)
        assert first >= 0 and last <= self.height
        return first, last


CHUNK = 16


def chunks(first, last):
    at = first
    while at < last:
        size = min(CHUNK, last - at)
        yield at, size
        at += size


def each_plane(count, body):
    if count <= 8:
        for plane in range(count):
            body(plane)
    else:
        lax.fori_loop(0, count, lambda plane, _: (body(plane), 0)[1], 0)


def lane_index(size):
    return lax.broadcasted_iota(jnp.int32, (size, LANES), 1)


def row_index(size):
    return lax.broadcasted_iota(jnp.int32, (size, LANES), 0)


def sideways(values, step):
    size = values[0].shape[0]
    lane = lane_index(size)
    back = [pltpu.roll(entry, LANES - step, 1) for entry in values]
    forth = [pltpu.roll(entry, step, 1) for entry in values]
    zero = jnp.zeros_like(values[0])
    count = len(values)
    after = [
        jnp.where(lane >= LANES - step, back[i + 1] if i + 1 < count else zero, back[i])
        for i in range(count)
    ]
    before = [
        jnp.where(lane < step, forth[i - 1] if i else zero, forth[i]) for i in range(count)
    ]
    return after, before


def operator(field, coeff, plane, at, size, step):
    tiles = field.shape[0]
    centre = [field[i, plane + 2, pl.ds(PAD + at, size), :] for i in range(tiles)]
    after, before = sideways(centre, step)
    result = []
    for i in range(tiles):
        deep_after = field[i, plane + 3, pl.ds(PAD + at, size), :]
        deep_before = field[i, plane + 1, pl.ds(PAD + at, size), :]
        row_after = field[i, plane + 2, pl.ds(PAD + at + step, size), :]
        row_before = field[i, plane + 2, pl.ds(PAD + at - step, size), :]
        c = [coeff[k, plane, pl.ds(at, size), i * LANES : (i + 1) * LANES] for k in range(4)]
        total = (deep_after + deep_before) + (row_after + row_before) + (after[i] + before[i])
        spread = c[0] * (total - 6.0 * centre[i])
        drift = (
            c[1] * (deep_after - deep_before)
            + c[2] * (row_after - row_before)
            + c[3] * (after[i] - before[i])
        )
        result.append((spread, drift, centre[i]))
    return result


def clear(field):
    field[...] = jnp.zeros_like(field)


def fine_body(box, margin, start, coeff, end, one, two):
    scales, carries, tildes = chebyshev_coefficients(SECTIONS)
    clear(one)
    clear(two)
    inner = slice(PAD, PAD + box.height)
    for i in range(box.tiles):
        one[i, 2 : 2 + box.depth, inner, :] = start[:, :, i * LANES : (i + 1) * LANES]
    stage = 0
    current, other = one, two
    for repeat in range(FINE_STEPS):
        for degree in range(1, SECTIONS + 1):
            stage += 1
            first, last = box.span(margin + FINE_REACH - stage)

            def plane_body(plane, current=current, other=other, degree=degree):
                for at, size in chunks(first, last):
                    values = operator(current, coeff, plane, at, size, 1)
                    for i, (spread, drift, centre) in enumerate(values):
                        change = tildes[degree] * FINE_STEP * (spread - 0.5 * drift)
                        where = (i, plane + 2, pl.ds(PAD + at, size), slice(None))
                        if degree == 1:
                            other[where] = centre + change
                        else:
                            other[where] = (
                                scales[degree] * centre + carries[degree] * other[where] + change
                            )

            each_plane(box.depth, plane_body)
            current, other = other, current
    first, last = box.span(margin)
    for i in range(box.tiles):
        end[:, :, i * LANES : (i + 1) * LANES] = current[
            i, 2 : 2 + box.depth, PAD + first : PAD + last, :
        ]


def pair_columns(value):
    lane = lane_index(value.shape[0])
    other = jnp.where(
        lane % 2 == 0, pltpu.roll(value, LANES - 1, 1), pltpu.roll(value, 1, 1)
    )
    return value + other


def pair_rows(field, i, plane, at, size):
    row = row_index(size)
    other = jnp.where(
        row % 2 == 0,
        field[i, plane + 2, pl.ds(PAD + at + 1, size), :],
        field[i, plane + 2, pl.ds(PAD + at - 1, size), :],
    )
    return field[i, plane + 2, pl.ds(PAD + at, size), :] + other


def prepare_body(box, coeff, coarse, weight, coarse_weight, work):
    clear(work)
    for k in range(4):

        def columns_body(plane, k=k):
            for at, size in chunks(0, box.height):
                for i in range(box.tiles):
                    cols = slice(i * LANES, (i + 1) * LANES)
                    low = coeff[k, 2 * plane, pl.ds(at, size), cols]
                    high = coeff[k, 2 * plane + 1, pl.ds(at, size), cols]
                    work[i, plane + 2, pl.ds(PAD + at, size), :] = pair_columns(low + high)
                    if k == 0:
                        weight[2 * plane, pl.ds(at, size), cols] = RELAX / (
                            1.0 + 6.0 * INTERVAL * low
                        )
                        weight[2 * plane + 1, pl.ds(at, size), cols] = RELAX / (
                            1.0 + 6.0 * INTERVAL * high
                        )

        each_plane(box.depth // 2, columns_body)

        def rows_body(plane, k=k):
            for at, size in chunks(0, box.height):
                for i in range(box.tiles):
                    cols = slice(i * LANES, (i + 1) * LANES)
                    mean = 0.125 * pair_rows(work, i, plane, at, size)
                    coarse[k, plane, pl.ds(at, size), cols] = mean
                    if k == 0:
                        coarse_weight[plane, pl.ds(at, size), cols] = RELAX / (
                            1.0 + 6.0 * INTERVAL * mean / 4.0
                        )

        each_plane(box.depth // 2, rows_body)


def coarse_step_body(box, margin, source, trial, pairs, guess, residual, params, finish):
    coeff, coarse, weight, coarse_weight = params
    half = box.depth // 2

    def cols(i):
        return slice(i * LANES, (i + 1) * LANES)

    first, last = box.span(margin + 5)

    def smooth(plane):
        for at, size in chunks(first, last):
            values = operator(source, coeff, plane, at, size, 1)
            for i, (spread, drift, centre) in enumerate(values):
                change = INTERVAL * spread - (INTERVAL * 0.5) * drift
                trial[i, plane + 2, pl.ds(PAD + at, size), :] = (
                    centre + weight[plane, pl.ds(at, size), cols(i)] * change
                )

    each_plane(box.depth, smooth)

    first, last = box.span(margin + 4)

    def restrict(plane):
        for at, size in chunks(first, last):
            sums = [None] * box.tiles
            for half_plane in range(2):
                fine_plane = 2 * plane + half_plane
                values = operator(trial, coeff, fine_plane, at, size, 1)
                for i, (spread, drift, centre) in enumerate(values):
                    misfit = (
                        source[i, fine_plane + 2, pl.ds(PAD + at, size), :]
                        - centre
                        + (INTERVAL * spread - (INTERVAL * 0.5) * drift)
                    )
                    sums[i] = misfit if sums[i] is None else sums[i] + misfit
            for i in range(box.tiles):
                pairs[i, plane + 2, pl.ds(PAD + at, size), :] = pair_columns(sums[i])

    each_plane(half, restrict)

    def first_guess(plane):
        for at, size in chunks(first, last):
            for i in range(box.tiles):
                mean = 0.125 * pair_rows(pairs, i, plane, at, size)
                residual[i, plane + 2, pl.ds(PAD + at, size), :] = mean
                guess[i, plane + 2, pl.ds(PAD + at, size), :] = (
                    coarse_weight[plane, pl.ds(at, size), cols(i)] * mean
                )

    each_plane(half, first_guess)

    first, last = box.span(margin + 2)

    def correct(plane):
        for at, size in chunks(first, last):
            values = operator(guess, coarse, plane, at, size, 2)
            for i, (spread, drift, centre) in enumerate(values):
                change = (INTERVAL / 4.0) * (spread - drift)
                rest = residual[i, plane + 2, pl.ds(PAD + at, size), :] - centre + change
                fix = centre + coarse_weight[plane, pl.ds(at, size), cols(i)] * rest
                for half_plane in range(2):
                    where = (i, 2 * plane + half_plane + 2, pl.ds(PAD + at, size), slice(None))
                    trial[where] = trial[where] + fix

    each_plane(half, correct)

    first, last = box.span(margin)

    def smooth_again(plane):
        for at, size in chunks(first, last):
            values = operator(trial, coeff, plane, at, size, 1)
            for i, (spread, drift, centre) in enumerate(values):
                misfit = (
                    source[i, plane + 2, pl.ds(PAD + at, size), :]
                    - centre
                    + (INTERVAL * spread - (INTERVAL * 0.5) * drift)
                )
                finish(
                    plane, i, at, size, centre + weight[plane, pl.ds(at, size), cols(i)] * misfit
                )

    each_plane(box.depth, smooth_again)


def coarse_scratch(box):
    half = box.depth // 2
    return [box.scratch(), box.scratch(half), box.scratch(half), box.scratch(half)]


def pair_body(
    box, low_side, start_end, second_start, second_end, *rest
):
    params, out, (source, trial, pairs, guess, residual) = rest[:4], rest[4], rest[5:]
    clear(source)
    clear(trial)
    clear(pairs)
    clear(guess)
    first, last = box.span(COARSE_REACH)
    for i in range(box.tiles):
        cols = slice(i * LANES, (i + 1) * LANES)
        source[i, 2 : 2 + box.depth, PAD + first : PAD + last, :] = (
            start_end[:, :, cols] - second_start[:, first:last, cols]
        )

    def finish(plane, i, at, size, value):
        cols = slice(i * LANES, (i + 1) * LANES)
        out[plane, pl.ds(at - box.side, size), cols] = (
            value + second_end[plane, pl.ds(at - first, size), cols]
        )

    coarse_step_body(box, 0, source, trial, pairs, guess, residual, params, finish)


def last_body(box, error, *rest):
    params, once, twice, (source, second, trial, pairs, guess, residual) = (
        rest[:4],
        rest[4],
        rest[5],
        rest[6:],
    )
    clear(source)
    clear(second)
    clear(trial)
    clear(pairs)
    clear(guess)
    for i in range(box.tiles):
        cols = slice(i * LANES, (i + 1) * LANES)
        source[i, 2 : 2 + box.depth, PAD : PAD + box.height, :] = error[:, :, cols]

    def finish_once(plane, i, at, size, value):
        second[i, plane + 2, pl.ds(PAD + at, size), :] = value

    coarse_step_body(
        box, COARSE_REACH, source, trial, pairs, guess, residual, params, finish_once
    )
    for i in range(box.tiles):
        cols = slice(i * LANES, (i + 1) * LANES)
        once[:, :, cols] = second[
            i, 2 : 2 + box.depth, PAD + box.side : PAD + box.side + box.rows, :
        ]

    def finish_twice(plane, i, at, size, value):
        cols = slice(i * LANES, (i + 1) * LANES)
        twice[plane, pl.ds(at - box.side, size), cols] = value

    coarse_step_body(box, 0, second, trial, pairs, guess, residual, params, finish_twice)


def run(body, outs, scratch, *args):
    whole = pl.BlockSpec(memory_space=pltpu.VMEM)
    single = not isinstance(outs, list)
    shapes = [outs] if single else outs
    result = pl.pallas_call(
        body,
        out_shape=[jax.ShapeDtypeStruct(shape, jnp.float32) for shape in shapes],
        in_specs=[whole] * len(args),
        out_specs=[whole] * len(shapes),
        scratch_shapes=scratch,
    )(*args)
    return result[0] if single else result


def slab_gathered(block, dim):
    count = lax.axis_size("slab")
    if count == 1:
        return block
    if count != 2:
        return lax.all_gather(block, "slab", axis=dim, tiled=True)
    other = lax.ppermute(block, "slab", [(0, 1), (1, 0)])
    first = lax.axis_index("slab") == 0
    low = jnp.where(first, block, other)
    high = jnp.where(first, other, block)
    return jnp.concatenate([low, high], axis=dim)


def row_slice(block, first, last):
    return lax.slice_in_dim(block, first, last, axis=block.ndim - 2)


def with_rows(block, width, side):
    count = lax.axis_size("coarse")
    rows = block.shape[-2]
    place = lax.axis_index("coarse")
    odd = place % 2 == 1
    one = [(i, i ^ 1) for i in range(count) if i ^ 1 < count]
    two = [(i, i + 1 if i % 2 else i - 1) for i in range(count)]
    two = [(i, j) for i, j in two if 0 <= j < count]
    low, high = [], []
    from_low, from_high = block, block
    left = width
    while left > 0:
        size = min(rows, left)
        up = row_slice(from_low, from_low.shape[-2] - size, from_low.shape[-2])
        down = row_slice(from_high, 0, size)
        got_one = lax.ppermute(jnp.where(odd, down, up), "coarse", one)
        got_two = lax.ppermute(jnp.where(odd, up, down), "coarse", two)
        from_low = jnp.where(odd, got_one, got_two)
        from_high = jnp.where(odd, got_two, got_one)
        low.insert(0, from_low)
        high.append(from_high)
        left -= size
    shape = list(block.shape)
    shape[-2] = side - width
    zeros = jnp.zeros(shape, jnp.float32)
    return jnp.concatenate([zeros, *low, block, *high, zeros], axis=block.ndim - 2)


def core_swapped(block):
    count = lax.axis_size("tm")
    assert count % 2 == 0
    return lax.ppermute(block, "tm", [(i, i ^ 1) for i in range(count)])


def ordered(mine, other, second):
    return jnp.where(second, other, mine), jnp.where(second, mine, other)


def per_device(states, diffusivity, velocity):
    windows = lax.axis_size("tm")
    place = lax.axis_index("tm")
    second = place % 2 == 1
    own_depth = diffusivity.shape[0]
    rows, columns = diffusivity.shape[1:]
    reach = FINE_REACH + COARSE_REACH
    side = round_up(max(reach, 2 * COARSE_REACH), 8)
    depth = own_depth * lax.axis_size("slab")
    box = Box(depth, rows, side, columns)

    coeffs = jnp.concatenate([diffusivity[None], velocity], 0)
    share = jnp.where(second, coeffs[2:], coeffs[:2])
    parcel = jnp.concatenate([states, share], 0)
    parcel = with_rows(slab_gathered(parcel, 1), reach, side)
    other = core_swapped(parcel)
    start = parcel[0]
    first_start, second_start = ordered(start, other[0], second)
    low_coeffs, high_coeffs = ordered(parcel[1:], other[1:], second)
    coeff = jnp.concatenate([low_coeffs, high_coeffs], 0)

    first, last = box.span(COARSE_REACH)
    end = run(
        functools.partial(fine_body, box, COARSE_REACH),
        (depth, last - first, columns),
        [box.scratch(), box.scratch()],
        start,
        coeff,
    )
    half = depth // 2
    params = run(
        functools.partial(prepare_body, box),
        [
            (4, half, box.height, columns),
            (depth, box.height, columns),
            (half, box.height, columns),
        ],
        [box.scratch(half)],
        coeff,
    )
    params = [coeff, *params]
    first_end, second_end = ordered(end, core_swapped(end), second)
    joined = run(
        functools.partial(pair_body, box, first),
        (depth, rows, columns),
        [box.scratch()] + coarse_scratch(box),
        first_end,
        second_start,
        second_end,
        *params,
    )
    own_first = row_slice(first_end, side - first, side - first + rows)
    result_first, result_second = own_first, joined
    leaving = joined
    for turn in range(1, windows // 2):
        arrived = lax.ppermute(
            leaving, "tm", [(i, (i + 2) % windows) for i in range(windows)]
        )
        arrived = with_rows(arrived, 2 * COARSE_REACH, side)
        mine = place // 2 == turn
        error = arrived - first_start
        once, twice = run(
            functools.partial(last_body, box),
            [(depth, rows, columns)] * 2,
            [box.scratch()] * 2 + coarse_scratch(box),
            error,
            *params,
        )
        result_first = jnp.where(mine, own_first + once, result_first)
        leaving = joined + twice
        result_second = jnp.where(mine, leaving, result_second)
    result = jnp.where(second, result_second, result_first)
    return lax.dynamic_slice_in_dim(
        result, lax.axis_index("slab") * own_depth, own_depth, 0
    )[None]


def solution(mesh):
    return jax.shard_map(
        per_device,
        mesh=mesh,
        in_specs=(
            P("tm", "slab", "coarse", None),
            P("slab", "coarse", None),
            P(None, "slab", "coarse", None),
        ),
        out_specs=P("tm", "slab", "coarse", None),
        check_vma=False,
    )
```

time: 369 us -> 64 us (0.17)
  the two profiles are of different devices: /device:TPU:30 before, /device:TPU:0 now
where the time goes in v1:
time: 64 us; the launch traced here: 63.6 us
  waiting for transfers between devices  22.3 us (35%)
  Pallas kernels  16.8 us (26%)
  starting transfers between devices  14.3 us (22%)
  other arithmetic  8.3 us (13%)
  local copies, waits for them, and re-layouts  1.85 us (3%)
    pallas_call x4, Pallas kernels, run(): pl.pallas_call(body, out_shape=[jax.ShapeDtypeStruct(shape, jnp.float32)...  16.8 us
    ppermute x2, waiting for transfers between devices, with_rows(): got_one = lax.ppermute(jnp.where(odd, down, up), 'coarse', one)  10.9 us
    ppermute x2, starting transfers between devices, with_rows(): got_one = lax.ppermute(jnp.where(odd, down, up), 'coarse', one)  8.18 us
    ppermute x1, waiting for transfers between devices, slab_gathered(): other = lax.ppermute(block, 'slab', [(0, 1), (1, 0)])  4.9 us
    ppermute x1, waiting for transfers between devices, per_device(): lax.ppermute(leaving, 'tm', [(i, (i + 2) % windows) for i in range(window...  4.47 us
    ppermute x1, starting transfers between devices, slab_gathered(): other = lax.ppermute(block, 'slab', [(0, 1), (1, 0)])  3.03 us
    ppermute x2, waiting for transfers between devices, core_swapped(): return lax.ppermute(block, 'tm', [(i, i ^ 1) for i in range(count)])  2.05 us
    select_n x3, other arithmetic, ordered(): return (jnp.where(second, other, mine), jnp.where(second, mine, other))  1.76 us
  transfers between devices with their start and end apart: 8, of which 5 were waited for; matrix products, arithmetic and copies ran while one was open for 3% of the time, Pallas kernels for 5%

profile of v1, /device:TPU:0, one launch (start us, length us, event | category | flops | bytes accessed | tf_op | source)
XLA Modules:
  0.0 63.6 jit_solution(3288037118923765217)
XLA Ops:
  0.0 1.0 %fusion.3 = f32[2,4,16,256]{3,2,1,0:T(8,128)S(1)} fusion(f32[3,4,16,256]{3,2,1,0:T(8,128)} %param.5, f32[1,4,16,256]{3,2,1,0:T(8,128)} %bitcast.15, pred[]{:T(512)S(6)} %eq.17), kind=kLoop, calls=%fused_computation.20 | loop fusion | flops 65536 | bytes 524289 | tf_op jit(solution)/shard_map/jit(_where)/select_n | solution.py:456
  1.0 0.9 %pad_maximum_fusion.2 = f32[3,4,16,256]{3,2,1,0:T(8,128)S(1)} fusion(f32[2,4,16,256]{3,2,1,0:T(8,128)S(1)} %fusion.3, f32[1,4,16,256]{3,2,1,0:T(8,128)} %param.3), kind=kLoop, calls=%fused_computation.14 | loop fusion | flops 49152 | bytes 393216 | tf_op jit(solution)/shard_map/concatenate | solution.py:457
  1.8 3.0 %collective-permute-start = (f32[3,4,16,256]{3,2,1,0:T(8,128)S(1)}, f32[3,4,16,256]{3,2,1,0:T(8,128)S(1)}, u32[]{:S(2)}, u32[]{:S(2)}) collective-permute-start(f32[3,4,16,256]{3,2,1,0:T(8,128)S(1)} %pad_maximum_fusion.2), channel_id=1, source_target_pairs={{0,4},{4,0},{1,5},{5,1},{2,6},{6,2},{3,7},{7,3},{8,12},{12,8},{9,1... | collective-permute-start | bytes 589832 | tf_op jit(solution)/shard_map/ppermute | solution.py:395
  4.8 4.9 %collective-permute-done = f32[3,4,16,256]{3,2,1,0:T(8,128)S(1)} collective-permute-done((f32[3,4,16,256]{3,2,1,0:T(8,128)S(1)}, f32[3,4,16,256]{3,2,1,0:T(8,128)S(1)}, u32[]{:S(2)}, u32[]{:S(2)}) %collective-permute-start) | collective-permute-done | bytes 196640 | tf_op jit(solution)/shard_map/ppermute | solution.py:395
  9.7 0.9 %broadcast_select_fusion.7 = (f32[3,4,16,256]{3,2,1,0:T(8,128)S(1)}, f32[3,4,16,256]{3,2,1,0:T(8,128)S(1)}) fusion(f32[3,4,16,256]{3,2,1,0:T(8,128)S(1)} %collective-permute-done, pred[]{:T(512)S(6)} %eq.20, f32[2,4,16,256]{3,2,1,0:T(8,128)S(1)} %fusion.3, f32[1,4,16,256]{3,2,1,0:T(8,128)} %param.3), kind=kLoop, calls=%fused_computation.28 | loop fusion | flops 147456 | bytes 786433 | tf_op jit(solution)/shard_map/jit(_where)/select_n | solution.py:397
  10.6 0.1 broadcast_select_fusion.2
  10.7 0.7 %collective-permute-start.2 = (f32[3,8,14,256]{3,2,1,0:T(8,128)S(1)}, f32[3,8,14,256]{3,2,1,0:T(8,128)S(1)}, u32[]{:S(2)}, u32[]{:S(2)}) collective-permute-start(f32[3,8,14,256]{3,2,1,0:T(8,128)S(1)} %get-tuple-element.21), channel_id=1, source_target_pairs={{1,2},{2,1},{5,6},{6,5},{9,10},{10,9},{13,14},{14,13},{17,18},{18,... | collective-permute-start | bytes 1032200 | tf_op jit(solution)/shard_map/ppermute | solution.py:422
  11.4 4.7 %collective-permute-start.1 = (f32[3,8,14,256]{3,2,1,0:T(8,128)S(1)}, f32[3,8,14,256]{3,2,1,0:T(8,128)S(1)}, u32[]{:S(2)}, u32[]{:S(2)}) collective-permute-start(f32[3,8,14,256]{3,2,1,0:T(8,128)S(1)} %get-tuple-element.22), channel_id=1, source_target_pairs={{0,1},{1,0},{2,3},{3,2},{4,5},{5,4},{6,7},{7,6},{8,9},{9,8},{10,11... | collective-permute-start | bytes 1032200 | tf_op jit(solution)/shard_map/ppermute | solution.py:421
  16.1 7.9 %collective-permute-done.1 = f32[3,8,14,256]{3,2,1,0:T(8,128)S(1)} collective-permute-done((f32[3,8,14,256]{3,2,1,0:T(8,128)S(1)}, f32[3,8,14,256]{3,2,1,0:T(8,128)S(1)}, u32[]{:S(2)}, u32[]{:S(2)}) %collective-permute-start.1) | collective-permute-done | bytes 344096 | tf_op jit(solution)/shard_map/ppermute | solution.py:421
  24.1 0.1 broadcast_select_fusion
  24.2 0.8 %concatenate.21 = f32[3,8,48,256]{3,2,1,0:T(8,128)S(1)} concatenate(f32[3,8,2,256]{3,2,1,0:T(2,128)S(1)} %broadcast_in_dim.12, f32[3,8,14,256]{3,2,1,0:T(8,128)S(1)} %get-tuple-element.18, f32[3,8,16,256]{3,2,1,0:T(8,128)S(1)} %pad_maximum_fusion.1, f32[3,8,14,256]{3,2,1,0:T(8,128)S(1)} %get-tuple-element.17, f32[3,8,2,256]{3,2,1,0:T(2,128)S(1)} %broadcast_in_dim.12), dimensions={2} | concatenate | bytes 2359296 | tf_op jit(solution)/shard_map/concatenate | solution.py:431
  25.0 0.1 collective-permute-start.3
  25.1 0.8 %slice_bitcast_fusion.1.start = f32[8,48,256]{2,1,0:T(8,128)} fusion(f32[3,8,48,256]{3,2,1,0:T(8,128)S(1)} %concatenate.21), kind=kLoop, calls=%fused_computation.11 | loop fusion | bytes 786432 | tf_op jit(solution)/shard_map/squeeze | solution.py:460
  25.8 2.0 %collective-permute-done.3 = f32[3,8,48,256]{3,2,1,0:T(8,128)S(1)} collective-permute-done((f32[3,8,48,256]{3,2,1,0:T(8,128)S(1)}, f32[3,8,48,256]{3,2,1,0:T(8,128)S(1)}, u32[]{:S(2)}, u32[]{:S(2)}) %collective-permute-start.3) | collective-permute-done | bytes 1179680 | tf_op jit(solution)/shard_map/ppermute | solution.py:437
  27.9 0.1 slice_select_fusion.1
  28.0 1.3 %pad_maximum_fusion.coeff.rest_0_ = f32[4,8,48,256]{3,2,1,0:T(8,128)} fusion(f32[2,8,48,256]{3,2,1,0:T(8,128)S(1)} %get-tuple-element.16, f32[2,8,48,256]{3,2,1,0:T(8,128)S(1)} %get-tuple-element.15), kind=kLoop, calls=%fused_computation | loop fusion | flops 393216 | bytes 3145728 | tf_op jit(solution)/shard_map/concatenate | solution.py:463
  29.3 4.4 %shard_map.37 = f32[8,32,256]{2,1,0:T(8,128)} custom-call(f32[8,48,256]{2,1,0:T(8,128)} %slice_bitcast_fusion.1.start, f32[4,8,48,256]{3,2,1,0:T(8,128)} %pad_maximum_fusion.coeff.rest_0_), custom_call_target="tpu_custom_call" | custom-call | tf_op jit(solution)/shard_map/pallas_call | solution.py:379
  33.7 0.1 collective-permute-start.4
  33.9 2.9 %shard_map.38 = (f32[4,4,48,256]{3,2,1,0:T(8,128)}, f32[8,48,256]{2,1,0:T(8,128)}, f32[4,48,256]{2,1,0:T(8,128)}) custom-call(f32[4,8,48,256]{3,2,1,0:T(8,128)} %pad_maximum_fusion.coeff.rest_0_), custom_call_target="tpu_custom_call" | custom-call | tf_op jit(solution)/shard_map/pallas_call | solution.py:379
  36.8 0.8 %fusion.2.second_start = f32[8,48,256]{2,1,0:T(8,128)} fusion(f32[3,8,48,256]{3,2,1,0:T(8,128)S(1)} %collective-permute-done.3, pred[]{:T(512)S(6)} %eq.17, f32[3,8,48,256]{3,2,1,0:T(8,128)S(1)} %concatenate.21), kind=kLoop, calls=%fused_computation.13 | loop fusion | flops 98304 | bytes 1179649 | tf_op jit(solution)/shard_map/jit(_where)/select_n | solution.py:441
  37.6 0.8 %broadcast_select_fusion.4 = (f32[8,32,256]{2,1,0:T(8,128)}, f32[8,32,256]{2,1,0:T(8,128)}) fusion(f32[8,32,256]{2,1,0:T(8,128)S(1)} %copy-done.1, f32[8,32,256]{2,1,0:T(8,128)S(1)} %collective-permute-done.4, pred[]{:T(512)S(6)} %eq.17), kind=kLoop, calls=%fused_computation.21 | loop fusion | flops 131072 | bytes 1048577 | tf_op jit(solution)/shard_map/jit(_where)/select_n | solution.py:441
  38.5 3.9 %shard_map.39 = f32[8,16,256]{2,1,0:T(8,128)} custom-call(f32[8,32,256]{2,1,0:T(8,128)} %get-tuple-element.20.start_end, f32[8,48,256]{2,1,0:T(8,128)} %fusion.2.second_start, f32[8,32,256]{2,1,0:T(8,128)} %get-tuple-element.19.second_end, f32[4,8,48,256]{3,2,1,0:T(8,128)} %pad_maximum_fusion.coeff.rest_0_, f32[4,4,48,256]{3,2,1,0:T(8,128)} %get-tuple-element.10.rest_1_, ...), custom_call_target="tpu_custom_call" | custom-call | tf_op jit(solution)/shard_map/pallas_call | solution.py:379
  42.3 1.5 %collective-permute-start.5 = (f32[8,16,256]{2,1,0:T(8,128)}, f32[8,16,256]{2,1,0:T(8,128)S(1)}, u32[]{:S(2)}, u32[]{:S(2)}) collective-permute-start(f32[8,16,256]{2,1,0:T(8,128)} %shard_map.39), channel_id=1, source_target_pairs={{0,16},{8,24},{16,0},{24,8},{1,17},{9,25},{17,1},{25,9},{2,18},{10... | collective-permute-start | bytes 393224 | tf_op jit(solution)/shard_map/ppermute | solution.py:499
  43.8 4.5 %collective-permute-done.5 = f32[8,16,256]{2,1,0:T(8,128)S(1)} collective-permute-done((f32[8,16,256]{2,1,0:T(8,128)}, f32[8,16,256]{2,1,0:T(8,128)S(1)}, u32[]{:S(2)}, u32[]{:S(2)}) %collective-permute-start.5) | collective-permute-done | bytes 131104 | tf_op jit(solution)/shard_map/ppermute | solution.py:499
  48.3 0.7 %collective-permute-start.7 = (f32[8,12,256]{2,1,0:T(8,128)S(1)}, f32[8,12,256]{2,1,0:T(8,128)S(1)}, u32[]{:S(2)}, u32[]{:S(2)}) collective-permute-start(f32[8,12,256]{2,1,0:T(8,128)S(1)} %get-tuple-element.27), channel_id=1, source_target_pairs={{1,2},{2,1},{5,6},{6,5},{9,10},{10,9},{13,14},{14,13},{17,18},{18,... | collective-permute-start | bytes 294920 | tf_op jit(solution)/shard_map/ppermute | solution.py:422
  49.0 3.5 %collective-permute-start.6 = (f32[8,12,256]{2,1,0:T(8,128)S(1)}, f32[8,12,256]{2,1,0:T(8,128)S(1)}, u32[]{:S(2)}, u32[]{:S(2)}) collective-permute-start(f32[8,12,256]{2,1,0:T(8,128)S(1)} %get-tuple-element.28), channel_id=1, source_target_pairs={{0,1},{1,0},{2,3},{3,2},{4,5},{5,4},{6,7},{7,6},{8,9},{9,8},{10,11... | collective-permute-start | bytes 294920 | tf_op jit(solution)/shard_map/ppermute | solution.py:421
  52.5 0.0 collective-permute-done.7
  52.5 2.9 %collective-permute-done.6 = f32[8,12,256]{2,1,0:T(8,128)S(1)} collective-permute-done((f32[8,12,256]{2,1,0:T(8,128)S(1)}, f32[8,12,256]{2,1,0:T(8,128)S(1)}, u32[]{:S(2)}, u32[]{:S(2)}) %collective-permute-start.6) | collective-permute-done | bytes 98336 | tf_op jit(solution)/shard_map/ppermute | solution.py:421
  55.5 0.2 concatenate.23
  55.7 0.8 %select_subtract_fusion.error = f32[8,48,256]{2,1,0:T(8,128)} fusion(f32[8,48,256]{2,1,0:T(8,128)S(1)} %concatenate.23, f32[3,8,48,256]{3,2,1,0:T(8,128)S(1)} %collective-permute-done.3, pred[]{:T(512)S(6)} %eq.17, f32[3,8,48,256]{3,2,1,0:T(8,128)S(1)} %concatenate.21), kind=kLoop, calls=%fused_computation.12 | loop fusion | flops 196608 | bytes 1572865 | tf_op jit(solution)/shard_map/sub | solution.py:504
  56.6 5.5 %shard_map.40 = (f32[8,16,256]{2,1,0:T(8,128)}, f32[8,16,256]{2,1,0:T(8,128)}) custom-call(f32[8,48,256]{2,1,0:T(8,128)} %select_subtract_fusion.error, f32[4,8,48,256]{3,2,1,0:T(8,128)} %pad_maximum_fusion.coeff.rest_0_, f32[4,4,48,256]{3,2,1,0:T(8,128)} %get-tuple-element.10.rest_1_, f32[8,48,256]{2,1,0:T(8,128)} %get-tuple-element.11.rest_2_, ...), custom_call_target="tpu_custom_call" | custom-call | tf_op jit(solution)/shard_map/pallas_call | solution.py:379
  62.1 1.5 %fusion.5 = f32[1,4,16,256]{3,2,1,0:T(8,128)} fusion(f32[8,16,256]{2,1,0:T(8,128)} %get-tuple-element.14, s32[]{:T(128)S(6)} %select_n.166, f32[8,16,256]{2,1,0:T(8,128)S(1)} %slice.54, f32[8,16,256]{2,1,0:T(8,128)} %get-tuple-element.13, f32[8,16,256]{2,1,0:T(8,128)S(1)} %copy-done.2, pred[]{:T(512)S(6)} %eq.17, pred[]{:T(512)S(6)} %eq.18), kind=kLoop, calls=%fused_computation.30 | loop fusion | flops 81920 | bytes 327686 | tf_op jit(solution)/shard_map/broadcast_in_dim | solution.py:516
  (14 shorter events, 0.1 us)
Async XLA Ops:
  1.8 7.9 %collective-permute-start = (f32[3,4,16,256]{3,2,1,0:T(8,128)S(1)}, f32[3,4,16,256]{3,2,1,0:T(8,128)S(1)}, u32[]{:S(2)}, u32[]{:S(2)}) collective-permute-start(f32[3,4,16,256]{3,2,1,0:T(8,128)S(1)} %pad_maximum_fusion.2), channel_id=1, source_target_pairs={{0,4},{4,0},{1,5},{5,1},{2,6},{6,2},{3,7},{7,3},{8,12},{12,8},{9,1... | collective-permute-start | bytes 589832 | tf_op jit(solution)/shard_map/ppermute | solution.py:395
  10.7 5.4 %collective-permute-start.2 = (f32[3,8,14,256]{3,2,1,0:T(8,128)S(1)}, f32[3,8,14,256]{3,2,1,0:T(8,128)S(1)}, u32[]{:S(2)}, u32[]{:S(2)}) collective-permute-start(f32[3,8,14,256]{3,2,1,0:T(8,128)S(1)} %get-tuple-element.21), channel_id=1, source_target_pairs={{1,2},{2,1},{5,6},{6,5},{9,10},{10,9},{13,14},{14,13},{17,18},{18,... | collective-permute-start | bytes 1032200 | tf_op jit(solution)/shard_map/ppermute | solution.py:422
  11.4 12.7 %collective-permute-start.1 = (f32[3,8,14,256]{3,2,1,0:T(8,128)S(1)}, f32[3,8,14,256]{3,2,1,0:T(8,128)S(1)}, u32[]{:S(2)}, u32[]{:S(2)}) collective-permute-start(f32[3,8,14,256]{3,2,1,0:T(8,128)S(1)} %get-tuple-element.22), channel_id=1, source_target_pairs={{0,1},{1,0},{2,3},{3,2},{4,5},{5,4},{6,7},{7,6},{8,9},{9,8},{10,11... | collective-permute-start | bytes 1032200 | tf_op jit(solution)/shard_map/ppermute | solution.py:421
  25.0 2.9 %collective-permute-start.3 = (f32[3,8,48,256]{3,2,1,0:T(8,128)S(1)}, f32[3,8,48,256]{3,2,1,0:T(8,128)S(1)}, u32[]{:S(2)}, u32[]{:S(2)}) collective-permute-start(f32[3,8,48,256]{3,2,1,0:T(8,128)S(1)} %concatenate.21), channel_id=1, source_target_pairs={{0,8},{8,0},{16,24},{24,16},{1,9},{9,1},{17,25},{25,17},{2,10},{10... | collective-permute-start | bytes 3538952 | tf_op jit(solution)/shard_map/ppermute | solution.py:437
  33.7 3.9 %copy-start.1 = (f32[8,32,256]{2,1,0:T(8,128)S(1)}, f32[8,32,256]{2,1,0:T(8,128)}, u32[]{:S(2)}) copy-start(f32[8,32,256]{2,1,0:T(8,128)} %shard_map.37) | copy-start | bytes 786436
  33.7 3.9 %collective-permute-start.4 = (f32[8,32,256]{2,1,0:T(8,128)}, f32[8,32,256]{2,1,0:T(8,128)S(1)}, u32[]{:S(2)}, u32[]{:S(2)}) collective-permute-start(f32[8,32,256]{2,1,0:T(8,128)} %shard_map.37), channel_id=1, source_target_pairs={{0,8},{8,0},{16,24},{24,16},{1,9},{9,1},{17,25},{25,17},{2,10},{10... | collective-permute-start | bytes 786440 | tf_op jit(solution)/shard_map/ppermute | solution.py:437
  38.4 14.1 %copy-start = (f32[8,32,256]{2,1,0:T(8,128)S(1)}, f32[8,32,256]{2,1,0:T(8,128)}, u32[]{:S(2)}) copy-start(f32[8,32,256]{2,1,0:T(8,128)} %get-tuple-element.20.start_end) | copy-start | bytes 786436
  42.3 6.0 %collective-permute-start.5 = (f32[8,16,256]{2,1,0:T(8,128)}, f32[8,16,256]{2,1,0:T(8,128)S(1)}, u32[]{:S(2)}, u32[]{:S(2)}) collective-permute-start(f32[8,16,256]{2,1,0:T(8,128)} %shard_map.39), channel_id=1, source_target_pairs={{0,16},{8,24},{16,0},{24,8},{1,17},{9,25},{17,1},{25,9},{2,18},{10... | collective-permute-start | bytes 393224 | tf_op jit(solution)/shard_map/ppermute | solution.py:499
  48.3 4.2 %collective-permute-start.7 = (f32[8,12,256]{2,1,0:T(8,128)S(1)}, f32[8,12,256]{2,1,0:T(8,128)S(1)}, u32[]{:S(2)}, u32[]{:S(2)}) collective-permute-start(f32[8,12,256]{2,1,0:T(8,128)S(1)} %get-tuple-element.27), channel_id=1, source_target_pairs={{1,2},{2,1},{5,6},{6,5},{9,10},{10,9},{13,14},{14,13},{17,18},{18,... | collective-permute-start | bytes 294920 | tf_op jit(solution)/shard_map/ppermute | solution.py:422
  49.0 6.4 %collective-permute-start.6 = (f32[8,12,256]{2,1,0:T(8,128)S(1)}, f32[8,12,256]{2,1,0:T(8,128)S(1)}, u32[]{:S(2)}, u32[]{:S(2)}) collective-permute-start(f32[8,12,256]{2,1,0:T(8,128)S(1)} %get-tuple-element.28), channel_id=1, source_target_pairs={{0,1},{1,0},{2,3},{3,2},{4,5},{5,4},{6,7},{7,6},{8,9},{9,8},{10,11... | collective-permute-start | bytes 294920 | tf_op jit(solution)/shard_map/ppermute | solution.py:421
  56.6 5.5 %copy-start.2 = (f32[8,16,256]{2,1,0:T(8,128)S(1)}, f32[8,16,256]{2,1,0:T(8,128)}, u32[]{:S(2)}) copy-start(f32[8,16,256]{2,1,0:T(8,128)} %shard_map.39) | copy-start | bytes 393220

commit v2 on v1

--- a/solution.py
+++ b/solution.py
@@ -119,7 +119,7 @@
         deep_before = field[i, plane + 1, pl.ds(PAD + at, size), :]
         row_after = field[i, plane + 2, pl.ds(PAD + at + step, size), :]
         row_before = field[i, plane + 2, pl.ds(PAD + at - step, size), :]
-        c = [coeff[k, plane, pl.ds(at, size), i * LANES : (i + 1) * LANES] for k in range(4)]
+        c = [coeff[k, i, plane, pl.ds(at, size), :] for k in range(4)]
         total = (deep_after + deep_before) + (row_after + row_before) + (after[i] + before[i])
         spread = c[0] * (total - 6.0 * centre[i])
         drift = (
@@ -135,13 +135,47 @@
     field[...] = jnp.zeros_like(field)
 
 
-def fine_body(box, margin, start, coeff, end, one, two):
-    scales, carries, tildes = chebyshev_coefficients(SECTIONS)
+def fine_body(box, margin, own_depth, blocks, *refs):
+    own, own_halo = refs[:blocks], refs[blocks]
+    other, other_halo = refs[blocks + 1 : 2 * blocks + 1], refs[2 * blocks + 1]
+    end, starts, coeff, one, two = refs[2 * blocks + 2 :]
+    core = lax.axis_index("tm") % 2
+    shift = lax.axis_index("slab") if blocks == 2 else 0
+    rows, side = box.rows, box.side
+    width = own_halo.shape[-2]
     clear(one)
     clear(two)
     inner = slice(PAD, PAD + box.height)
-    for i in range(box.tiles):
-        one[i, 2 : 2 + box.depth, inner, :] = start[:, :, i * LANES : (i + 1) * LANES]
+    if width < side:
+        zeros = jnp.zeros((box.tiles, box.depth, 8, LANES), jnp.float32)
+        for array in range(4):
+            coeff[array, :, :, 0:8, :] = zeros
+            coeff[array, :, :, box.height - 8 :, :] = zeros
+        for array in range(2):
+            starts[array, :, :, 0:8, :] = zeros
+            starts[array, :, :, box.height - 8 :, :] = zeros
+    for pieces, halo, rank in ((own, own_halo, core), (other, other_halo, 1 - core)):
+        for block in range(blocks):
+            base = (block + shift) % blocks * own_depth
+            for plane in range(own_depth):
+                for i in range(box.tiles):
+                    cols = slice(i * LANES, (i + 1) * LANES)
+                    for array in range(3):
+                        centre = pieces[block][array, plane, :, cols]
+                        low = halo[0, block, array, plane, :, cols]
+                        high = halo[1, block, array, plane, :, cols]
+                        targets = []
+                        if array == 0:
+                            targets.append((starts.at[rank, i, base + plane], 0))
+                            if pieces is own:
+                                targets.append((one.at[i, base + plane + 2], PAD))
+                        else:
+                            targets.append((coeff.at[2 * rank + array - 1, i, base + plane], 0))
+                        for target, at in targets:
+                            target[at + side - width : at + side, :] = low
+                            target[at + side : at + side + rows, :] = centre
+                            target[at + side + rows : at + side + rows + width, :] = high
+    scales, carries, tildes = chebyshev_coefficients(SECTIONS)
     stage = 0
     current, other = one, two
     for repeat in range(FINE_STEPS):
@@ -165,10 +199,7 @@
             each_plane(box.depth, plane_body)
             current, other = other, current
     first, last = box.span(margin)
-    for i in range(box.tiles):
-        end[:, :, i * LANES : (i + 1) * LANES] = current[
-            i, 2 : 2 + box.depth, PAD + first : PAD + last, :
-        ]
+    end[...] = current[:, 2 : 2 + box.depth, PAD + first : PAD + last, :]
 
 
 def pair_columns(value):
@@ -196,15 +227,14 @@
         def columns_body(plane, k=k):
             for at, size in chunks(0, box.height):
                 for i in range(box.tiles):
-                    cols = slice(i * LANES, (i + 1) * LANES)
-                    low = coeff[k, 2 * plane, pl.ds(at, size), cols]
-                    high = coeff[k, 2 * plane + 1, pl.ds(at, size), cols]
+                    low = coeff[k, i, 2 * plane, pl.ds(at, size), :]
+                    high = coeff[k, i, 2 * plane + 1, pl.ds(at, size), :]
                     work[i, plane + 2, pl.ds(PAD + at, size), :] = pair_columns(low + high)
                     if k == 0:
-                        weight[2 * plane, pl.ds(at, size), cols] = RELAX / (
+                        weight[i, 2 * plane, pl.ds(at, size), :] = RELAX / (
                             1.0 + 6.0 * INTERVAL * low
                         )
-                        weight[2 * plane + 1, pl.ds(at, size), cols] = RELAX / (
+                        weight[i, 2 * plane + 1, pl.ds(at, size), :] = RELAX / (
                             1.0 + 6.0 * INTERVAL * high
                         )
 
@@ -213,11 +243,10 @@
         def rows_body(plane, k=k):
             for at, size in chunks(0, box.height):
                 for i in range(box.tiles):
-                    cols = slice(i * LANES, (i + 1) * LANES)
                     mean = 0.125 * pair_rows(work, i, plane, at, size)
-                    coarse[k, plane, pl.ds(at, size), cols] = mean
+                    coarse[k, i, plane, pl.ds(at, size), :] = mean
                     if k == 0:
-                        coarse_weight[plane, pl.ds(at, size), cols] = RELAX / (
+                        coarse_weight[i, plane, pl.ds(at, size), :] = RELAX / (
                             1.0 + 6.0 * INTERVAL * mean / 4.0
                         )
 
@@ -227,9 +256,6 @@
 def coarse_step_body(box, margin, source, trial, pairs, guess, residual, params, finish):
     coeff, coarse, weight, coarse_weight = params
     half = box.depth // 2
-
-    def cols(i):
-        return slice(i * LANES, (i + 1) * LANES)
 
     first, last = box.span(margin + 5)
 
@@ -239,7 +265,7 @@
             for i, (spread, drift, centre) in enumerate(values):
                 change = INTERVAL * spread - (INTERVAL * 0.5) * drift
                 trial[i, plane + 2, pl.ds(PAD + at, size), :] = (
-                    centre + weight[plane, pl.ds(at, size), cols(i)] * change
+                    centre + weight[i, plane, pl.ds(at, size), :] * change
                 )
 
     each_plane(box.depth, smooth)
@@ -270,7 +296,7 @@
                 mean = 0.125 * pair_rows(pairs, i, plane, at, size)
                 residual[i, plane + 2, pl.ds(PAD + at, size), :] = mean
                 guess[i, plane + 2, pl.ds(PAD + at, size), :] = (
-                    coarse_weight[plane, pl.ds(at, size), cols(i)] * mean
+                    coarse_weight[i, plane, pl.ds(at, size), :] * mean
                 )
 
     each_plane(half, first_guess)
@@ -283,7 +309,7 @@
             for i, (spread, drift, centre) in enumerate(values):
                 change = (INTERVAL / 4.0) * (spread - drift)
                 rest = residual[i, plane + 2, pl.ds(PAD + at, size), :] - centre + change
-                fix = centre + coarse_weight[plane, pl.ds(at, size), cols(i)] * rest
+                fix = centre + coarse_weight[i, plane, pl.ds(at, size), :] * rest
                 for half_plane in range(2):
                     where = (i, 2 * plane + half_plane + 2, pl.ds(PAD + at, size), slice(None))
                     trial[where] = trial[where] + fix
@@ -302,7 +328,7 @@
                     + (INTERVAL * spread - (INTERVAL * 0.5) * drift)
                 )
                 finish(
-                    plane, i, at, size, centre + weight[plane, pl.ds(at, size), cols(i)] * misfit
+                    plane, i, at, size, centre + weight[i, plane, pl.ds(at, size), :] * misfit
                 )
 
     each_plane(box.depth, smooth_again)
@@ -313,45 +339,63 @@
     return [box.scratch(), box.scratch(half), box.scratch(half), box.scratch(half)]
 
 
-def pair_body(
-    box, low_side, start_end, second_start, second_end, *rest
-):
-    params, out, (source, trial, pairs, guess, residual) = rest[:4], rest[4], rest[5:]
+def pair_body(box, own_end, other_end, starts, *rest):
+    params, out, first_out = rest[:4], rest[4], rest[5]
+    source, trial, pairs, guess, residual = rest[6:]
+    core = lax.axis_index("tm") % 2
     clear(source)
     clear(trial)
     clear(pairs)
     clear(guess)
     first, last = box.span(COARSE_REACH)
-    for i in range(box.tiles):
-        cols = slice(i * LANES, (i + 1) * LANES)
-        source[i, 2 : 2 + box.depth, PAD + first : PAD + last, :] = (
-            start_end[:, :, cols] - second_start[:, first:last, cols]
+
+    def put(first_end, second_end):
+        source[:, 2 : 2 + box.depth, PAD + first : PAD + last, :] = (
+            first_end[...] - starts[1, :, :, first:last, :]
         )
+        inner = slice(box.side - first, box.side - first + box.rows)
+        out[...] = second_end[:, :, inner, :]
+        first_out[...] = first_end[:, :, inner, :]
+
+    @pl.when(core == 0)
+    def _():
+        put(own_end, other_end)
+
+    @pl.when(core == 1)
+    def _():
+        put(other_end, own_end)
 
     def finish(plane, i, at, size, value):
-        cols = slice(i * LANES, (i + 1) * LANES)
-        out[plane, pl.ds(at - box.side, size), cols] = (
-            value + second_end[plane, pl.ds(at - first, size), cols]
-        )
+        where = (i, plane, pl.ds(at - box.side, size), slice(None))
+        out[where] = value + out[where]
 
     coarse_step_body(box, 0, source, trial, pairs, guess, residual, params, finish)
 
 
-def last_body(box, error, *rest):
-    params, once, twice, (source, second, trial, pairs, guess, residual) = (
-        rest[:4],
-        rest[4],
-        rest[5],
-        rest[6:],
-    )
+def last_body(box, own_depth, turn, first_end, joined, centre, low, high, starts, *rest):
+    params, result, leaving = rest[:4], rest[4], rest[5]
+    source, second, trial, pairs, guess, residual = rest[6:]
+    place = lax.axis_index("tm")
+    core = place % 2
+    active = place // 2 == turn
     clear(source)
     clear(second)
     clear(trial)
     clear(pairs)
     clear(guess)
-    for i in range(box.tiles):
-        cols = slice(i * LANES, (i + 1) * LANES)
-        source[i, 2 : 2 + box.depth, PAD : PAD + box.height, :] = error[:, :, cols]
+    side, rows = box.side, box.rows
+    width = low.shape[-2]
+
+    @pl.when(active)
+    def _():
+        for value, at, size in (
+            (low, side - width, width),
+            (centre, side, rows),
+            (high, side + rows, width),
+        ):
+            source[:, 2 : 2 + box.depth, PAD + at : PAD + at + size, :] = (
+                value[...] - starts[0, :, :, at : at + size, :]
+            )
 
     def finish_once(plane, i, at, size, value):
         second[i, plane + 2, pl.ds(PAD + at, size), :] = value
@@ -359,17 +403,26 @@
     coarse_step_body(
         box, COARSE_REACH, source, trial, pairs, guess, residual, params, finish_once
     )
-    for i in range(box.tiles):
-        cols = slice(i * LANES, (i + 1) * LANES)
-        once[:, :, cols] = second[
-            i, 2 : 2 + box.depth, PAD + box.side : PAD + box.side + box.rows, :
-        ]
 
     def finish_twice(plane, i, at, size, value):
-        cols = slice(i * LANES, (i + 1) * LANES)
-        twice[plane, pl.ds(at - box.side, size), cols] = value
+        where = (i, plane, pl.ds(at - box.side, size), slice(None))
+        leaving[where] = value + joined[where]
 
     coarse_step_body(box, 0, second, trial, pairs, guess, residual, params, finish_twice)
+    base = lax.axis_index("slab") * own_depth
+
+    @pl.when(core == 0)
+    def _():
+        for i in range(box.tiles):
+            result[0, :, :, i * LANES : (i + 1) * LANES] = (
+                first_end[i, pl.ds(base, own_depth)]
+                + second[i, pl.ds(base + 2, own_depth), PAD + side : PAD + side + rows, :]
+            )
+
+    @pl.when(core == 1)
+    def _():
+        for i in range(box.tiles):
+            result[0, :, :, i * LANES : (i + 1) * LANES] = leaving[i, pl.ds(base, own_depth)]
 
 
 def run(body, outs, scratch, *args):
@@ -386,49 +439,47 @@
     return result[0] if single else result
 
 
-def slab_gathered(block, dim):
+def slab_blocks(block):
     count = lax.axis_size("slab")
     if count == 1:
-        return block
-    if count != 2:
-        return lax.all_gather(block, "slab", axis=dim, tiled=True)
-    other = lax.ppermute(block, "slab", [(0, 1), (1, 0)])
-    first = lax.axis_index("slab") == 0
-    low = jnp.where(first, block, other)
-    high = jnp.where(first, other, block)
-    return jnp.concatenate([low, high], axis=dim)
+        return [block]
+    if count == 2:
+        return [block, lax.ppermute(block, "slab", [(0, 1), (1, 0)])]
+    gathered = lax.all_gather(block, "slab", axis=0)
+    return [gathered[i] for i in range(count)]
 
 
 def row_slice(block, first, last):
     return lax.slice_in_dim(block, first, last, axis=block.ndim - 2)
 
 
-def with_rows(block, width, side):
-    count = lax.axis_size("coarse")
-    rows = block.shape[-2]
-    place = lax.axis_index("coarse")
-    odd = place % 2 == 1
+def row_pairs(count):
     one = [(i, i ^ 1) for i in range(count) if i ^ 1 < count]
     two = [(i, i + 1 if i % 2 else i - 1) for i in range(count)]
-    two = [(i, j) for i, j in two if 0 <= j < count]
+    return one, [(i, j) for i, j in two if 0 <= j < count]
+
+
+def row_halo(blocks, width):
+    rows = blocks[0].shape[-2]
+    odd = lax.axis_index("coarse") % 2 == 1
+    one, two = row_pairs(lax.axis_size("coarse"))
     low, high = [], []
-    from_low, from_high = block, block
+    from_low, from_high = blocks, blocks
     left = width
     while left > 0:
         size = min(rows, left)
-        up = row_slice(from_low, from_low.shape[-2] - size, from_low.shape[-2])
-        down = row_slice(from_high, 0, size)
+        up = jnp.stack([row_slice(b, b.shape[-2] - size, b.shape[-2]) for b in from_low])
+        down = jnp.stack([row_slice(b, 0, size) for b in from_high])
         got_one = lax.ppermute(jnp.where(odd, down, up), "coarse", one)
         got_two = lax.ppermute(jnp.where(odd, up, down), "coarse", two)
-        from_low = jnp.where(odd, got_one, got_two)
-        from_high = jnp.where(odd, got_two, got_one)
-        low.insert(0, from_low)
-        high.append(from_high)
+        low.insert(0, jnp.where(odd, got_one, got_two))
+        high.append(jnp.where(odd, got_two, got_one))
+        from_low, from_high = list(low[0]), list(high[-1])
         left -= size
-    shape = list(block.shape)
-    shape[-2] = side - width
-    zeros = jnp.zeros(shape, jnp.float32)
-    return jnp.concatenate([zeros, *low, block, *high, zeros], axis=block.ndim - 2)
+    low, high = (
+        x[0] if len(x) == 1 else jnp.concatenate(x, axis=x[0].ndim - 2) for x in (low, high)
+    )
+    return jnp.stack([low, high])
 
 
 def core_swapped(block):
@@ -437,85 +488,102 @@
     return lax.ppermute(block, "tm", [(i, i ^ 1) for i in range(count)])
 
 
-def ordered(mine, other, second):
-    return jnp.where(second, other, mine), jnp.where(second, mine, other)
+def next_pair(block, width):
+    windows, count = lax.axis_size("tm"), lax.axis_size("coarse")
+    rows = block.shape[-2]
+    hop = [(t, (t + 2) % windows) for t in range(windows)]
+    if width > rows:
+        centre = lax.ppermute(block, "tm", hop)
+        halo = row_halo([centre], width)
+        return centre, halo[0, 0], halo[1, 0]
+    odd = lax.axis_index("coarse") % 2 == 1
+    both = ("tm", "coarse")
+    one, two = (
+        [(t * count + i, u * count + j) for t, u in hop for i, j in pairs]
+        for pairs in row_pairs(count)
+    )
+    up, down = row_slice(block, rows - width, rows), row_slice(block, 0, width)
+    centre = lax.ppermute(block, "tm", hop)
+    got_one = lax.ppermute(jnp.where(odd, down, up), both, one)
+    got_two = lax.ppermute(jnp.where(odd, up, down), both, two)
+    return centre, jnp.where(odd, got_one, got_two), jnp.where(odd, got_two, got_one)
 
 
 def per_device(states, diffusivity, velocity):
     windows = lax.axis_size("tm")
     place = lax.axis_index("tm")
     second = place % 2 == 1
-    own_depth = diffusivity.shape[0]
-    rows, columns = diffusivity.shape[1:]
+    own_depth, rows, columns = diffusivity.shape
     reach = FINE_REACH + COARSE_REACH
     side = round_up(max(reach, 2 * COARSE_REACH), 8)
     depth = own_depth * lax.axis_size("slab")
     box = Box(depth, rows, side, columns)
-
-    coeffs = jnp.concatenate([diffusivity[None], velocity], 0)
-    share = jnp.where(second, coeffs[2:], coeffs[:2])
-    parcel = jnp.concatenate([states, share], 0)
-    parcel = with_rows(slab_gathered(parcel, 1), reach, side)
-    other = core_swapped(parcel)
-    start = parcel[0]
-    first_start, second_start = ordered(start, other[0], second)
-    low_coeffs, high_coeffs = ordered(parcel[1:], other[1:], second)
-    coeff = jnp.concatenate([low_coeffs, high_coeffs], 0)
+    tiles, height, half = box.tiles, box.height, depth // 2
+
+    parcel = jnp.stack(
+        [
+            states[0],
+            jnp.where(second, velocity[1], diffusivity),
+            jnp.where(second, velocity[2], velocity[0]),
+        ]
+    )
+    blocks = slab_blocks(parcel)
+    other_blocks = [core_swapped(block) for block in blocks]
+    halo = row_halo(blocks, reach)
+    other_halo = core_swapped(halo)
 
     first, last = box.span(COARSE_REACH)
-    end = run(
-        functools.partial(fine_body, box, COARSE_REACH),
-        (depth, last - first, columns),
+    end, starts, coeff = run(
+        functools.partial(fine_body, box, COARSE_REACH, own_depth, len(blocks)),
+        [
+            (tiles, depth, last - first, LANES),
+            (2, tiles, depth, height, LANES),
+            (4, tiles, depth, height, LANES),
+        ],
         [box.scratch(), box.scratch()],
-        start,
-        coeff,
-    )
-    half = depth // 2
+        *blocks,
+        halo,
+        *other_blocks,
+        other_halo,
+    )
     params = run(
         functools.partial(prepare_body, box),
         [
-            (4, half, box.height, columns),
-            (depth, box.height, columns),
-            (half, box.height, columns),
+            (4, tiles, half, height, LANES),
+            (tiles, depth, height, LANES),
+            (tiles, half, height, LANES),
         ],
         [box.scratch(half)],
         coeff,
     )
     params = [coeff, *params]
-    first_end, second_end = ordered(end, core_swapped(end), second)
-    joined = run(
-        functools.partial(pair_body, box, first),
-        (depth, rows, columns),
+    joined, first_end = run(
+        functools.partial(pair_body, box),
+        [(tiles, depth, rows, LANES)] * 2,
         [box.scratch()] + coarse_scratch(box),
-        first_end,
-        second_start,
-        second_end,
+        end,
+        core_swapped(end),
+        starts,
         *params,
     )
-    own_first = row_slice(first_end, side - first, side - first + rows)
-    result_first, result_second = own_first, joined
-    leaving = joined
+    ends = jnp.where(second, joined, first_end)
+    ends = jnp.concatenate([ends[i] for i in range(tiles)], axis=-1)
+    base = lax.axis_index("slab") * own_depth
+    result, leaving = lax.dynamic_slice_in_dim(ends, base, own_depth, 0)[None], joined
     for turn in range(1, windows // 2):
-        arrived = lax.ppermute(
-            leaving, "tm", [(i, (i + 2) % windows) for i in range(windows)]
-        )
-        arrived = with_rows(arrived, 2 * COARSE_REACH, side)
-        mine = place // 2 == turn
-        error = arrived - first_start
-        once, twice = run(
-            functools.partial(last_body, box),
-            [(depth, rows, columns)] * 2,
+        arrived = next_pair(leaving, 2 * COARSE_REACH)
+        out, leaving = run(
+            functools.partial(last_body, box, own_depth, turn),
+            [(1, own_depth, rows, columns), (tiles, depth, rows, LANES)],
             [box.scratch()] * 2 + coarse_scratch(box),
-            error,
+            first_end,
+            joined,
+            *arrived,
+            starts,
             *params,
         )
-        result_first = jnp.where(mine, own_first + once, result_first)
-        leaving = joined + twice
-        result_second = jnp.where(mine, leaving, result_second)
-    result = jnp.where(second, result_second, result_first)
-    return lax.dynamic_slice_in_dim(
-        result, lax.axis_index("slab") * own_depth, own_depth, 0
-    )[None]
+        result = out if turn == 1 else jnp.where(place // 2 >= turn, out, result)
+    return result
 
 
 def solution(mesh):

time: 64 us -> 63.9 us (level)
  waiting for transfers between devices: 22.3 us -> 18.5 us
  other arithmetic: 8.3 us -> 4.56 us
  starting transfers between devices: 14.3 us -> 17.1 us
  local copies, waits for them, and re-layouts: 1.85 us -> 4.28 us
  Pallas kernels: 16.8 us -> 18.7 us
    ppermute x6, waiting for transfers between devices: 20.2 us -> 16.9 us  [the longest x1 7.74 us: row_halo(): got_one = lax.ppermute(jnp.where(odd, down, up), 'coarse', one)]
    unnamed x6 -> x14, local copies, waits for them, and re-layouts: 0.01 us -> 2.74 us
    ppermute x6, starting transfers between devices: 14.1 us -> 16.3 us  [the longest x1 8.5 us: next_pair(): got_one = lax.ppermute(jnp.where(odd, down, up), both, one)]
    concatenate x3 -> x0, other arithmetic: 2.16 us -> none  [the longest x1 1.28 us: per_device(): coeff = jnp.concatenate([low_coeffs, high_coeffs], 0)]
    pallas_call x4, Pallas kernels: 16.8 us -> 18.7 us  [run(): pl.pallas_call(body, out_shape=[jax.ShapeDtypeStruct(shape, jnp.float32)...]
    another operation x0 -> x4, other arithmetic: none -> 1.87 us  [the longest x2 1.75 us: per_device(): jnp.stack([states[0], jnp.where(second, velocity[1], diffusivity), jnp.wh...]
    broadcast_in_dim x1 -> x0, other arithmetic: 1.52 us -> none  [per_device(): lax.dynamic_slice_in_dim(result, lax.axis_index('slab') * own_depth, own_...]
    select_n x9 -> x4, other arithmetic: 3.78 us -> 2.69 us  [the longest x1 1 us: next_pair(): got_two = lax.ppermute(jnp.where(odd, up, down), both, two)]
  transfers between devices with their start and end apart: 8 -> 10, of which waited for: 5 -> 5; matrix products, arithmetic and copies ran while one was open for 3% -> 3% of each run, Pallas kernels for 5% -> 5%
where the time goes in v2:
time: 63.9 us; the launch traced here: 63.2 us
  Pallas kernels  18.7 us (29%)
  waiting for transfers between devices  18.5 us (29%)
  starting transfers between devices  17.1 us (27%)
  other arithmetic  4.56 us (7%)
  local copies, waits for them, and re-layouts  4.28 us (7%)
    pallas_call x4, Pallas kernels, run(): pl.pallas_call(body, out_shape=[jax.ShapeDtypeStruct(shape, jnp.float32)...  18.7 us
    ppermute x1, starting transfers between devices, next_pair(): got_one = lax.ppermute(jnp.where(odd, down, up), both, one)  8.5 us
    ppermute x1, waiting for transfers between devices, row_halo(): got_one = lax.ppermute(jnp.where(odd, down, up), 'coarse', one)  7.74 us
    ppermute x1, waiting for transfers between devices, slab_blocks(): return [block, lax.ppermute(block, 'slab', [(0, 1), (1, 0)])]  4.84 us
    ppermute x1, starting transfers between devices, slab_blocks(): return [block, lax.ppermute(block, 'slab', [(0, 1), (1, 0)])]  3.03 us
    ppermute x1, waiting for transfers between devices, next_pair(): got_one = lax.ppermute(jnp.where(odd, down, up), both, one)  2.86 us
    unnamed x14, local copies, waits for them, and re-layouts  2.74 us
    ppermute x1, starting transfers between devices, row_halo(): got_one = lax.ppermute(jnp.where(odd, down, up), 'coarse', one)  1.89 us
  transfers between devices with their start and end apart: 10, of which 5 were waited for; matrix products, arithmetic and copies ran while one was open for 3% of the time, Pallas kernels for 5%

profile of v2, /device:TPU:0, one launch (start us, length us, event | category | flops | bytes accessed | tf_op | source)
XLA Modules:
  0.0 63.2 jit_solution(16807908988497630779)
XLA Ops:
  0.0 0.9 %slice_select_fusion.2 = f32[1,4,16,256]{3,2,1,0:T(8,128)S(1)} fusion(f32[3,4,16,256]{3,2,1,0:T(8,128)} %param.5, pred[]{:T(512)S(6)} %eq.11), kind=kLoop, calls=%fused_computation.16 | loop fusion | flops 16384 | bytes 196609 | tf_op jit(solution)/shard_map/jit(_where)/select_n | solution.py:527
  0.9 0.9 %fusion.2 = f32[1,4,16,256]{3,2,1,0:T(8,128)S(1)} fusion(f32[4,16,256]{2,1,0:T(8,128)} %param.4, f32[3,4,16,256]{3,2,1,0:T(8,128)} %param.5, pred[]{:T(512)S(6)} %eq.11), kind=kLoop, calls=%fused_computation.15 | loop fusion | flops 16384 | bytes 196609 | tf_op jit(solution)/shard_map/stack | solution.py:523
  1.8 0.9 %pad_maximum_fusion.3.refs_0_ = f32[3,4,16,256]{3,2,1,0:T(8,128)S(1)} fusion(f32[1,4,16,256]{3,2,1,0:T(8,128)S(1)} %slice_select_fusion.2, f32[1,4,16,256]{3,2,1,0:T(8,128)S(1)} %fusion.2, f32[1,4,16,256]{3,2,1,0:T(8,128)} %param.3), kind=kLoop, calls=%fused_computation.11 | loop fusion | flops 98304 | bytes 393216 | tf_op jit(solution)/shard_map/stack | solution.py:523
  2.6 3.0 %collective-permute-start = (f32[3,4,16,256]{3,2,1,0:T(8,128)S(1)}, f32[3,4,16,256]{3,2,1,0:T(8,128)S(1)}, u32[]{:S(2)}, u32[]{:S(2)}) collective-permute-start(f32[3,4,16,256]{3,2,1,0:T(8,128)S(1)} %pad_maximum_fusion.3.refs_0_), channel_id=1, source_target_pairs={{0,4},{4,0},{1,5},{5,1},{2,6},{6,2},{3,7},{7,3},{8,12},{12,8},{9,1... | collective-permute-start | bytes 589832 | tf_op jit(solution)/shard_map/ppermute | solution.py:447
  5.7 4.8 %collective-permute-done.refs_1_ = f32[3,4,16,256]{3,2,1,0:T(8,128)S(1)} collective-permute-done((f32[3,4,16,256]{3,2,1,0:T(8,128)S(1)}, f32[3,4,16,256]{3,2,1,0:T(8,128)S(1)}, u32[]{:S(2)}, u32[]{:S(2)}) %collective-permute-start) | collective-permute-done | bytes 196640 | tf_op jit(solution)/shard_map/ppermute | solution.py:447
  10.6 0.1 fusion.1
  10.7 1.9 %collective-permute-start.1 = (f32[2,3,4,14,256]{4,3,2,1,0:T(8,128)S(1)}, f32[2,3,4,14,256]{4,3,2,1,0:T(8,128)S(1)}, u32[]{:S(2)}, u32[]{:S(2)}) collective-permute-start(f32[2,3,4,14,256]{4,3,2,1,0:T(8,128)S(1)} %get-tuple-element.25), channel_id=1, source_target_pairs={{0,1},{1,0},{2,3},{3,2},{4,5},{5,4},{6,7},{7,6},{8,9},{9,8},{10,11... | collective-permute-start | bytes 1032200 | tf_op jit(solution)/shard_map/ppermute | solution.py:473
  12.6 0.7 %collective-permute-start.2 = (f32[2,3,4,14,256]{4,3,2,1,0:T(8,128)S(1)}, f32[2,3,4,14,256]{4,3,2,1,0:T(8,128)S(1)}, u32[]{:S(2)}, u32[]{:S(2)}) collective-permute-start(f32[2,3,4,14,256]{4,3,2,1,0:T(8,128)S(1)} %get-tuple-element.26), channel_id=1, source_target_pairs={{1,2},{2,1},{5,6},{6,5},{9,10},{10,9},{13,14},{14,13},{17,18},{18,... | collective-permute-start | bytes 1032200 | tf_op jit(solution)/shard_map/ppermute | solution.py:474
  13.3 7.7 %collective-permute-done.1 = f32[2,3,4,14,256]{4,3,2,1,0:T(8,128)S(1)} collective-permute-done((f32[2,3,4,14,256]{4,3,2,1,0:T(8,128)S(1)}, f32[2,3,4,14,256]{4,3,2,1,0:T(8,128)S(1)}, u32[]{:S(2)}, u32[]{:S(2)}) %collective-permute-start.1) | collective-permute-done | bytes 344096 | tf_op jit(solution)/shard_map/ppermute | solution.py:473
  21.0 0.1 select_bitcast_fusion.1
  21.1 0.5 copy.4
  21.6 0.1 collective-permute-start.5
  21.7 0.5 collective-permute-start.3
  22.2 0.1 collective-permute-start.4
  22.3 1.5 %collective-permute-done.5 = f32[2,2,3,4,14,256]{5,3,4,2,1,0:T(4,128)S(1)} collective-permute-done((f32[2,2,3,4,14,256]{5,3,4,2,1,0:T(4,128)S(1)}, f32[2,2,3,4,14,256]{5,3,4,2,1,0:T(4,128)S(1)}, u32[]{:S(2)}, u32[]{:S(2)}) %collective-permute-start.5) | collective-permute-done | bytes 688160 | tf_op jit(solution)/shard_map/ppermute | solution.py:488
  23.8 1.0 %copy.5.refs_5_ = f32[2,2,3,4,14,256]{5,4,3,2,1,0:T(8,128)} copy(f32[2,2,3,4,14,256]{5,3,4,2,1,0:T(4,128)S(1)} %collective-permute-done.5) | data formatting | bytes 1376256 | tf_op jit(solution)/shard_map/ppermute | solution.py:488
  24.9 0.7 %copy-done.4 = f32[3,4,16,256]{3,2,1,0:T(8,128)} copy-done((f32[3,4,16,256]{3,2,1,0:T(8,128)}, f32[3,4,16,256]{3,2,1,0:T(8,128)S(1)}, u32[]{:S(2)}) %copy-start.4) | copy-done | bytes 196632
  25.5 0.7 %copy-done.5 = f32[3,4,16,256]{3,2,1,0:T(8,128)} copy-done((f32[3,4,16,256]{3,2,1,0:T(8,128)}, f32[3,4,16,256]{3,2,1,0:T(8,128)S(1)}, u32[]{:S(2)}) %copy-start.5) | copy-done | bytes 196632
  26.2 5.6 %shard_map.37 = (f32[2,8,32,128]{3,2,1,0:T(8,128)}, f32[2,2,8,48,128]{4,3,2,1,0:T(8,128)}, f32[4,2,8,48,128]{4,3,2,1,0:T(8,128)}) custom-call(f32[3,4,16,256]{3,2,1,0:T(8,128)} %copy-done.1, f32[3,4,16,256]{3,2,1,0:T(8,128)} %copy-done.2, f32[2,2,3,4,14,256]{5,4,3,2,1,0:T(8,128)} %copy-done, f32[3,4,16,256]{3,2,1,0:T(8,128)} %copy-done.4, ...), custom_call_target="tpu_custom_call" | custom-call | tf_op jit(solution)/shard_map/pallas_call | solution.py:432
  31.9 0.1 collective-permute-start.6
  32.0 2.9 %shard_map.38 = (f32[4,2,4,48,128]{4,3,2,1,0:T(8,128)}, f32[2,8,48,128]{3,2,1,0:T(8,128)}, f32[2,4,48,128]{3,2,1,0:T(8,128)}) custom-call(f32[4,2,8,48,128]{4,3,2,1,0:T(8,128)} %get-tuple-element.16.coeff.rest_0_), custom_call_target="tpu_custom_call" | custom-call | tf_op jit(solution)/shard_map/pallas_call | solution.py:432
  34.9 0.7 %copy-done.3 = f32[2,8,32,128]{3,2,1,0:T(8,128)} copy-done((f32[2,8,32,128]{3,2,1,0:T(8,128)}, f32[2,8,32,128]{3,2,1,0:T(8,128)S(1)}, u32[]{:S(2)}) %copy-start.3) | copy-done | bytes 262168
  35.6 4.1 %shard_map.39 = (f32[2,8,16,128]{3,2,1,0:T(8,128)}, f32[2,8,16,128]{3,2,1,0:T(8,128)}) custom-call(f32[2,8,32,128]{3,2,1,0:T(8,128)} %get-tuple-element.14.own_end, f32[2,8,32,128]{3,2,1,0:T(8,128)} %copy-done.3, f32[2,2,8,48,128]{4,3,2,1,0:T(8,128)} %get-tuple-element.15.starts, f32[4,2,8,48,128]{4,3,2,1,0:T(8,128)} %get-tuple-element.16.coeff.rest_0_, ...), custom_call_target="tpu_custom_call" | custom-call | tf_op jit(solution)/shard_map/pallas_call | solution.py:432
  39.7 1.0 %slice_select_fusion = (f32[2,8,12,128]{3,2,1,0:T(8,128)S(1)}, f32[2,8,12,128]{3,2,1,0:T(8,128)S(1)}) fusion(f32[2,8,16,128]{3,2,1,0:T(8,128)} %get-tuple-element.21.joined, pred[]{:T(512)S(6)} %eq.12), kind=kLoop, calls=%fused_computation.12 | loop fusion | flops 49152 | bytes 393217 | tf_op jit(solution)/shard_map/jit(_where)/select_n | solution.py:508
  40.7 0.7 %collective-permute-start.9 = (f32[2,8,12,128]{3,2,1,0:T(8,128)S(1)}, f32[2,8,12,128]{3,2,1,0:T(8,128)S(1)}, u32[]{:S(2)}, u32[]{:S(2)}) collective-permute-start(f32[2,8,12,128]{3,2,1,0:T(8,128)S(1)} %get-tuple-element.33), channel_id=1, source_target_pairs={{1,18},{2,17},{9,26},{10,25},{17,2},{18,1},{25,10},{26,9},{5,22},{... | collective-permute-start | bytes 294920 | tf_op jit(solution)/shard_map/ppermute | solution.py:508
  41.4 8.5 %collective-permute-start.8 = (f32[2,8,12,128]{3,2,1,0:T(8,128)S(1)}, f32[2,8,12,128]{3,2,1,0:T(8,128)S(1)}, u32[]{:S(2)}, u32[]{:S(2)}) collective-permute-start(f32[2,8,12,128]{3,2,1,0:T(8,128)S(1)} %get-tuple-element.34), channel_id=1, source_target_pairs={{0,17},{1,16},{2,19},{3,18},{8,25},{9,24},{10,27},{11,26},{16,1},{... | collective-permute-start | bytes 294920 | tf_op jit(solution)/shard_map/ppermute | solution.py:507
  49.9 1.5 %collective-permute-start.7 = (f32[2,8,16,128]{3,2,1,0:T(8,128)}, f32[2,8,16,128]{3,2,1,0:T(8,128)S(1)}, u32[]{:S(2)}, u32[]{:S(2)}) collective-permute-start(f32[2,8,16,128]{3,2,1,0:T(8,128)} %get-tuple-element.21.joined), channel_id=1, source_target_pairs={{0,16},{8,24},{16,0},{24,8},{1,17},{9,25},{17,1},{25,9},{2,18},{10... | collective-permute-start | bytes 393224 | tf_op jit(solution)/shard_map/ppermute | solution.py:506
  51.4 2.9 %collective-permute-done.8 = f32[2,8,12,128]{3,2,1,0:T(8,128)S(1)} collective-permute-done((f32[2,8,12,128]{3,2,1,0:T(8,128)S(1)}, f32[2,8,12,128]{3,2,1,0:T(8,128)S(1)}, u32[]{:S(2)}, u32[]{:S(2)}) %collective-permute-start.8) | collective-permute-done | bytes 98336 | tf_op jit(solution)/shard_map/ppermute | solution.py:507
  54.3 0.7 %broadcast_select_fusion = (f32[2,8,12,128]{3,2,1,0:T(8,128)}, f32[2,8,12,128]{3,2,1,0:T(8,128)}) fusion(f32[2,8,12,128]{3,2,1,0:T(8,128)S(1)} %collective-permute-done.9, f32[2,8,12,128]{3,2,1,0:T(8,128)S(1)} %collective-permute-done.8, pred[]{:T(512)S(6)} %eq.12), kind=kLoop, calls=%fused_computation.17 | loop fusion | flops 49152 | bytes 393217 | tf_op jit(solution)/shard_map/jit(_where)/select_n | solution.py:509
  55.0 1.5 %collective-permute-done.7.centre = f32[2,8,16,128]{3,2,1,0:T(8,128)S(1)} collective-permute-done((f32[2,8,16,128]{3,2,1,0:T(8,128)}, f32[2,8,16,128]{3,2,1,0:T(8,128)S(1)}, u32[]{:S(2)}, u32[]{:S(2)}) %collective-permute-start.7) | collective-permute-done | bytes 131104 | tf_op jit(solution)/shard_map/ppermute | solution.py:506
  56.5 0.7 %copy-done.6 = f32[2,8,16,128]{3,2,1,0:T(8,128)} copy-done((f32[2,8,16,128]{3,2,1,0:T(8,128)}, f32[2,8,16,128]{3,2,1,0:T(8,128)S(1)}, u32[]{:S(2)}) %copy-start.6) | copy-done | bytes 131096
  57.1 6.0 %shard_map.40 = (f32[1,4,16,256]{3,2,1,0:T(8,128)}, f32[2,8,16,128]{3,2,1,0:T(8,128)}) custom-call(f32[2,8,16,128]{3,2,1,0:T(8,128)} %get-tuple-element.20.first_end, f32[2,8,16,128]{3,2,1,0:T(8,128)} %get-tuple-element.21.joined, f32[2,8,16,128]{3,2,1,0:T(8,128)} %copy-done.6, f32[2,8,12,128]{3,2,1,0:T(8,128)} %get-tuple-element.28.low, ...), custom_call_target="tpu_custom_call" | custom-call | tf_op jit(solution)/shard_map/pallas_call | solution.py:432
  (18 shorter events, 0.1 us)
Async XLA Ops:
  2.6 19.1 %copy-start.1 = (f32[3,4,16,256]{3,2,1,0:T(8,128)}, f32[3,4,16,256]{3,2,1,0:T(8,128)S(1)}, u32[]{:S(2)}) copy-start(f32[3,4,16,256]{3,2,1,0:T(8,128)S(1)} %pad_maximum_fusion.3.refs_0_) | copy-start | bytes 589828
  2.6 7.9 %collective-permute-start = (f32[3,4,16,256]{3,2,1,0:T(8,128)S(1)}, f32[3,4,16,256]{3,2,1,0:T(8,128)S(1)}, u32[]{:S(2)}, u32[]{:S(2)}) collective-permute-start(f32[3,4,16,256]{3,2,1,0:T(8,128)S(1)} %pad_maximum_fusion.3.refs_0_), channel_id=1, source_target_pairs={{0,4},{4,0},{1,5},{5,1},{2,6},{6,2},{3,7},{7,3},{8,12},{12,8},{9,1... | collective-permute-start | bytes 589832 | tf_op jit(solution)/shard_map/ppermute | solution.py:447
  10.6 11.6 %copy-start.2 = (f32[3,4,16,256]{3,2,1,0:T(8,128)}, f32[3,4,16,256]{3,2,1,0:T(8,128)S(1)}, u32[]{:S(2)}) copy-start(f32[3,4,16,256]{3,2,1,0:T(8,128)S(1)} %collective-permute-done.refs_1_) | copy-start | bytes 589828
  10.7 10.3 %collective-permute-start.1 = (f32[2,3,4,14,256]{4,3,2,1,0:T(8,128)S(1)}, f32[2,3,4,14,256]{4,3,2,1,0:T(8,128)S(1)}, u32[]{:S(2)}, u32[]{:S(2)}) collective-permute-start(f32[2,3,4,14,256]{4,3,2,1,0:T(8,128)S(1)} %get-tuple-element.25), channel_id=1, source_target_pairs={{0,1},{1,0},{2,3},{3,2},{4,5},{5,4},{6,7},{7,6},{8,9},{9,8},{10,11... | collective-permute-start | bytes 1032200 | tf_op jit(solution)/shard_map/ppermute | solution.py:473
  12.6 8.4 %collective-permute-start.2 = (f32[2,3,4,14,256]{4,3,2,1,0:T(8,128)S(1)}, f32[2,3,4,14,256]{4,3,2,1,0:T(8,128)S(1)}, u32[]{:S(2)}, u32[]{:S(2)}) collective-permute-start(f32[2,3,4,14,256]{4,3,2,1,0:T(8,128)S(1)} %get-tuple-element.26), channel_id=1, source_target_pairs={{1,2},{2,1},{5,6},{6,5},{9,10},{10,9},{13,14},{14,13},{17,18},{18,... | collective-permute-start | bytes 1032200 | tf_op jit(solution)/shard_map/ppermute | solution.py:474
  21.1 3.7 %copy-start = (f32[2,2,3,4,14,256]{5,4,3,2,1,0:T(8,128)}, f32[2,2,3,4,14,256]{5,4,3,2,1,0:T(8,128)S(1)}, u32[]{:S(2)}) copy-start(f32[2,2,3,4,14,256]{5,4,3,2,1,0:T(8,128)S(1)} %pad_maximum_fusion.refs_2_) | copy-start | bytes 2064388
  21.6 2.2 %collective-permute-start.5 = (f32[2,2,3,4,14,256]{5,3,4,2,1,0:T(4,128)S(1)}, f32[2,2,3,4,14,256]{5,3,4,2,1,0:T(4,128)S(1)}, u32[]{:S(2)}, u32[]{:S(2)}) collective-permute-start(f32[2,2,3,4,14,256]{5,3,4,2,1,0:T(4,128)S(1)} %copy.4), channel_id=1, source_target_pairs={{0,8},{8,0},{16,24},{24,16},{1,9},{9,1},{17,25},{25,17},{2,10},{10... | collective-permute-start | bytes 2064392 | tf_op jit(solution)/shard_map/ppermute | solution.py:488
  21.7 3.2 %collective-permute-start.3 = (f32[3,4,16,256]{3,2,1,0:T(8,128)S(1)}, f32[3,4,16,256]{3,2,1,0:T(8,128)S(1)}, u32[]{:S(2)}, u32[]{:S(2)}) collective-permute-start(f32[3,4,16,256]{3,2,1,0:T(8,128)S(1)} %pad_maximum_fusion.3.refs_0_), channel_id=1, source_target_pairs={{0,8},{8,0},{16,24},{24,16},{1,9},{9,1},{17,25},{25,17},{2,10},{10... | collective-permute-start | bytes 589832 | tf_op jit(solution)/shard_map/ppermute | solution.py:488
  22.2 2.7 %collective-permute-start.4 = (f32[3,4,16,256]{3,2,1,0:T(8,128)S(1)}, f32[3,4,16,256]{3,2,1,0:T(8,128)S(1)}, u32[]{:S(2)}, u32[]{:S(2)}) collective-permute-start(f32[3,4,16,256]{3,2,1,0:T(8,128)S(1)} %collective-permute-done.refs_1_), channel_id=1, source_target_pairs={{0,8},{8,0},{16,24},{24,16},{1,9},{9,1},{17,25},{25,17},{2,10},{10... | collective-permute-start | bytes 589832 | tf_op jit(solution)/shard_map/ppermute | solution.py:488
  24.9 0.7 %copy-start.4 = (f32[3,4,16,256]{3,2,1,0:T(8,128)}, f32[3,4,16,256]{3,2,1,0:T(8,128)S(1)}, u32[]{:S(2)}) copy-start(f32[3,4,16,256]{3,2,1,0:T(8,128)S(1)} %collective-permute-done.3.refs_3_) | copy-start | bytes 589828
  25.5 0.7 %copy-start.5 = (f32[3,4,16,256]{3,2,1,0:T(8,128)}, f32[3,4,16,256]{3,2,1,0:T(8,128)S(1)}, u32[]{:S(2)}) copy-start(f32[3,4,16,256]{3,2,1,0:T(8,128)S(1)} %collective-permute-done.4.refs_4_) | copy-start | bytes 589828
  31.9 3.1 %collective-permute-start.6 = (f32[2,8,32,128]{3,2,1,0:T(8,128)}, f32[2,8,32,128]{3,2,1,0:T(8,128)S(1)}, u32[]{:S(2)}, u32[]{:S(2)}) collective-permute-start(f32[2,8,32,128]{3,2,1,0:T(8,128)} %get-tuple-element.14.own_end), channel_id=1, source_target_pairs={{0,8},{8,0},{16,24},{24,16},{1,9},{9,1},{17,25},{25,17},{2,10},{10... | collective-permute-start | bytes 786440 | tf_op jit(solution)/shard_map/ppermute | solution.py:488
  34.9 0.7 %copy-start.3 = (f32[2,8,32,128]{3,2,1,0:T(8,128)}, f32[2,8,32,128]{3,2,1,0:T(8,128)S(1)}, u32[]{:S(2)}) copy-start(f32[2,8,32,128]{3,2,1,0:T(8,128)S(1)} %collective-permute-done.6.other_end) | copy-start | bytes 786436
  40.7 10.7 %collective-permute-start.9 = (f32[2,8,12,128]{3,2,1,0:T(8,128)S(1)}, f32[2,8,12,128]{3,2,1,0:T(8,128)S(1)}, u32[]{:S(2)}, u32[]{:S(2)}) collective-permute-start(f32[2,8,12,128]{3,2,1,0:T(8,128)S(1)} %get-tuple-element.33), channel_id=1, source_target_pairs={{1,18},{2,17},{9,26},{10,25},{17,2},{18,1},{25,10},{26,9},{5,22},{... | collective-permute-start | bytes 294920 | tf_op jit(solution)/shard_map/ppermute | solution.py:508
  41.4 12.9 %collective-permute-start.8 = (f32[2,8,12,128]{3,2,1,0:T(8,128)S(1)}, f32[2,8,12,128]{3,2,1,0:T(8,128)S(1)}, u32[]{:S(2)}, u32[]{:S(2)}) collective-permute-start(f32[2,8,12,128]{3,2,1,0:T(8,128)S(1)} %get-tuple-element.34), channel_id=1, source_target_pairs={{0,17},{1,16},{2,19},{3,18},{8,25},{9,24},{10,27},{11,26},{16,1},{... | collective-permute-start | bytes 294920 | tf_op jit(solution)/shard_map/ppermute | solution.py:507
  49.9 6.6 %collective-permute-start.7 = (f32[2,8,16,128]{3,2,1,0:T(8,128)}, f32[2,8,16,128]{3,2,1,0:T(8,128)S(1)}, u32[]{:S(2)}, u32[]{:S(2)}) collective-permute-start(f32[2,8,16,128]{3,2,1,0:T(8,128)} %get-tuple-element.21.joined), channel_id=1, source_target_pairs={{0,16},{8,24},{16,0},{24,8},{1,17},{9,25},{17,1},{25,9},{2,18},{10... | collective-permute-start | bytes 393224 | tf_op jit(solution)/shard_map/ppermute | solution.py:506
  56.5 0.7 %copy-start.6 = (f32[2,8,16,128]{3,2,1,0:T(8,128)}, f32[2,8,16,128]{3,2,1,0:T(8,128)S(1)}, u32[]{:S(2)}) copy-start(f32[2,8,16,128]{3,2,1,0:T(8,128)S(1)} %collective-permute-done.7.centre) | copy-start | bytes 393220

commit v3 on v2

--- a/solution.py
+++ b/solution.py
@@ -135,46 +135,83 @@
     field[...] = jnp.zeros_like(field)
 
 
+def gather_body(states, diffusivity, velocity, parcel, sem):
+    core = lax.axis_index("tm") % 2
+    start = pltpu.make_async_copy(states, parcel.at[pl.ds(0, 1)], sem.at[0])
+    start.start()
+
+    @pl.when(core == 0)
+    def _():
+        one = pltpu.make_async_copy(diffusivity, parcel.at[1], sem.at[1])
+        two = pltpu.make_async_copy(velocity.at[0], parcel.at[2], sem.at[2])
+        one.start()
+        two.start()
+        one.wait()
+        two.wait()
+
+    @pl.when(core == 1)
+    def _():
+        both = pltpu.make_async_copy(
+            velocity.at[pl.ds(1, 2)], parcel.at[pl.ds(1, 2)], sem.at[1]
+        )
+        both.start()
+        both.wait()
+
+    start.wait()
+
+
+def row_places(box, sizes):
+    place, count = lax.axis_index("coarse"), lax.axis_size("coarse")
+    odd = place % 2
+    result = []
+    gone = 0
+    for step, size in enumerate(sizes, 1):
+        below = pl.multiple_of(box.side - gone - size, 8)
+        above = pl.multiple_of(box.side + box.rows + gone, 8)
+        gone += size
+        one = pl.multiple_of(jnp.where(odd == 1, below, above), 8)
+        two = pl.multiple_of(jnp.where(odd == 1, above, below), 8)
+        below_valid, above_valid = place >= step, place + step < count
+        one_valid = jnp.where(odd == 1, below_valid, above_valid)
+        two_valid = jnp.where(odd == 1, above_valid, below_valid)
+        result.append(((one, one_valid), (two, two_valid)))
+    return result
+
+
 def fine_body(box, margin, own_depth, blocks, *refs):
-    own, own_halo = refs[:blocks], refs[blocks]
-    other, other_halo = refs[blocks + 1 : 2 * blocks + 1], refs[2 * blocks + 1]
-    end, starts, coeff, one, two = refs[2 * blocks + 2 :]
+    end, starts, coeff, one, two = refs[-5:]
+    half = (len(refs) - 5) // 2
+    each = half // blocks
     core = lax.axis_index("tm") % 2
     shift = lax.axis_index("slab") if blocks == 2 else 0
-    rows, side = box.rows, box.side
-    width = own_halo.shape[-2]
+    places = row_places(box, [refs[at].shape[-2] for at in range(1, each, 2)])
     clear(one)
     clear(two)
-    inner = slice(PAD, PAD + box.height)
-    if width < side:
-        zeros = jnp.zeros((box.tiles, box.depth, 8, LANES), jnp.float32)
-        for array in range(4):
-            coeff[array, :, :, 0:8, :] = zeros
-            coeff[array, :, :, box.height - 8 :, :] = zeros
-        for array in range(2):
-            starts[array, :, :, 0:8, :] = zeros
-            starts[array, :, :, box.height - 8 :, :] = zeros
-    for pieces, halo, rank in ((own, own_halo, core), (other, other_halo, 1 - core)):
+    for side, rank in ((0, core), (1, 1 - core)):
         for block in range(blocks):
+            pieces = refs[side * half + block * each : side * half + (block + 1) * each]
             base = (block + shift) % blocks * own_depth
-            for plane in range(own_depth):
-                for i in range(box.tiles):
-                    cols = slice(i * LANES, (i + 1) * LANES)
-                    for array in range(3):
-                        centre = pieces[block][array, plane, :, cols]
-                        low = halo[0, block, array, plane, :, cols]
-                        high = halo[1, block, array, plane, :, cols]
-                        targets = []
-                        if array == 0:
-                            targets.append((starts.at[rank, i, base + plane], 0))
-                            if pieces is own:
-                                targets.append((one.at[i, base + plane + 2], PAD))
-                        else:
-                            targets.append((coeff.at[2 * rank + array - 1, i, base + plane], 0))
-                        for target, at in targets:
-                            target[at + side - width : at + side, :] = low
-                            target[at + side : at + side + rows, :] = centre
-                            target[at + side + rows : at + side + rows + width, :] = high
+            moves = [(pieces[0], box.side, None)]
+            for step, pair in enumerate(places):
+                for ref, (at, valid) in zip(pieces[1 + 2 * step : 3 + 2 * step], pair):
+                    moves.append((ref, at, valid))
+            for ref, at, valid in moves:
+                size = ref.shape[-2]
+                for plane in range(own_depth):
+                    for i in range(box.tiles):
+                        cols = slice(i * LANES, (i + 1) * LANES)
+                        for array in range(3):
+                            value = ref[array, plane, :, cols]
+                            if valid is not None:
+                                value = jnp.where(valid, value, 0.0)
+                            if array == 0:
+                                starts[rank, i, base + plane, pl.ds(at, size), :] = value
+                                if side == 0:
+                                    one[i, base + plane + 2, pl.ds(PAD + at, size), :] = value
+                            else:
+                                coeff[
+                                    2 * rank + array - 1, i, base + plane, pl.ds(at, size), :
+                                ] = value
     scales, carries, tildes = chebyshev_coefficients(SECTIONS)
     stage = 0
     current, other = one, two
@@ -340,8 +377,8 @@
 
 
 def pair_body(box, own_end, other_end, starts, *rest):
-    params, out, first_out = rest[:4], rest[4], rest[5]
-    source, trial, pairs, guess, residual = rest[6:]
+    params, out, first_out, leaving = rest[:4], rest[4], rest[5], rest[6]
+    source, trial, pairs, guess, residual = rest[7:]
     core = lax.axis_index("tm") % 2
     clear(source)
     clear(trial)
@@ -370,11 +407,14 @@
         out[where] = value + out[where]
 
     coarse_step_body(box, 0, source, trial, pairs, guess, residual, params, finish)
-
-
-def last_body(box, own_depth, turn, first_end, joined, centre, low, high, starts, *rest):
-    params, result, leaving = rest[:4], rest[4], rest[5]
-    source, second, trial, pairs, guess, residual = rest[6:]
+    half = box.depth // 2
+    leaving[...] = out[:, pl.ds(core * half, half)]
+
+
+def last_body(box, own_depth, turn, pieces, first_end, joined, *rest):
+    arrived, rest = rest[:pieces], rest[pieces:]
+    starts, params, result, leaving = rest[0], rest[1:5], rest[5], rest[6]
+    source, second, trial, pairs, guess, residual, total = rest[7:]
     place = lax.axis_index("tm")
     core = place % 2
     active = place // 2 == turn
@@ -384,18 +424,29 @@
     clear(pairs)
     clear(guess)
     side, rows = box.side, box.rows
-    width = low.shape[-2]
+    half = box.depth // 2
+    each = pieces // 2
+    places = row_places(box, [arrived[at].shape[-2] for at in range(1, each, 2)])
 
     @pl.when(active)
     def _():
-        for value, at, size in (
-            (low, side - width, width),
-            (centre, side, rows),
-            (high, side + rows, width),
-        ):
-            source[:, 2 : 2 + box.depth, PAD + at : PAD + at + size, :] = (
-                value[...] - starts[0, :, :, at : at + size, :]
-            )
+        for part, rank in ((0, core), (1, 1 - core)):
+            moves = [(arrived[part * each], side, None)]
+            for step, pair in enumerate(places):
+                at = part * each + 1 + 2 * step
+                for ref, (where, valid) in zip(arrived[at : at + 2], pair):
+                    moves.append((ref, where, valid))
+            base = rank * half
+            for ref, at, valid in moves:
+                size = ref.shape[-2]
+                for plane in range(half):
+                    for i in range(box.tiles):
+                        value = ref[i, plane]
+                        if valid is not None:
+                            value = jnp.where(valid, value, 0.0)
+                        source[i, base + plane + 2, pl.ds(PAD + at, size), :] = (
+                            value - starts[0, i, base + plane, pl.ds(at, size), :]
+                        )
 
     def finish_once(plane, i, at, size, value):
         second[i, plane + 2, pl.ds(PAD + at, size), :] = value
@@ -406,7 +457,7 @@
 
     def finish_twice(plane, i, at, size, value):
         where = (i, plane, pl.ds(at - box.side, size), slice(None))
-        leaving[where] = value + joined[where]
+        total[where] = value + joined[where]
 
     coarse_step_body(box, 0, second, trial, pairs, guess, residual, params, finish_twice)
     base = lax.axis_index("slab") * own_depth
@@ -422,21 +473,20 @@
     @pl.when(core == 1)
     def _():
         for i in range(box.tiles):
-            result[0, :, :, i * LANES : (i + 1) * LANES] = leaving[i, pl.ds(base, own_depth)]
-
-
-def run(body, outs, scratch, *args):
-    whole = pl.BlockSpec(memory_space=pltpu.VMEM)
-    single = not isinstance(outs, list)
-    shapes = [outs] if single else outs
-    result = pl.pallas_call(
+            result[0, :, :, i * LANES : (i + 1) * LANES] = total[i, pl.ds(base, own_depth)]
+
+    leaving[...] = total[:, pl.ds(core * half, half)]
+
+
+def run(body, outs, scratch, *args, space=pltpu.VMEM):
+    return pl.pallas_call(
         body,
-        out_shape=[jax.ShapeDtypeStruct(shape, jnp.float32) for shape in shapes],
-        in_specs=[whole] * len(args),
-        out_specs=[whole] * len(shapes),
+        out_shape=[jax.ShapeDtypeStruct(shape, jnp.float32) for shape in outs],
+        in_specs=[pl.BlockSpec(memory_space=space)] * len(args),
+        out_specs=[pl.BlockSpec(memory_space=pltpu.VMEM)] * len(outs),
         scratch_shapes=scratch,
+        compiler_params=pltpu.CompilerParams(vmem_limit_bytes=20 * 1024 * 1024),
     )(*args)
-    return result[0] if single else result
 
 
 def slab_blocks(block):
@@ -449,37 +499,44 @@
     return [gathered[i] for i in range(count)]
 
 
-def row_slice(block, first, last):
-    return lax.slice_in_dim(block, first, last, axis=block.ndim - 2)
-
-
-def row_pairs(count):
-    one = [(i, i ^ 1) for i in range(count) if i ^ 1 < count]
-    two = [(i, i + 1 if i % 2 else i - 1) for i in range(count)]
-    return one, [(i, j) for i, j in two if 0 <= j < count]
-
-
-def row_halo(blocks, width):
-    rows = blocks[0].shape[-2]
+def row_swaps(hop, away):
+    windows, count = lax.axis_size("tm"), lax.axis_size("coarse")
+    rounds = []
+    for first in (0, 1):
+        pairs = []
+        for place in range(count):
+            other = place + 1 if place % 2 == first else place - 1
+            for t in range(windows):
+                inside = 0 <= other < count
+                target = (hop(t), other) if inside else (away(t), place)
+                pairs.append((t * count + place, target[0] * count + target[1]))
+        rounds.append(pairs)
+    return rounds
+
+
+def row_pieces(block, width, rounds):
+    rows = block.shape[-2]
+    axis = block.ndim - 2
+    both = ("tm", "coarse")
     odd = lax.axis_index("coarse") % 2 == 1
-    one, two = row_pairs(lax.axis_size("coarse"))
-    low, high = [], []
-    from_low, from_high = blocks, blocks
+    pieces = []
+    up, down = block, block
     left = width
     while left > 0:
         size = min(rows, left)
-        up = jnp.stack([row_slice(b, b.shape[-2] - size, b.shape[-2]) for b in from_low])
-        down = jnp.stack([row_slice(b, 0, size) for b in from_high])
-        got_one = lax.ppermute(jnp.where(odd, down, up), "coarse", one)
-        got_two = lax.ppermute(jnp.where(odd, up, down), "coarse", two)
-        low.insert(0, jnp.where(odd, got_one, got_two))
-        high.append(jnp.where(odd, got_two, got_one))
-        from_low, from_high = list(low[0]), list(high[-1])
+        if size == rows and up is down:
+            send_one = send_two = block
+        else:
+            high = lax.slice_in_dim(up, up.shape[axis] - size, None, axis=axis)
+            low = lax.slice_in_dim(down, 0, size, axis=axis)
+            send_one, send_two = jnp.where(odd, low, high), jnp.where(odd, high, low)
+        got_one = lax.ppermute(send_one, both, rounds[0])
+        got_two = lax.ppermute(send_two, both, rounds[1])
+        pieces += [got_one, got_two]
         left -= size
-    low, high = (
-        x[0] if len(x) == 1 else jnp.concatenate(x, axis=x[0].ndim - 2) for x in (low, high)
-    )
-    return jnp.stack([low, high])
+        if left > 0:
+            up, down = jnp.where(odd, got_one, got_two), jnp.where(odd, got_two, got_one)
+    return pieces
 
 
 def core_swapped(block):
@@ -488,49 +545,30 @@
     return lax.ppermute(block, "tm", [(i, i ^ 1) for i in range(count)])
 
 
-def next_pair(block, width):
-    windows, count = lax.axis_size("tm"), lax.axis_size("coarse")
-    rows = block.shape[-2]
-    hop = [(t, (t + 2) % windows) for t in range(windows)]
-    if width > rows:
-        centre = lax.ppermute(block, "tm", hop)
-        halo = row_halo([centre], width)
-        return centre, halo[0, 0], halo[1, 0]
-    odd = lax.axis_index("coarse") % 2 == 1
-    both = ("tm", "coarse")
-    one, two = (
-        [(t * count + i, u * count + j) for t, u in hop for i, j in pairs]
-        for pairs in row_pairs(count)
-    )
-    up, down = row_slice(block, rows - width, rows), row_slice(block, 0, width)
-    centre = lax.ppermute(block, "tm", hop)
-    got_one = lax.ppermute(jnp.where(odd, down, up), both, one)
-    got_two = lax.ppermute(jnp.where(odd, up, down), both, two)
-    return centre, jnp.where(odd, got_one, got_two), jnp.where(odd, got_two, got_one)
-
-
 def per_device(states, diffusivity, velocity):
     windows = lax.axis_size("tm")
     place = lax.axis_index("tm")
-    second = place % 2 == 1
     own_depth, rows, columns = diffusivity.shape
-    reach = FINE_REACH + COARSE_REACH
-    side = round_up(max(reach, 2 * COARSE_REACH), 8)
+    side = round_up(FINE_REACH + COARSE_REACH, 8)
     depth = own_depth * lax.axis_size("slab")
     box = Box(depth, rows, side, columns)
     tiles, height, half = box.tiles, box.height, depth // 2
 
-    parcel = jnp.stack(
-        [
-            states[0],
-            jnp.where(second, velocity[1], diffusivity),
-            jnp.where(second, velocity[2], velocity[0]),
-        ]
-    )
+    (parcel,) = run(
+        gather_body,
+        [(3, own_depth, rows, columns)],
+        [pltpu.SemaphoreType.DMA((3,))],
+        states,
+        diffusivity,
+        velocity,
+        space=pl.ANY,
+    )
+    rounds = row_swaps(lambda t: t, lambda t: t ^ 1)
     blocks = slab_blocks(parcel)
-    other_blocks = [core_swapped(block) for block in blocks]
-    halo = row_halo(blocks, reach)
-    other_halo = core_swapped(halo)
+    own_pieces = []
+    for block in blocks:
+        own_pieces += [block, *row_pieces(block, side, rounds)]
+    other_pieces = [core_swapped(piece) for piece in own_pieces]
 
     first, last = box.span(COARSE_REACH)
     end, starts, coeff = run(
@@ -541,10 +579,8 @@
             (4, tiles, depth, height, LANES),
         ],
         [box.scratch(), box.scratch()],
-        *blocks,
-        halo,
-        *other_blocks,
-        other_halo,
+        *own_pieces,
+        *other_pieces,
     )
     params = run(
         functools.partial(prepare_body, box),
@@ -557,25 +593,35 @@
         coeff,
     )
     params = [coeff, *params]
-    joined, first_end = run(
+    joined, first_end, leaving = run(
         functools.partial(pair_body, box),
-        [(tiles, depth, rows, LANES)] * 2,
+        [(tiles, depth, rows, LANES)] * 2 + [(tiles, half, rows, LANES)],
         [box.scratch()] + coarse_scratch(box),
         end,
         core_swapped(end),
         starts,
         *params,
     )
-    ends = jnp.where(second, joined, first_end)
+    ends = jnp.where(place % 2 == 1, joined, first_end)
     ends = jnp.concatenate([ends[i] for i in range(tiles)], axis=-1)
     base = lax.axis_index("slab") * own_depth
-    result, leaving = lax.dynamic_slice_in_dim(ends, base, own_depth, 0)[None], joined
+    result = lax.dynamic_slice_in_dim(ends, base, own_depth, 0)[None]
+    hop = lambda t: (t + 2) % windows
+    rounds = row_swaps(hop, hop)
     for turn in range(1, windows // 2):
-        arrived = next_pair(leaving, 2 * COARSE_REACH)
+        centre = lax.ppermute(leaving, "tm", [(t, hop(t)) for t in range(windows)])
+        if rows >= 2 * COARSE_REACH:
+            arrived = [centre, *row_pieces(leaving, min(rows, side), rounds)]
+        else:
+            near = row_swaps(lambda t: t, lambda t: t ^ 1)
+            arrived = [centre, *row_pieces(centre, side, near)]
+        arrived += [core_swapped(piece) for piece in arrived]
         out, leaving = run(
-            functools.partial(last_body, box, own_depth, turn),
-            [(1, own_depth, rows, columns), (tiles, depth, rows, LANES)],
-            [box.scratch()] * 2 + coarse_scratch(box),
+            functools.partial(last_body, box, own_depth, turn, len(arrived)),
+            [(1, own_depth, rows, columns), (tiles, half, rows, LANES)],
+            [box.scratch()] * 2
+            + coarse_scratch(box)
+            + [pltpu.VMEM((tiles, depth, rows, LANES), jnp.float32)],
             first_end,
             joined,
             *arrived,

time: 63.9 us -> 38.7 us (0.61)
  Pallas kernels: 18.7 us -> 8.41 us
  waiting for transfers between devices: 18.5 us -> 11.3 us
  other arithmetic: 4.56 us -> 0 us
  local copies, waits for them, and re-layouts: 4.28 us -> 2.6 us
  starting transfers between devices: 17.1 us -> 16.1 us
    pallas_call x4 -> x5, Pallas kernels: 18.7 us -> 8.41 us  [run(): pl.pallas_call(body, out_shape=[jax.ShapeDtypeStruct(shape, jnp.float32)...]
    ppermute x5 -> x7, waiting for transfers between devices: 12.1 us -> 6.09 us  [the longest x3 4.89 us: row_pieces(): got_one = lax.ppermute(send_one, both, rounds[0])]
    ppermute x1, waiting for transfers between devices: 4.84 us -> 1.74 us  [slab_blocks(): return [block, lax.ppermute(block, 'slab', [(0, 1), (1, 0)])]]
    select_n x4 -> x0, other arithmetic: 2.69 us -> none  [the longest x1 1 us: next_pair(): got_two = lax.ppermute(jnp.where(odd, up, down), both, two)]
    ppermute x4 -> x10, waiting for transfers between devices: 1.55 us -> 3.43 us  [core_swapped(): return lax.ppermute(block, 'tm', [(i, i ^ 1) for i in range(count)])]
    another operation x4 -> x0, other arithmetic: 1.87 us -> none  [the longest x2 1.75 us: per_device(): jnp.stack([states[0], jnp.where(second, velocity[1], diffusivity), jnp.wh...]
    ppermute x5 -> x7, starting transfers between devices: 13.3 us -> 11.8 us  [the longest x3 8.22 us: row_pieces(): got_one = lax.ppermute(send_one, both, rounds[0])]
    ppermute x1 -> x0, local copies, waits for them, and re-layouts: 1.03 us -> none  [core_swapped(): return lax.ppermute(block, 'tm', [(i, i ^ 1) for i in range(count)])]
  transfers between devices with their start and end apart: 10 -> 18, of which waited for: 5 -> 9; matrix products, arithmetic and copies ran while one was open for 3% -> 0% of each run, Pallas kernels for 5% -> 2%
where the time goes in v3:
time: 38.7 us; the launch traced here: 38.4 us
  starting transfers between devices  16.1 us (42%)
  waiting for transfers between devices  11.3 us (29%)
  Pallas kernels  8.41 us (22%)
  local copies, waits for them, and re-layouts  2.6 us (7%)
    pallas_call x5, Pallas kernels, run(): pl.pallas_call(body, out_shape=[jax.ShapeDtypeStruct(shape, jnp.float32)...  8.41 us
    ppermute x3, starting transfers between devices, row_pieces(): got_one = lax.ppermute(send_one, both, rounds[0])  8.22 us
    ppermute x3, waiting for transfers between devices, row_pieces(): got_one = lax.ppermute(send_one, both, rounds[0])  4.89 us
    ppermute x10, waiting for transfers between devices, core_swapped(): return lax.ppermute(block, 'tm', [(i, i ^ 1) for i in range(count)])  3.43 us
    ppermute x1, starting transfers between devices, slab_blocks(): return [block, lax.ppermute(block, 'slab', [(0, 1), (1, 0)])]  3.03 us
    unnamed x6, local copies, waits for them, and re-layouts  2.6 us
    ppermute x3, starting transfers between devices, row_pieces(): got_two = lax.ppermute(send_two, both, rounds[1])  2.09 us
    ppermute x1, waiting for transfers between devices, slab_blocks(): return [block, lax.ppermute(block, 'slab', [(0, 1), (1, 0)])]  1.74 us
  transfers between devices with their start and end apart: 18, of which 9 were waited for; matrix products, arithmetic and copies ran while one was open for 0% of the time, Pallas kernels for 2%

profile of v3, /device:TPU:0, one launch (start us, length us, event | category | flops | bytes accessed | tf_op | source)
XLA Modules:
  0.0 38.4 jit_solution(3720326734306238021)
XLA Ops:
  0.0 0.9 %copy-done = f32[3,4,16,256]{3,2,1,0:T(8,128)S(1)} copy-done((f32[3,4,16,256]{3,2,1,0:T(8,128)S(1)}, f32[3,4,16,256]{3,2,1,0:T(8,128)}, u32[]{:S(2)}) %copy-start) | copy-done | bytes 196632
  0.9 0.8 %copy-done.1 = f32[1,4,16,256]{3,2,1,0:T(8,128)S(1)} copy-done((f32[1,4,16,256]{3,2,1,0:T(8,128)S(1)}, f32[1,4,16,256]{3,2,1,0:T(8,128)}, u32[]{:S(2)}) %copy-start.1) | copy-done | bytes 65560
  1.8 0.8 %copy-done.2 = f32[4,16,256]{2,1,0:T(8,128)S(1)} copy-done((f32[4,16,256]{2,1,0:T(8,128)S(1)}, f32[4,16,256]{2,1,0:T(8,128)}, u32[]{:S(2)}) %copy-start.2) | copy-done | bytes 65560
  2.6 0.3 shard_map.37.refs_0_
  2.9 3.0 %collective-permute-start.2 = (f32[3,4,16,256]{3,2,1,0:T(8,128)S(1)}, f32[3,4,16,256]{3,2,1,0:T(8,128)S(1)}, u32[]{:S(2)}, u32[]{:S(2)}) collective-permute-start(f32[3,4,16,256]{3,2,1,0:T(8,128)S(1)} %shard_map.37.refs_0_), channel_id=1, source_target_pairs={{0,4},{4,0},{1,5},{5,1},{2,6},{6,2},{3,7},{7,3},{8,12},{12,8},{9,1... | collective-permute-start | bytes 589832 | tf_op jit(solution)/shard_map/ppermute | solution.py:497
  5.9 0.0 collective-permute-start.5
  5.9 0.5 %collective-permute-start.1 = (f32[3,4,16,256]{3,2,1,0:T(8,128)S(1)}, f32[3,4,16,256]{3,2,1,0:T(8,128)S(1)}, u32[]{:S(2)}, u32[]{:S(2)}) collective-permute-start(f32[3,4,16,256]{3,2,1,0:T(8,128)S(1)} %shard_map.37.refs_0_), channel_id=1, source_target_pairs={{0,8},{8,0},{16,24},{24,16},{1,2},{9,10},{17,18},{25,26},{2,1},{10... | collective-permute-start | bytes 589832 | tf_op jit(solution)/shard_map/ppermute | solution.py:534
  6.4 2.6 %collective-permute-start = (f32[3,4,16,256]{3,2,1,0:T(8,128)S(1)}, f32[3,4,16,256]{3,2,1,0:T(8,128)S(1)}, u32[]{:S(2)}, u32[]{:S(2)}) collective-permute-start(f32[3,4,16,256]{3,2,1,0:T(8,128)S(1)} %shard_map.37.refs_0_), channel_id=1, source_target_pairs={{0,1},{8,9},{16,17},{24,25},{1,0},{9,8},{17,16},{25,24},{2,3},{10,... | collective-permute-start | bytes 589832 | tf_op jit(solution)/shard_map/ppermute | solution.py:533
  9.1 1.7 %collective-permute-done.2.refs_3_ = f32[3,4,16,256]{3,2,1,0:T(8,128)S(1)} collective-permute-done((f32[3,4,16,256]{3,2,1,0:T(8,128)S(1)}, f32[3,4,16,256]{3,2,1,0:T(8,128)S(1)}, u32[]{:S(2)}, u32[]{:S(2)}) %collective-permute-start.2) | collective-permute-done | bytes 196640 | tf_op jit(solution)/shard_map/ppermute | solution.py:497
  10.8 3.4 %collective-permute-start.3 = (f32[3,4,16,256]{3,2,1,0:T(8,128)S(1)}, f32[3,4,16,256]{3,2,1,0:T(8,128)S(1)}, u32[]{:S(2)}, u32[]{:S(2)}) collective-permute-start(f32[3,4,16,256]{3,2,1,0:T(8,128)S(1)} %collective-permute-done.2.refs_3_), channel_id=1, source_target_pairs={{0,1},{8,9},{16,17},{24,25},{1,0},{9,8},{17,16},{25,24},{2,3},{10,... | collective-permute-start | bytes 589832 | tf_op jit(solution)/shard_map/ppermute | solution.py:533
  14.2 0.0 collective-permute-done.5.refs_6_
  14.2 0.0 collective-permute-start.8
  14.2 0.0 collective-permute-done.1.refs_2_
  14.2 0.5 %collective-permute-start.7 = (f32[3,4,16,256]{3,2,1,0:T(8,128)S(1)}, f32[3,4,16,256]{3,2,1,0:T(8,128)S(1)}, u32[]{:S(2)}, u32[]{:S(2)}) collective-permute-start(f32[3,4,16,256]{3,2,1,0:T(8,128)S(1)} %collective-permute-done.1.refs_2_), channel_id=1, source_target_pairs={{0,8},{8,0},{16,24},{24,16},{1,9},{9,1},{17,25},{25,17},{2,10},{10... | collective-permute-start | bytes 589832 | tf_op jit(solution)/shard_map/ppermute | solution.py:545
  14.7 0.1 collective-permute-done.refs_1_
  14.8 0.0 collective-permute-start.6
  14.8 0.5 %collective-permute-start.10 = (f32[3,4,16,256]{3,2,1,0:T(8,128)S(1)}, f32[3,4,16,256]{3,2,1,0:T(8,128)S(1)}, u32[]{:S(2)}, u32[]{:S(2)}) collective-permute-start(f32[3,4,16,256]{3,2,1,0:T(8,128)S(1)} %collective-permute-done.4.refs_5_), channel_id=1, source_target_pairs={{0,8},{8,0},{16,24},{24,16},{1,9},{9,1},{17,25},{25,17},{2,10},{10... | collective-permute-start | bytes 589832 | tf_op jit(solution)/shard_map/ppermute | solution.py:545
  15.3 3.3 %collective-permute-done.3.refs_4_ = f32[3,4,16,256]{3,2,1,0:T(8,128)S(1)} collective-permute-done((f32[3,4,16,256]{3,2,1,0:T(8,128)S(1)}, f32[3,4,16,256]{3,2,1,0:T(8,128)S(1)}, u32[]{:S(2)}, u32[]{:S(2)}) %collective-permute-start.3) | collective-permute-done | bytes 196640 | tf_op jit(solution)/shard_map/ppermute | solution.py:533
  18.6 1.4 %collective-permute-done.9.refs_10_ = f32[3,4,16,256]{3,2,1,0:T(8,128)S(1)} collective-permute-done((f32[3,4,16,256]{3,2,1,0:T(8,128)S(1)}, f32[3,4,16,256]{3,2,1,0:T(8,128)S(1)}, u32[]{:S(2)}, u32[]{:S(2)}) %collective-permute-start.9) | collective-permute-done | bytes 196640 | tf_op jit(solution)/shard_map/ppermute | solution.py:545
  20.0 2.5 %shard_map.38 = (f32[2,8,32,128]{3,2,1,0:T(8,128)S(1)}, f32[2,2,8,48,128]{4,3,2,1,0:T(8,128)S(1)}, f32[4,2,8,48,128]{4,3,2,1,0:T(8,128)S(1)}) custom-call(f32[3,4,16,256]{3,2,1,0:T(8,128)S(1)} %shard_map.37.refs_0_, f32[3,4,16,256]{3,2,1,0:T(8,128)S(1)} %collective-permute-done.refs_1_, f32[3,4,16,256]{3,2,1,0:T(8,128)S(1)} %collective-permute-done.1.refs_2_, ...), custom_call_target="tpu_custom_call" | custom-call | tf_op jit(solution)/shard_map/pallas_call | solution.py:482
  22.5 0.2 collective-permute-start.11
  22.7 0.6 %shard_map.39 = (f32[4,2,4,48,128]{4,3,2,1,0:T(8,128)S(1)}, f32[2,8,48,128]{3,2,1,0:T(8,128)S(1)}, f32[2,4,48,128]{3,2,1,0:T(8,128)S(1)}) custom-call(f32[4,2,8,48,128]{4,3,2,1,0:T(8,128)S(1)} %get-tuple-element.17.coeff.rest_0_.rest_7_), custom_call_target="tpu_custom_call" | custom-call | tf_op jit(solution)/shard_map/pallas_call | solution.py:482
  23.3 0.8 %collective-permute-done.11.other_end = f32[2,8,32,128]{3,2,1,0:T(8,128)S(1)} collective-permute-done((f32[2,8,32,128]{3,2,1,0:T(8,128)S(1)}, f32[2,8,32,128]{3,2,1,0:T(8,128)S(1)}, u32[]{:S(2)}, u32[]{:S(2)}) %collective-permute-start.11) | collective-permute-done | bytes 262176 | tf_op jit(solution)/shard_map/ppermute | solution.py:545
  24.1 1.3 %shard_map.40 = (f32[2,8,16,128]{3,2,1,0:T(8,128)S(1)}, f32[2,8,16,128]{3,2,1,0:T(8,128)S(1)}, f32[2,4,16,128]{3,2,1,0:T(8,128)S(1)}) custom-call(f32[2,8,32,128]{3,2,1,0:T(8,128)S(1)} %get-tuple-element.15.own_end, f32[2,8,32,128]{3,2,1,0:T(8,128)S(1)} %collective-permute-done.11.other_end, f32[2,2,8,48,128]{4,3,2,1,0:T(8,128)S(1)} %get-tuple-element.16.starts.rest_6_, ...), custom_call_target="tpu_custom_call" | custom-call | tf_op jit(solution)/shard_map/pallas_call | solution.py:482
  25.4 1.6 %collective-permute-start.14 = (f32[2,4,16,128]{3,2,1,0:T(8,128)S(1)}, f32[2,4,16,128]{3,2,1,0:T(8,128)S(1)}, u32[]{:S(2)}, u32[]{:S(2)}) collective-permute-start(f32[2,4,16,128]{3,2,1,0:T(8,128)S(1)} %get-tuple-element.23), channel_id=1, source_target_pairs={{0,16},{8,24},{16,0},{24,8},{1,18},{9,26},{17,2},{25,10},{2,17},{1... | collective-permute-start | bytes 196616 | tf_op jit(solution)/shard_map/ppermute | solution.py:534
  27.0 2.2 %collective-permute-start.13 = (f32[2,4,16,128]{3,2,1,0:T(8,128)S(1)}, f32[2,4,16,128]{3,2,1,0:T(8,128)S(1)}, u32[]{:S(2)}, u32[]{:S(2)}) collective-permute-start(f32[2,4,16,128]{3,2,1,0:T(8,128)S(1)} %get-tuple-element.23), channel_id=1, source_target_pairs={{0,17},{8,25},{16,1},{24,9},{1,16},{9,24},{17,0},{25,8},{2,19},{10... | collective-permute-start | bytes 196616 | tf_op jit(solution)/shard_map/ppermute | solution.py:533
  29.1 1.5 %collective-permute-start.12 = (f32[2,4,16,128]{3,2,1,0:T(8,128)S(1)}, f32[2,4,16,128]{3,2,1,0:T(8,128)S(1)}, u32[]{:S(2)}, u32[]{:S(2)}) collective-permute-start(f32[2,4,16,128]{3,2,1,0:T(8,128)S(1)} %get-tuple-element.23), channel_id=1, source_target_pairs={{0,16},{8,24},{16,0},{24,8},{1,17},{9,25},{17,1},{25,9},{2,18},{10... | collective-permute-start | bytes 196616 | tf_op jit(solution)/shard_map/ppermute | solution.py:612
  30.7 1.6 %collective-permute-done.13.rest_1_ = f32[2,4,16,128]{3,2,1,0:T(8,128)S(1)} collective-permute-done((f32[2,4,16,128]{3,2,1,0:T(8,128)S(1)}, f32[2,4,16,128]{3,2,1,0:T(8,128)S(1)}, u32[]{:S(2)}, u32[]{:S(2)}) %collective-permute-start.13) | collective-permute-done | bytes 65568 | tf_op jit(solution)/shard_map/ppermute | solution.py:533
  32.2 1.2 %collective-permute-done.12.rest_0_ = f32[2,4,16,128]{3,2,1,0:T(8,128)S(1)} collective-permute-done((f32[2,4,16,128]{3,2,1,0:T(8,128)S(1)}, f32[2,4,16,128]{3,2,1,0:T(8,128)S(1)}, u32[]{:S(2)}, u32[]{:S(2)}) %collective-permute-start.12) | collective-permute-done | bytes 65568 | tf_op jit(solution)/shard_map/ppermute | solution.py:612
  33.4 0.1 collective-permute-done.16.rest_4_
  33.5 1.2 %collective-permute-done.15.rest_3_ = f32[2,4,16,128]{3,2,1,0:T(8,128)S(1)} collective-permute-done((f32[2,4,16,128]{3,2,1,0:T(8,128)S(1)}, f32[2,4,16,128]{3,2,1,0:T(8,128)S(1)}, u32[]{:S(2)}, u32[]{:S(2)}) %collective-permute-start.15) | collective-permute-done | bytes 65568 | tf_op jit(solution)/shard_map/ppermute | solution.py:545
  34.7 3.8 %shard_map.41 = (f32[1,4,16,256]{3,2,1,0:T(8,128)}, f32[2,4,16,128]{3,2,1,0:T(8,128)}) custom-call(f32[2,8,16,128]{3,2,1,0:T(8,128)S(1)} %get-tuple-element.21.first_end, f32[2,8,16,128]{3,2,1,0:T(8,128)S(1)} %get-tuple-element.22.joined, f32[2,4,16,128]{3,2,1,0:T(8,128)S(1)} %collective-permute-done.12.rest_0_, ...), custom_call_target="tpu_custom_call" | custom-call | tf_op jit(solution)/shard_map/pallas_call | solution.py:482
  (15 shorter events, 0.0 us)
Async XLA Ops:
  0.0 0.9 %copy-start = (f32[3,4,16,256]{3,2,1,0:T(8,128)S(1)}, f32[3,4,16,256]{3,2,1,0:T(8,128)}, u32[]{:S(2)}) copy-start(f32[3,4,16,256]{3,2,1,0:T(8,128)} %velocity.1) | copy-start | bytes 589828
  0.9 0.8 %copy-start.1 = (f32[1,4,16,256]{3,2,1,0:T(8,128)S(1)}, f32[1,4,16,256]{3,2,1,0:T(8,128)}, u32[]{:S(2)}) copy-start(f32[1,4,16,256]{3,2,1,0:T(8,128)} %states.1) | copy-start | bytes 196612
  1.8 0.8 %copy-start.2 = (f32[4,16,256]{2,1,0:T(8,128)S(1)}, f32[4,16,256]{2,1,0:T(8,128)}, u32[]{:S(2)}) copy-start(f32[4,16,256]{2,1,0:T(8,128)} %diffusivity.1) | copy-start | bytes 196612
  2.9 7.9 %collective-permute-start.2 = (f32[3,4,16,256]{3,2,1,0:T(8,128)S(1)}, f32[3,4,16,256]{3,2,1,0:T(8,128)S(1)}, u32[]{:S(2)}, u32[]{:S(2)}) collective-permute-start(f32[3,4,16,256]{3,2,1,0:T(8,128)S(1)} %shard_map.37.refs_0_), channel_id=1, source_target_pairs={{0,4},{4,0},{1,5},{5,1},{2,6},{6,2},{3,7},{7,3},{8,12},{12,8},{9,1... | collective-permute-start | bytes 589832 | tf_op jit(solution)/shard_map/ppermute | solution.py:497
  5.9 8.3 %collective-permute-start.5 = (f32[3,4,16,256]{3,2,1,0:T(8,128)S(1)}, f32[3,4,16,256]{3,2,1,0:T(8,128)S(1)}, u32[]{:S(2)}, u32[]{:S(2)}) collective-permute-start(f32[3,4,16,256]{3,2,1,0:T(8,128)S(1)} %shard_map.37.refs_0_), channel_id=1, source_target_pairs={{0,8},{8,0},{16,24},{24,16},{1,9},{9,1},{17,25},{25,17},{2,10},{10... | collective-permute-start | bytes 589832 | tf_op jit(solution)/shard_map/ppermute | solution.py:545
  5.9 8.3 %collective-permute-start.1 = (f32[3,4,16,256]{3,2,1,0:T(8,128)S(1)}, f32[3,4,16,256]{3,2,1,0:T(8,128)S(1)}, u32[]{:S(2)}, u32[]{:S(2)}) collective-permute-start(f32[3,4,16,256]{3,2,1,0:T(8,128)S(1)} %shard_map.37.refs_0_), channel_id=1, source_target_pairs={{0,8},{8,0},{16,24},{24,16},{1,2},{9,10},{17,18},{25,26},{2,1},{10... | collective-permute-start | bytes 589832 | tf_op jit(solution)/shard_map/ppermute | solution.py:534
  6.4 8.4 %collective-permute-start = (f32[3,4,16,256]{3,2,1,0:T(8,128)S(1)}, f32[3,4,16,256]{3,2,1,0:T(8,128)S(1)}, u32[]{:S(2)}, u32[]{:S(2)}) collective-permute-start(f32[3,4,16,256]{3,2,1,0:T(8,128)S(1)} %shard_map.37.refs_0_), channel_id=1, source_target_pairs={{0,1},{8,9},{16,17},{24,25},{1,0},{9,8},{17,16},{25,24},{2,3},{10,... | collective-permute-start | bytes 589832 | tf_op jit(solution)/shard_map/ppermute | solution.py:533
  10.8 4.0 %collective-permute-start.4 = (f32[3,4,16,256]{3,2,1,0:T(8,128)S(1)}, f32[3,4,16,256]{3,2,1,0:T(8,128)S(1)}, u32[]{:S(2)}, u32[]{:S(2)}) collective-permute-start(f32[3,4,16,256]{3,2,1,0:T(8,128)S(1)} %collective-permute-done.2.refs_3_), channel_id=1, source_target_pairs={{0,8},{8,0},{16,24},{24,16},{1,2},{9,10},{17,18},{25,26},{2,1},{10... | collective-permute-start | bytes 589832 | tf_op jit(solution)/shard_map/ppermute | solution.py:534
  10.8 7.8 %collective-permute-start.3 = (f32[3,4,16,256]{3,2,1,0:T(8,128)S(1)}, f32[3,4,16,256]{3,2,1,0:T(8,128)S(1)}, u32[]{:S(2)}, u32[]{:S(2)}) collective-permute-start(f32[3,4,16,256]{3,2,1,0:T(8,128)S(1)} %collective-permute-done.2.refs_3_), channel_id=1, source_target_pairs={{0,1},{8,9},{16,17},{24,25},{1,0},{9,8},{17,16},{25,24},{2,3},{10,... | collective-permute-start | bytes 589832 | tf_op jit(solution)/shard_map/ppermute | solution.py:533
  14.2 4.4 %collective-permute-start.8 = (f32[3,4,16,256]{3,2,1,0:T(8,128)S(1)}, f32[3,4,16,256]{3,2,1,0:T(8,128)S(1)}, u32[]{:S(2)}, u32[]{:S(2)}) collective-permute-start(f32[3,4,16,256]{3,2,1,0:T(8,128)S(1)} %collective-permute-done.2.refs_3_), channel_id=1, source_target_pairs={{0,8},{8,0},{16,24},{24,16},{1,9},{9,1},{17,25},{25,17},{2,10},{10... | collective-permute-start | bytes 589832 | tf_op jit(solution)/shard_map/ppermute | solution.py:545
  14.2 4.4 %collective-permute-start.7 = (f32[3,4,16,256]{3,2,1,0:T(8,128)S(1)}, f32[3,4,16,256]{3,2,1,0:T(8,128)S(1)}, u32[]{:S(2)}, u32[]{:S(2)}) collective-permute-start(f32[3,4,16,256]{3,2,1,0:T(8,128)S(1)} %collective-permute-done.1.refs_2_), channel_id=1, source_target_pairs={{0,8},{8,0},{16,24},{24,16},{1,9},{9,1},{17,25},{25,17},{2,10},{10... | collective-permute-start | bytes 589832 | tf_op jit(solution)/shard_map/ppermute | solution.py:545
  14.8 3.8 %collective-permute-start.6 = (f32[3,4,16,256]{3,2,1,0:T(8,128)S(1)}, f32[3,4,16,256]{3,2,1,0:T(8,128)S(1)}, u32[]{:S(2)}, u32[]{:S(2)}) collective-permute-start(f32[3,4,16,256]{3,2,1,0:T(8,128)S(1)} %collective-permute-done.refs_1_), channel_id=1, source_target_pairs={{0,8},{8,0},{16,24},{24,16},{1,9},{9,1},{17,25},{25,17},{2,10},{10... | collective-permute-start | bytes 589832 | tf_op jit(solution)/shard_map/ppermute | solution.py:545
  14.8 3.8 %collective-permute-start.10 = (f32[3,4,16,256]{3,2,1,0:T(8,128)S(1)}, f32[3,4,16,256]{3,2,1,0:T(8,128)S(1)}, u32[]{:S(2)}, u32[]{:S(2)}) collective-permute-start(f32[3,4,16,256]{3,2,1,0:T(8,128)S(1)} %collective-permute-done.4.refs_5_), channel_id=1, source_target_pairs={{0,8},{8,0},{16,24},{24,16},{1,9},{9,1},{17,25},{25,17},{2,10},{10... | collective-permute-start | bytes 589832 | tf_op jit(solution)/shard_map/ppermute | solution.py:545
  18.6 1.4 %collective-permute-start.9 = (f32[3,4,16,256]{3,2,1,0:T(8,128)S(1)}, f32[3,4,16,256]{3,2,1,0:T(8,128)S(1)}, u32[]{:S(2)}, u32[]{:S(2)}) collective-permute-start(f32[3,4,16,256]{3,2,1,0:T(8,128)S(1)} %collective-permute-done.3.refs_4_), channel_id=1, source_target_pairs={{0,8},{8,0},{16,24},{24,16},{1,9},{9,1},{17,25},{25,17},{2,10},{10... | collective-permute-start | bytes 589832 | tf_op jit(solution)/shard_map/ppermute | solution.py:545
  22.5 1.6 %collective-permute-start.11 = (f32[2,8,32,128]{3,2,1,0:T(8,128)S(1)}, f32[2,8,32,128]{3,2,1,0:T(8,128)S(1)}, u32[]{:S(2)}, u32[]{:S(2)}) collective-permute-start(f32[2,8,32,128]{3,2,1,0:T(8,128)S(1)} %get-tuple-element.15.own_end), channel_id=1, source_target_pairs={{0,8},{8,0},{16,24},{24,16},{1,9},{9,1},{17,25},{25,17},{2,10},{10... | collective-permute-start | bytes 786440 | tf_op jit(solution)/shard_map/ppermute | solution.py:545
  25.4 5.3 %collective-permute-start.14 = (f32[2,4,16,128]{3,2,1,0:T(8,128)S(1)}, f32[2,4,16,128]{3,2,1,0:T(8,128)S(1)}, u32[]{:S(2)}, u32[]{:S(2)}) collective-permute-start(f32[2,4,16,128]{3,2,1,0:T(8,128)S(1)} %get-tuple-element.23), channel_id=1, source_target_pairs={{0,16},{8,24},{16,0},{24,8},{1,18},{9,26},{17,2},{25,10},{2,17},{1... | collective-permute-start | bytes 196616 | tf_op jit(solution)/shard_map/ppermute | solution.py:534
  27.0 5.3 %collective-permute-start.13 = (f32[2,4,16,128]{3,2,1,0:T(8,128)S(1)}, f32[2,4,16,128]{3,2,1,0:T(8,128)S(1)}, u32[]{:S(2)}, u32[]{:S(2)}) collective-permute-start(f32[2,4,16,128]{3,2,1,0:T(8,128)S(1)} %get-tuple-element.23), channel_id=1, source_target_pairs={{0,17},{8,25},{16,1},{24,9},{1,16},{9,24},{17,0},{25,8},{2,19},{10... | collective-permute-start | bytes 196616 | tf_op jit(solution)/shard_map/ppermute | solution.py:533
  29.1 4.3 %collective-permute-start.12 = (f32[2,4,16,128]{3,2,1,0:T(8,128)S(1)}, f32[2,4,16,128]{3,2,1,0:T(8,128)S(1)}, u32[]{:S(2)}, u32[]{:S(2)}) collective-permute-start(f32[2,4,16,128]{3,2,1,0:T(8,128)S(1)} %get-tuple-element.23), channel_id=1, source_target_pairs={{0,16},{8,24},{16,0},{24,8},{1,17},{9,25},{17,1},{25,9},{2,18},{10... | collective-permute-start | bytes 196616 | tf_op jit(solution)/shard_map/ppermute | solution.py:612
  30.7 2.8 %collective-permute-start.17 = (f32[2,4,16,128]{3,2,1,0:T(8,128)S(1)}, f32[2,4,16,128]{3,2,1,0:T(8,128)S(1)}, u32[]{:S(2)}, u32[]{:S(2)}) collective-permute-start(f32[2,4,16,128]{3,2,1,0:T(8,128)S(1)} %collective-permute-done.14.rest_2_), channel_id=1, source_target_pairs={{0,8},{8,0},{16,24},{24,16},{1,9},{9,1},{17,25},{25,17},{2,10},{10... | collective-permute-start | bytes 196616 | tf_op jit(solution)/shard_map/ppermute | solution.py:545
  32.2 1.3 %collective-permute-start.16 = (f32[2,4,16,128]{3,2,1,0:T(8,128)S(1)}, f32[2,4,16,128]{3,2,1,0:T(8,128)S(1)}, u32[]{:S(2)}, u32[]{:S(2)}) collective-permute-start(f32[2,4,16,128]{3,2,1,0:T(8,128)S(1)} %collective-permute-done.13.rest_1_), channel_id=1, source_target_pairs={{0,8},{8,0},{16,24},{24,16},{1,9},{9,1},{17,25},{25,17},{2,10},{10... | collective-permute-start | bytes 196616 | tf_op jit(solution)/shard_map/ppermute | solution.py:545
  33.4 1.3 %collective-permute-start.15 = (f32[2,4,16,128]{3,2,1,0:T(8,128)S(1)}, f32[2,4,16,128]{3,2,1,0:T(8,128)S(1)}, u32[]{:S(2)}, u32[]{:S(2)}) collective-permute-start(f32[2,4,16,128]{3,2,1,0:T(8,128)S(1)} %collective-permute-done.12.rest_0_), channel_id=1, source_target_pairs={{0,8},{8,0},{16,24},{24,16},{1,9},{9,1},{17,25},{25,17},{2,10},{10... | collective-permute-start | bytes 196616 | tf_op jit(solution)/shard_map/ppermute | solution.py:545

commit v4 on v3

--- a/solution.py
+++ b/solution.py
@@ -135,31 +135,6 @@
     field[...] = jnp.zeros_like(field)
 
 
-def gather_body(states, diffusivity, velocity, parcel, sem):
-    core = lax.axis_index("tm") % 2
-    start = pltpu.make_async_copy(states, parcel.at[pl.ds(0, 1)], sem.at[0])
-    start.start()
-
-    @pl.when(core == 0)
-    def _():
-        one = pltpu.make_async_copy(diffusivity, parcel.at[1], sem.at[1])
-        two = pltpu.make_async_copy(velocity.at[0], parcel.at[2], sem.at[2])
-        one.start()
-        two.start()
-        one.wait()
-        two.wait()
-
-    @pl.when(core == 1)
-    def _():
-        both = pltpu.make_async_copy(
-            velocity.at[pl.ds(1, 2)], parcel.at[pl.ds(1, 2)], sem.at[1]
-        )
-        both.start()
-        both.wait()
-
-    start.wait()
-
-
 def row_places(box, sizes):
     place, count = lax.axis_index("coarse"), lax.axis_size("coarse")
     odd = place % 2
@@ -188,6 +163,7 @@
     clear(one)
     clear(two)
     for side, rank in ((0, core), (1, 1 - core)):
+        slots = ((2 - 2 * rank, None), (rank, 1 + rank), (1 + rank, 3 * rank))
         for block in range(blocks):
             pieces = refs[side * half + block * each : side * half + (block + 1) * each]
             base = (block + shift) % blocks * own_depth
@@ -200,8 +176,8 @@
                 for plane in range(own_depth):
                     for i in range(box.tiles):
                         cols = slice(i * LANES, (i + 1) * LANES)
-                        for array in range(3):
-                            value = ref[array, plane, :, cols]
+                        for array, (slot, kind) in enumerate(slots):
+                            value = ref[slot, plane, :, cols]
                             if valid is not None:
                                 value = jnp.where(valid, value, 0.0)
                             if array == 0:
@@ -209,9 +185,7 @@
                                 if side == 0:
                                     one[i, base + plane + 2, pl.ds(PAD + at, size), :] = value
                             else:
-                                coeff[
-                                    2 * rank + array - 1, i, base + plane, pl.ds(at, size), :
-                                ] = value
+                                coeff[kind, i, base + plane, pl.ds(at, size), :] = value
     scales, carries, tildes = chebyshev_coefficients(SECTIONS)
     stage = 0
     current, other = one, two
@@ -478,11 +452,11 @@
     leaving[...] = total[:, pl.ds(core * half, half)]
 
 
-def run(body, outs, scratch, *args, space=pltpu.VMEM):
+def run(body, outs, scratch, *args):
     return pl.pallas_call(
         body,
         out_shape=[jax.ShapeDtypeStruct(shape, jnp.float32) for shape in outs],
-        in_specs=[pl.BlockSpec(memory_space=space)] * len(args),
+        in_specs=[pl.BlockSpec(memory_space=pltpu.VMEM)] * len(args),
         out_specs=[pl.BlockSpec(memory_space=pltpu.VMEM)] * len(outs),
         scratch_shapes=scratch,
         compiler_params=pltpu.CompilerParams(vmem_limit_bytes=20 * 1024 * 1024),
@@ -554,14 +528,10 @@
     box = Box(depth, rows, side, columns)
     tiles, height, half = box.tiles, box.height, depth // 2
 
-    (parcel,) = run(
-        gather_body,
-        [(3, own_depth, rows, columns)],
-        [pltpu.SemaphoreType.DMA((3,))],
-        states,
-        diffusivity,
-        velocity,
-        space=pl.ANY,
+    second = place % 2 == 1
+    slot = lax.broadcasted_iota(jnp.int32, (3, 1, 1, 1), 0)
+    parcel = jnp.where(
+        (slot == 0) != second, velocity, jnp.where(slot == 1, diffusivity[None], states)
     )
     rounds = row_swaps(lambda t: t, lambda t: t ^ 1)
     blocks = slab_blocks(parcel)

time: 38.7 us -> 36.8 us (0.951)
  local copies, waits for them, and re-layouts: 2.6 us -> 0 us
  other arithmetic: 0 us -> 1.06 us
    unnamed x6 -> x0, local copies, waits for them, and re-layouts: 2.6 us -> none
    select_n x0 -> x1, other arithmetic: none -> 1.06 us  [per_device(): jnp.where((slot == 0) != second, velocity, jnp.where(slot == 1, diffusivi...]
    pallas_call x5 -> x4, Pallas kernels: 8.41 us -> 8.17 us  [run(): pl.pallas_call(body, out_shape=[jax.ShapeDtypeStruct(shape, jnp.float32)...]
where the time goes in v4:
time: 36.8 us; the launch traced here: 36.7 us
  starting transfers between devices  16.1 us (44%)
  waiting for transfers between devices  11.3 us (31%)
  Pallas kernels  8.17 us (22%)
  other arithmetic  1.06 us (3%)
    ppermute x3, starting transfers between devices, row_pieces(): got_one = lax.ppermute(send_one, both, rounds[0])  8.22 us
    pallas_call x4, Pallas kernels, run(): pl.pallas_call(body, out_shape=[jax.ShapeDtypeStruct(shape, jnp.float32)...  8.17 us
    ppermute x3, waiting for transfers between devices, row_pieces(): got_one = lax.ppermute(send_one, both, rounds[0])  4.89 us
    ppermute x10, waiting for transfers between devices, core_swapped(): return lax.ppermute(block, 'tm', [(i, i ^ 1) for i in range(count)])  3.43 us
    ppermute x1, starting transfers between devices, slab_blocks(): return [block, lax.ppermute(block, 'slab', [(0, 1), (1, 0)])]  3.04 us
    ppermute x3, starting transfers between devices, row_pieces(): got_two = lax.ppermute(send_two, both, rounds[1])  2.09 us
    ppermute x1, waiting for transfers between devices, slab_blocks(): return [block, lax.ppermute(block, 'slab', [(0, 1), (1, 0)])]  1.74 us
    ppermute x1, starting transfers between devices, per_device(): centre = lax.ppermute(leaving, 'tm', [(t, hop(t)) for t in range(windows)])  1.52 us
  transfers between devices with their start and end apart: 18, of which 9 were waited for; matrix products, arithmetic and copies ran while one was open for 0% of the time, Pallas kernels for 2%

profile of v4, /device:TPU:0, one launch (start us, length us, event | category | flops | bytes accessed | tf_op | source)
XLA Modules:
  0.0 36.7 jit_solution(17641281038454457644)
XLA Ops:
  0.0 1.1 %select_select_fusion.refs_0_ = f32[3,4,16,256]{3,2,1,0:T(8,128)S(1)} fusion(f32[3,4,16,256]{3,2,1,0:T(8,128)} %param.5, f32[4,16,256]{2,1,0:T(8,128)} %bitcast.1, f32[4,16,256]{2,1,0:T(8,128)} %param.4, pred[3]{0:T(512)(128)(4,1)S(1)} %get-tuple-element.26, pred[3]{0:T(512)(128)(4,1)S(1)} %get-tuple-element.25), kind=kLoop, calls=%fused_computation | loop fusion | flops 98304 | bytes 524294 | tf_op jit(solution)/shard_map/jit(_where)/select_n | solution.py:533
  1.1 3.0 %collective-permute-start.2 = (f32[3,4,16,256]{3,2,1,0:T(8,128)S(1)}, f32[3,4,16,256]{3,2,1,0:T(8,128)S(1)}, u32[]{:S(2)}, u32[]{:S(2)}) collective-permute-start(f32[3,4,16,256]{3,2,1,0:T(8,128)S(1)} %select_select_fusion.refs_0_), channel_id=1, source_target_pairs={{0,4},{4,0},{1,5},{5,1},{2,6},{6,2},{3,7},{7,3},{8,12},{12,8},{9,1... | collective-permute-start | bytes 589832 | tf_op jit(solution)/shard_map/ppermute | solution.py:471
  4.1 0.5 %collective-permute-start.1 = (f32[3,4,16,256]{3,2,1,0:T(8,128)S(1)}, f32[3,4,16,256]{3,2,1,0:T(8,128)S(1)}, u32[]{:S(2)}, u32[]{:S(2)}) collective-permute-start(f32[3,4,16,256]{3,2,1,0:T(8,128)S(1)} %select_select_fusion.refs_0_), channel_id=1, source_target_pairs={{0,8},{8,0},{16,24},{24,16},{1,2},{9,10},{17,18},{25,26},{2,1},{10... | collective-permute-start | bytes 589832 | tf_op jit(solution)/shard_map/ppermute | solution.py:508
  4.6 2.6 %collective-permute-start = (f32[3,4,16,256]{3,2,1,0:T(8,128)S(1)}, f32[3,4,16,256]{3,2,1,0:T(8,128)S(1)}, u32[]{:S(2)}, u32[]{:S(2)}) collective-permute-start(f32[3,4,16,256]{3,2,1,0:T(8,128)S(1)} %select_select_fusion.refs_0_), channel_id=1, source_target_pairs={{0,1},{8,9},{16,17},{24,25},{1,0},{9,8},{17,16},{25,24},{2,3},{10,... | collective-permute-start | bytes 589832 | tf_op jit(solution)/shard_map/ppermute | solution.py:507
  7.3 1.7 %collective-permute-done.2.refs_3_ = f32[3,4,16,256]{3,2,1,0:T(8,128)S(1)} collective-permute-done((f32[3,4,16,256]{3,2,1,0:T(8,128)S(1)}, f32[3,4,16,256]{3,2,1,0:T(8,128)S(1)}, u32[]{:S(2)}, u32[]{:S(2)}) %collective-permute-start.2) | collective-permute-done | bytes 196640 | tf_op jit(solution)/shard_map/ppermute | solution.py:471
  9.0 3.4 %collective-permute-start.3 = (f32[3,4,16,256]{3,2,1,0:T(8,128)S(1)}, f32[3,4,16,256]{3,2,1,0:T(8,128)S(1)}, u32[]{:S(2)}, u32[]{:S(2)}) collective-permute-start(f32[3,4,16,256]{3,2,1,0:T(8,128)S(1)} %collective-permute-done.2.refs_3_), channel_id=1, source_target_pairs={{0,1},{8,9},{16,17},{24,25},{1,0},{9,8},{17,16},{25,24},{2,3},{10,... | collective-permute-start | bytes 589832 | tf_op jit(solution)/shard_map/ppermute | solution.py:507
  12.4 0.0 collective-permute-done.5.refs_6_
  12.4 0.0 collective-permute-start.8
  12.4 0.5 %collective-permute-start.7 = (f32[3,4,16,256]{3,2,1,0:T(8,128)S(1)}, f32[3,4,16,256]{3,2,1,0:T(8,128)S(1)}, u32[]{:S(2)}, u32[]{:S(2)}) collective-permute-start(f32[3,4,16,256]{3,2,1,0:T(8,128)S(1)} %collective-permute-done.1.refs_2_), channel_id=1, source_target_pairs={{0,8},{8,0},{16,24},{24,16},{1,9},{9,1},{17,25},{25,17},{2,10},{10... | collective-permute-start | bytes 589832 | tf_op jit(solution)/shard_map/ppermute | solution.py:519
  12.9 0.1 collective-permute-done.refs_1_
  13.0 0.0 collective-permute-start.6
  13.0 0.0 collective-permute-done.4.refs_5_
  13.0 0.5 %collective-permute-start.10 = (f32[3,4,16,256]{3,2,1,0:T(8,128)S(1)}, f32[3,4,16,256]{3,2,1,0:T(8,128)S(1)}, u32[]{:S(2)}, u32[]{:S(2)}) collective-permute-start(f32[3,4,16,256]{3,2,1,0:T(8,128)S(1)} %collective-permute-done.4.refs_5_), channel_id=1, source_target_pairs={{0,8},{8,0},{16,24},{24,16},{1,9},{9,1},{17,25},{25,17},{2,10},{10... | collective-permute-start | bytes 589832 | tf_op jit(solution)/shard_map/ppermute | solution.py:519
  13.5 3.3 %collective-permute-done.3.refs_4_ = f32[3,4,16,256]{3,2,1,0:T(8,128)S(1)} collective-permute-done((f32[3,4,16,256]{3,2,1,0:T(8,128)S(1)}, f32[3,4,16,256]{3,2,1,0:T(8,128)S(1)}, u32[]{:S(2)}, u32[]{:S(2)}) %collective-permute-start.3) | collective-permute-done | bytes 196640 | tf_op jit(solution)/shard_map/ppermute | solution.py:507
  16.8 0.0 collective-permute-start.9
  16.8 0.0 collective-permute-done.8.refs_9_
  16.8 0.0 collective-permute-done.7.refs_8_
  16.8 0.0 collective-permute-done.10.refs_11_
  16.8 1.4 %collective-permute-done.9.refs_10_ = f32[3,4,16,256]{3,2,1,0:T(8,128)S(1)} collective-permute-done((f32[3,4,16,256]{3,2,1,0:T(8,128)S(1)}, f32[3,4,16,256]{3,2,1,0:T(8,128)S(1)}, u32[]{:S(2)}, u32[]{:S(2)}) %collective-permute-start.9) | collective-permute-done | bytes 196640 | tf_op jit(solution)/shard_map/ppermute | solution.py:519
  18.2 2.5 %shard_map.37 = (f32[2,8,32,128]{3,2,1,0:T(8,128)S(1)}, f32[2,2,8,48,128]{4,3,2,1,0:T(8,128)S(1)}, f32[4,2,8,48,128]{4,3,2,1,0:T(8,128)S(1)}) custom-call(f32[3,4,16,256]{3,2,1,0:T(8,128)S(1)} %select_select_fusion.refs_0_, f32[3,4,16,256]{3,2,1,0:T(8,128)S(1)} %collective-permute-done.refs_1_, f32[3,4,16,256]{3,2,1,0:T(8,128)S(1)} %collective-permute-done.1.refs_2_, ...), custom_call_target="tpu_custom_call" | custom-call | tf_op jit(solution)/shard_map/pallas_call | solution.py:456
  20.7 0.2 collective-permute-start.11
  20.9 0.6 %shard_map.38 = (f32[4,2,4,48,128]{4,3,2,1,0:T(8,128)S(1)}, f32[2,8,48,128]{3,2,1,0:T(8,128)S(1)}, f32[2,4,48,128]{3,2,1,0:T(8,128)S(1)}) custom-call(f32[4,2,8,48,128]{4,3,2,1,0:T(8,128)S(1)} %get-tuple-element.17.coeff.rest_0_.rest_7_), custom_call_target="tpu_custom_call" | custom-call | tf_op jit(solution)/shard_map/pallas_call | solution.py:456
  21.6 0.8 %collective-permute-done.11.other_end = f32[2,8,32,128]{3,2,1,0:T(8,128)S(1)} collective-permute-done((f32[2,8,32,128]{3,2,1,0:T(8,128)S(1)}, f32[2,8,32,128]{3,2,1,0:T(8,128)S(1)}, u32[]{:S(2)}, u32[]{:S(2)}) %collective-permute-start.11) | collective-permute-done | bytes 262176 | tf_op jit(solution)/shard_map/ppermute | solution.py:519
  22.3 1.3 %shard_map.39 = (f32[2,8,16,128]{3,2,1,0:T(8,128)S(1)}, f32[2,8,16,128]{3,2,1,0:T(8,128)S(1)}, f32[2,4,16,128]{3,2,1,0:T(8,128)S(1)}) custom-call(f32[2,8,32,128]{3,2,1,0:T(8,128)S(1)} %get-tuple-element.15.own_end, f32[2,8,32,128]{3,2,1,0:T(8,128)S(1)} %collective-permute-done.11.other_end, f32[2,2,8,48,128]{4,3,2,1,0:T(8,128)S(1)} %get-tuple-element.16.starts.rest_6_, ...), custom_call_target="tpu_custom_call" | custom-call | tf_op jit(solution)/shard_map/pallas_call | solution.py:456
  23.6 1.6 %collective-permute-start.14 = (f32[2,4,16,128]{3,2,1,0:T(8,128)S(1)}, f32[2,4,16,128]{3,2,1,0:T(8,128)S(1)}, u32[]{:S(2)}, u32[]{:S(2)}) collective-permute-start(f32[2,4,16,128]{3,2,1,0:T(8,128)S(1)} %get-tuple-element.23), channel_id=1, source_target_pairs={{0,16},{8,24},{16,0},{24,8},{1,18},{9,26},{17,2},{25,10},{2,17},{1... | collective-permute-start | bytes 196616 | tf_op jit(solution)/shard_map/ppermute | solution.py:508
  25.2 2.2 %collective-permute-start.13 = (f32[2,4,16,128]{3,2,1,0:T(8,128)S(1)}, f32[2,4,16,128]{3,2,1,0:T(8,128)S(1)}, u32[]{:S(2)}, u32[]{:S(2)}) collective-permute-start(f32[2,4,16,128]{3,2,1,0:T(8,128)S(1)} %get-tuple-element.23), channel_id=1, source_target_pairs={{0,17},{8,25},{16,1},{24,9},{1,16},{9,24},{17,0},{25,8},{2,19},{10... | collective-permute-start | bytes 196616 | tf_op jit(solution)/shard_map/ppermute | solution.py:507
  27.4 1.5 %collective-permute-start.12 = (f32[2,4,16,128]{3,2,1,0:T(8,128)S(1)}, f32[2,4,16,128]{3,2,1,0:T(8,128)S(1)}, u32[]{:S(2)}, u32[]{:S(2)}) collective-permute-start(f32[2,4,16,128]{3,2,1,0:T(8,128)S(1)} %get-tuple-element.23), channel_id=1, source_target_pairs={{0,16},{8,24},{16,0},{24,8},{1,17},{9,25},{17,1},{25,9},{2,18},{10... | collective-permute-start | bytes 196616 | tf_op jit(solution)/shard_map/ppermute | solution.py:582
  28.9 1.6 %collective-permute-done.13.rest_1_ = f32[2,4,16,128]{3,2,1,0:T(8,128)S(1)} collective-permute-done((f32[2,4,16,128]{3,2,1,0:T(8,128)S(1)}, f32[2,4,16,128]{3,2,1,0:T(8,128)S(1)}, u32[]{:S(2)}, u32[]{:S(2)}) %collective-permute-start.13) | collective-permute-done | bytes 65568 | tf_op jit(solution)/shard_map/ppermute | solution.py:507
  30.5 1.2 %collective-permute-done.12.rest_0_ = f32[2,4,16,128]{3,2,1,0:T(8,128)S(1)} collective-permute-done((f32[2,4,16,128]{3,2,1,0:T(8,128)S(1)}, f32[2,4,16,128]{3,2,1,0:T(8,128)S(1)}, u32[]{:S(2)}, u32[]{:S(2)}) %collective-permute-start.12) | collective-permute-done | bytes 65568 | tf_op jit(solution)/shard_map/ppermute | solution.py:582
  31.7 0.1 collective-permute-done.16.rest_4_
  31.7 1.2 %collective-permute-done.15.rest_3_ = f32[2,4,16,128]{3,2,1,0:T(8,128)S(1)} collective-permute-done((f32[2,4,16,128]{3,2,1,0:T(8,128)S(1)}, f32[2,4,16,128]{3,2,1,0:T(8,128)S(1)}, u32[]{:S(2)}, u32[]{:S(2)}) %collective-permute-start.15) | collective-permute-done | bytes 65568 | tf_op jit(solution)/shard_map/ppermute | solution.py:519
  32.9 3.8 %shard_map.40 = (f32[1,4,16,256]{3,2,1,0:T(8,128)}, f32[2,4,16,128]{3,2,1,0:T(8,128)}) custom-call(f32[2,8,16,128]{3,2,1,0:T(8,128)S(1)} %get-tuple-element.21.first_end, f32[2,8,16,128]{3,2,1,0:T(8,128)S(1)} %get-tuple-element.22.joined, f32[2,4,16,128]{3,2,1,0:T(8,128)S(1)} %collective-permute-done.12.rest_0_, ...), custom_call_target="tpu_custom_call" | custom-call | tf_op jit(solution)/shard_map/pallas_call | solution.py:456
  (10 shorter events, 0.0 us)
Async XLA Ops:
  1.1 7.9 %collective-permute-start.2 = (f32[3,4,16,256]{3,2,1,0:T(8,128)S(1)}, f32[3,4,16,256]{3,2,1,0:T(8,128)S(1)}, u32[]{:S(2)}, u32[]{:S(2)}) collective-permute-start(f32[3,4,16,256]{3,2,1,0:T(8,128)S(1)} %select_select_fusion.refs_0_), channel_id=1, source_target_pairs={{0,4},{4,0},{1,5},{5,1},{2,6},{6,2},{3,7},{7,3},{8,12},{12,8},{9,1... | collective-permute-start | bytes 589832 | tf_op jit(solution)/shard_map/ppermute | solution.py:471
  4.1 8.3 %collective-permute-start.5 = (f32[3,4,16,256]{3,2,1,0:T(8,128)S(1)}, f32[3,4,16,256]{3,2,1,0:T(8,128)S(1)}, u32[]{:S(2)}, u32[]{:S(2)}) collective-permute-start(f32[3,4,16,256]{3,2,1,0:T(8,128)S(1)} %select_select_fusion.refs_0_), channel_id=1, source_target_pairs={{0,8},{8,0},{16,24},{24,16},{1,9},{9,1},{17,25},{25,17},{2,10},{10... | collective-permute-start | bytes 589832 | tf_op jit(solution)/shard_map/ppermute | solution.py:519
  4.1 8.3 %collective-permute-start.1 = (f32[3,4,16,256]{3,2,1,0:T(8,128)S(1)}, f32[3,4,16,256]{3,2,1,0:T(8,128)S(1)}, u32[]{:S(2)}, u32[]{:S(2)}) collective-permute-start(f32[3,4,16,256]{3,2,1,0:T(8,128)S(1)} %select_select_fusion.refs_0_), channel_id=1, source_target_pairs={{0,8},{8,0},{16,24},{24,16},{1,2},{9,10},{17,18},{25,26},{2,1},{10... | collective-permute-start | bytes 589832 | tf_op jit(solution)/shard_map/ppermute | solution.py:508
  4.6 8.4 %collective-permute-start = (f32[3,4,16,256]{3,2,1,0:T(8,128)S(1)}, f32[3,4,16,256]{3,2,1,0:T(8,128)S(1)}, u32[]{:S(2)}, u32[]{:S(2)}) collective-permute-start(f32[3,4,16,256]{3,2,1,0:T(8,128)S(1)} %select_select_fusion.refs_0_), channel_id=1, source_target_pairs={{0,1},{8,9},{16,17},{24,25},{1,0},{9,8},{17,16},{25,24},{2,3},{10,... | collective-permute-start | bytes 589832 | tf_op jit(solution)/shard_map/ppermute | solution.py:507
  9.0 4.0 %collective-permute-start.4 = (f32[3,4,16,256]{3,2,1,0:T(8,128)S(1)}, f32[3,4,16,256]{3,2,1,0:T(8,128)S(1)}, u32[]{:S(2)}, u32[]{:S(2)}) collective-permute-start(f32[3,4,16,256]{3,2,1,0:T(8,128)S(1)} %collective-permute-done.2.refs_3_), channel_id=1, source_target_pairs={{0,8},{8,0},{16,24},{24,16},{1,2},{9,10},{17,18},{25,26},{2,1},{10... | collective-permute-start | bytes 589832 | tf_op jit(solution)/shard_map/ppermute | solution.py:508
  9.0 7.8 %collective-permute-start.3 = (f32[3,4,16,256]{3,2,1,0:T(8,128)S(1)}, f32[3,4,16,256]{3,2,1,0:T(8,128)S(1)}, u32[]{:S(2)}, u32[]{:S(2)}) collective-permute-start(f32[3,4,16,256]{3,2,1,0:T(8,128)S(1)} %collective-permute-done.2.refs_3_), channel_id=1, source_target_pairs={{0,1},{8,9},{16,17},{24,25},{1,0},{9,8},{17,16},{25,24},{2,3},{10,... | collective-permute-start | bytes 589832 | tf_op jit(solution)/shard_map/ppermute | solution.py:507
  12.4 4.4 %collective-permute-start.8 = (f32[3,4,16,256]{3,2,1,0:T(8,128)S(1)}, f32[3,4,16,256]{3,2,1,0:T(8,128)S(1)}, u32[]{:S(2)}, u32[]{:S(2)}) collective-permute-start(f32[3,4,16,256]{3,2,1,0:T(8,128)S(1)} %collective-permute-done.2.refs_3_), channel_id=1, source_target_pairs={{0,8},{8,0},{16,24},{24,16},{1,9},{9,1},{17,25},{25,17},{2,10},{10... | collective-permute-start | bytes 589832 | tf_op jit(solution)/shard_map/ppermute | solution.py:519
  12.4 4.4 %collective-permute-start.7 = (f32[3,4,16,256]{3,2,1,0:T(8,128)S(1)}, f32[3,4,16,256]{3,2,1,0:T(8,128)S(1)}, u32[]{:S(2)}, u32[]{:S(2)}) collective-permute-start(f32[3,4,16,256]{3,2,1,0:T(8,128)S(1)} %collective-permute-done.1.refs_2_), channel_id=1, source_target_pairs={{0,8},{8,0},{16,24},{24,16},{1,9},{9,1},{17,25},{25,17},{2,10},{10... | collective-permute-start | bytes 589832 | tf_op jit(solution)/shard_map/ppermute | solution.py:519
  13.0 3.8 %collective-permute-start.6 = (f32[3,4,16,256]{3,2,1,0:T(8,128)S(1)}, f32[3,4,16,256]{3,2,1,0:T(8,128)S(1)}, u32[]{:S(2)}, u32[]{:S(2)}) collective-permute-start(f32[3,4,16,256]{3,2,1,0:T(8,128)S(1)} %collective-permute-done.refs_1_), channel_id=1, source_target_pairs={{0,8},{8,0},{16,24},{24,16},{1,9},{9,1},{17,25},{25,17},{2,10},{10... | collective-permute-start | bytes 589832 | tf_op jit(solution)/shard_map/ppermute | solution.py:519
  13.0 3.8 %collective-permute-start.10 = (f32[3,4,16,256]{3,2,1,0:T(8,128)S(1)}, f32[3,4,16,256]{3,2,1,0:T(8,128)S(1)}, u32[]{:S(2)}, u32[]{:S(2)}) collective-permute-start(f32[3,4,16,256]{3,2,1,0:T(8,128)S(1)} %collective-permute-done.4.refs_5_), channel_id=1, source_target_pairs={{0,8},{8,0},{16,24},{24,16},{1,9},{9,1},{17,25},{25,17},{2,10},{10... | collective-permute-start | bytes 589832 | tf_op jit(solution)/shard_map/ppermute | solution.py:519
  16.8 1.4 %collective-permute-start.9 = (f32[3,4,16,256]{3,2,1,0:T(8,128)S(1)}, f32[3,4,16,256]{3,2,1,0:T(8,128)S(1)}, u32[]{:S(2)}, u32[]{:S(2)}) collective-permute-start(f32[3,4,16,256]{3,2,1,0:T(8,128)S(1)} %collective-permute-done.3.refs_4_), channel_id=1, source_target_pairs={{0,8},{8,0},{16,24},{24,16},{1,9},{9,1},{17,25},{25,17},{2,10},{10... | collective-permute-start | bytes 589832 | tf_op jit(solution)/shard_map/ppermute | solution.py:519
  20.7 1.6 %collective-permute-start.11 = (f32[2,8,32,128]{3,2,1,0:T(8,128)S(1)}, f32[2,8,32,128]{3,2,1,0:T(8,128)S(1)}, u32[]{:S(2)}, u32[]{:S(2)}) collective-permute-start(f32[2,8,32,128]{3,2,1,0:T(8,128)S(1)} %get-tuple-element.15.own_end), channel_id=1, source_target_pairs={{0,8},{8,0},{16,24},{24,16},{1,9},{9,1},{17,25},{25,17},{2,10},{10... | collective-permute-start | bytes 786440 | tf_op jit(solution)/shard_map/ppermute | solution.py:519
  23.6 5.3 %collective-permute-start.14 = (f32[2,4,16,128]{3,2,1,0:T(8,128)S(1)}, f32[2,4,16,128]{3,2,1,0:T(8,128)S(1)}, u32[]{:S(2)}, u32[]{:S(2)}) collective-permute-start(f32[2,4,16,128]{3,2,1,0:T(8,128)S(1)} %get-tuple-element.23), channel_id=1, source_target_pairs={{0,16},{8,24},{16,0},{24,8},{1,18},{9,26},{17,2},{25,10},{2,17},{1... | collective-permute-start | bytes 196616 | tf_op jit(solution)/shard_map/ppermute | solution.py:508
  25.2 5.3 %collective-permute-start.13 = (f32[2,4,16,128]{3,2,1,0:T(8,128)S(1)}, f32[2,4,16,128]{3,2,1,0:T(8,128)S(1)}, u32[]{:S(2)}, u32[]{:S(2)}) collective-permute-start(f32[2,4,16,128]{3,2,1,0:T(8,128)S(1)} %get-tuple-element.23), channel_id=1, source_target_pairs={{0,17},{8,25},{16,1},{24,9},{1,16},{9,24},{17,0},{25,8},{2,19},{10... | collective-permute-start | bytes 196616 | tf_op jit(solution)/shard_map/ppermute | solution.py:507
  27.4 4.3 %collective-permute-start.12 = (f32[2,4,16,128]{3,2,1,0:T(8,128)S(1)}, f32[2,4,16,128]{3,2,1,0:T(8,128)S(1)}, u32[]{:S(2)}, u32[]{:S(2)}) collective-permute-start(f32[2,4,16,128]{3,2,1,0:T(8,128)S(1)} %get-tuple-element.23), channel_id=1, source_target_pairs={{0,16},{8,24},{16,0},{24,8},{1,17},{9,25},{17,1},{25,9},{2,18},{10... | collective-permute-start | bytes 196616 | tf_op jit(solution)/shard_map/ppermute | solution.py:582
  28.9 2.8 %collective-permute-start.17 = (f32[2,4,16,128]{3,2,1,0:T(8,128)S(1)}, f32[2,4,16,128]{3,2,1,0:T(8,128)S(1)}, u32[]{:S(2)}, u32[]{:S(2)}) collective-permute-start(f32[2,4,16,128]{3,2,1,0:T(8,128)S(1)} %collective-permute-done.14.rest_2_), channel_id=1, source_target_pairs={{0,8},{8,0},{16,24},{24,16},{1,9},{9,1},{17,25},{25,17},{2,10},{10... | collective-permute-start | bytes 196616 | tf_op jit(solution)/shard_map/ppermute | solution.py:519
  30.4 1.3 %collective-permute-start.16 = (f32[2,4,16,128]{3,2,1,0:T(8,128)S(1)}, f32[2,4,16,128]{3,2,1,0:T(8,128)S(1)}, u32[]{:S(2)}, u32[]{:S(2)}) collective-permute-start(f32[2,4,16,128]{3,2,1,0:T(8,128)S(1)} %collective-permute-done.13.rest_1_), channel_id=1, source_target_pairs={{0,8},{8,0},{16,24},{24,16},{1,9},{9,1},{17,25},{25,17},{2,10},{10... | collective-permute-start | bytes 196616 | tf_op jit(solution)/shard_map/ppermute | solution.py:519
  31.6 1.3 %collective-permute-start.15 = (f32[2,4,16,128]{3,2,1,0:T(8,128)S(1)}, f32[2,4,16,128]{3,2,1,0:T(8,128)S(1)}, u32[]{:S(2)}, u32[]{:S(2)}) collective-permute-start(f32[2,4,16,128]{3,2,1,0:T(8,128)S(1)} %collective-permute-done.12.rest_0_), channel_id=1, source_target_pairs={{0,8},{8,0},{16,24},{24,16},{1,9},{9,1},{17,25},{25,17},{2,10},{10... | collective-permute-start | bytes 196616 | tf_op jit(solution)/shard_map/ppermute | solution.py:519

commit v5 on v4

v5 whole, which is shorter than its diff:
```python
import functools

import jax
import jax.numpy as jnp
from jax import lax
from jax.experimental import pallas as pl
from jax.experimental.pallas import tpu as pltpu
from jax.sharding import PartitionSpec as P

SECTIONS = 4
FINE_STEPS = 2
FINE_STEP = 1.0
RELAX = 0.8
INTERVAL = FINE_STEPS * FINE_STEP
LANES = 128
PAD = 8
COARSE_REACH = 6
FINE_REACH = SECTIONS * FINE_STEPS


def chebyshev_coefficients(sections):
    damping = 0.05
    centre_point = 1.0 + damping / (sections * sections)
    chebyshev = [1.0, centre_point]
    slopes = [0.0, 1.0]
    for degree in range(2, sections + 1):
        chebyshev.append(2.0 * centre_point * chebyshev[degree - 1] - chebyshev[degree - 2])
        slopes.append(
            2.0 * chebyshev[degree - 1]
            + 2.0 * centre_point * slopes[degree - 1]
            - slopes[degree - 2]
        )
    slope_ratio = chebyshev[sections] / slopes[sections]
    weights = [1.0 / entry for entry in chebyshev]
    scales = [0.0, 0.0]
    carries = [0.0, 0.0]
    tildes = [0.0, slope_ratio / centre_point]
    for degree in range(2, sections + 1):
        scales.append(2.0 * weights[degree] * centre_point / weights[degree - 1])
        carries.append(-weights[degree] / weights[degree - 2])
        tildes.append(2.0 * weights[degree] * slope_ratio / weights[degree - 1])
    return (scales, carries, tildes)


def round_up(value, unit):
    return -(-value // unit) * unit


class Box:
    def __init__(self, depth, rows, side, columns):
        self.depth, self.rows, self.side, self.columns = depth, rows, side, columns
        self.height = rows + 2 * side
        self.tiles = columns // LANES

    def scratch(self, depth=None):
        depth = self.depth if depth is None else depth
        return pltpu.VMEM(
            (self.tiles, depth + 4, self.height + 2 * PAD, LANES), jnp.float32
        )

    def span(self, margin):
        first = (self.side - margin) // 8 * 8
        last = round_up(self.side + self.rows + margin, 8)
        assert first >= 0 and last <= self.height
        return first, last


CHUNK = 16
AFTER_DEPTH, BEFORE_DEPTH, AFTER_ROW, BEFORE_ROW, AFTER_COLUMN, BEFORE_COLUMN, CENTRE = range(7)


def chunks(first, last):
    at = first
    while at < last:
        size = min(CHUNK, last - at)
        yield at, size
        at += size


def sweep(count, first, last, body):
    if count <= 8:
        for at, size in chunks(first, last):
            cache = {}
            for plane in range(count):
                body(plane, at, size, cache)
    else:

        def step(plane, carry):
            for at, size in chunks(first, last):
                body(plane, at, size, None)
            return carry

        lax.fori_loop(0, count, step, 0)


def lane_index(size):
    return lax.broadcasted_iota(jnp.int32, (size, LANES), 1)


def row_index(size):
    return lax.broadcasted_iota(jnp.int32, (size, LANES), 0)


def sideways(values, step):
    lane = lane_index(values[0].shape[0])
    back = [pltpu.roll(entry, LANES - step, 1) for entry in values]
    forth = [pltpu.roll(entry, step, 1) for entry in values]
    count = len(values)
    after = [
        jnp.where(lane >= LANES - step, back[i + 1], back[i]) if i + 1 < count else back[i]
        for i in range(count)
    ]
    before = [jnp.where(lane < step, forth[i - 1], forth[i]) if i else forth[i] for i in range(count)]
    return after, before


def neighbours(field, weights, plane, at, size, step, cache):
    tiles = field.shape[0]

    def level(i, index):
        if cache is None:
            return field[i, index, pl.ds(PAD + at, size), :]
        if (i, index) not in cache:
            cache[i, index] = field[i, index, pl.ds(PAD + at, size), :]
        return cache[i, index]

    def weight(kind, i):
        return weights[kind, i, plane, pl.ds(at, size), :]

    centre = [level(i, plane + 2) for i in range(tiles)]
    after, before = sideways(centre, step)
    result = []
    for i in range(tiles):
        row_after = field[i, plane + 2, pl.ds(PAD + at + step, size), :]
        row_before = field[i, plane + 2, pl.ds(PAD + at - step, size), :]
        deep = weight(AFTER_DEPTH, i) * level(i, plane + 3) + weight(BEFORE_DEPTH, i) * level(
            i, plane + 1
        )
        down = weight(AFTER_ROW, i) * row_after + weight(BEFORE_ROW, i) * row_before
        along = weight(AFTER_COLUMN, i) * after[i] + weight(BEFORE_COLUMN, i) * before[i]
        result.append(((deep + down) + along, centre[i]))
    return result


def set_weights(weights, where, c, scale, drift_scale, tile, tiles, step):
    size = c[0].shape[-2]
    base = scale * c[0]
    for axis in range(3):
        drift = drift_scale * c[axis + 1]
        after, before = base - drift, base + drift
        if axis == 2 and tile == tiles - 1:
            after = jnp.where(lane_index(size) >= LANES - step, 0.0, after)
        if axis == 2 and tile == 0:
            before = jnp.where(lane_index(size) < step, 0.0, before)
        weights[(2 * axis,) + where] = after
        weights[(2 * axis + 1,) + where] = before


def clear_edges(field, first, last):
    tiles, planes = field.shape[:2]
    size = field.shape[2]
    plane = jnp.zeros((tiles, 1, size, LANES), jnp.float32)
    field[:, 1:2] = plane
    field[:, planes - 2 : planes - 1] = plane
    rows = jnp.zeros((tiles, planes - 4, PAD, LANES), jnp.float32)
    field[:, 2 : planes - 2, first : first + PAD, :] = rows
    field[:, 2 : planes - 2, PAD + last : PAD + last + PAD, :] = rows


def fine_scheme():
    scales, carries, tildes = chebyshev_coefficients(SECTIONS)
    centre = INTERVAL / (tildes[1] * FINE_STEP)
    factors = [1.0]
    for degree in range(1, SECTIONS + 1):
        factors.append(factors[-1] * tildes[degree] * FINE_STEP / INTERVAL)
    back = [0.0, 0.0]
    for degree in range(2, SECTIONS + 1):
        back.append(carries[degree] * factors[degree - 2] / factors[degree])
    return centre, back, factors[SECTIONS]


def row_places(box, sizes):
    place, count = lax.axis_index("coarse"), lax.axis_size("coarse")
    odd = place % 2
    result = []
    gone = 0
    for step, size in enumerate(sizes, 1):
        below = pl.multiple_of(box.side - gone - size, 8)
        above = pl.multiple_of(box.side + box.rows + gone, 8)
        gone += size
        one = pl.multiple_of(jnp.where(odd == 1, below, above), 8)
        two = pl.multiple_of(jnp.where(odd == 1, above, below), 8)
        below_valid, above_valid = place >= step, place + step < count
        one_valid = jnp.where(odd == 1, below_valid, above_valid)
        two_valid = jnp.where(odd == 1, above_valid, below_valid)
        result.append(((one, one_valid), (two, two_valid)))
    return result


def place_pieces(box, own_depth, pieces, starts, coeff, weights):
    core = lax.axis_index("tm") % 2
    centre_constant = fine_scheme()[0]
    for own, other, block, blocks, at, valid in pieces:
        shift = lax.axis_index("slab") if blocks == 2 else 0
        base = (block + shift) % blocks * own_depth
        size = own.shape[-2]
        for plane in range(own_depth):
            for i in range(box.tiles):
                cols = slice(i * LANES, (i + 1) * LANES)
                where = (i, base + plane, pl.ds(at, size), slice(None))
                for ref, rank in ((own, core), (other, 1 - core)):
                    for slot, kind in ((2 - 2 * rank, None), (rank, 1 + rank), (1 + rank, 3 * rank)):
                        value = ref[slot, plane, :, cols]
                        if valid is not None:
                            value = jnp.where(valid, value, 0.0)
                        if kind is None:
                            starts[(rank,) + where] = value
                        else:
                            coeff[(kind,) + where] = value
                c = [coeff[(k,) + where] for k in range(4)]
                set_weights(weights, where, c, INTERVAL, 0.5 * INTERVAL, i, box.tiles, 1)
                weights[(CENTRE,) + where] = centre_constant - 6.0 * INTERVAL * c[0]


def early_body(box, own_depth, blocks, *refs):
    starts, coeff, weights = refs[-3:]
    half = (len(refs) - 3) // 2
    own, other = refs[:half], refs[half : 2 * half]
    places = row_places(box, [ref.shape[-2] for ref in own[blocks::2]])
    moves = [(own[block], other[block], block, blocks, box.side, None) for block in range(blocks)]
    for step, pair in enumerate(places):
        for which, (at, valid) in enumerate(pair):
            index = blocks + 2 * step + which
            moves.append((own[index], other[index], 0, blocks, at, valid))
    place_pieces(box, own_depth, moves, starts, coeff, weights)


def fine_body(box, margin, own_depth, blocks, *refs):
    end, starts, coeff, weights, one, two = refs[-6:]
    half = (len(refs) - 9) // 2
    own, other = refs[:half], refs[half : 2 * half]
    core = lax.axis_index("tm") % 2
    moves = []
    if blocks > 1:
        each = half // (blocks - 1)
        places = row_places(box, [ref.shape[-2] for ref in own[0:each:2]])
        for block in range(1, blocks):
            for step, pair in enumerate(places):
                for which, (at, valid) in enumerate(pair):
                    index = (block - 1) * each + 2 * step + which
                    moves.append((own[index], other[index], block, blocks, at, valid))
    place_pieces(box, own_depth, moves, starts, coeff, weights)
    clear_edges(one, 0, box.height)
    clear_edges(two, 0, box.height)
    one[:, 2 : 2 + box.depth, PAD : PAD + box.height, :] = starts[core]
    _, back, factor = fine_scheme()
    stage = 0
    current, other_field = one, two
    first, last = box.span(margin)
    for repeat in range(FINE_STEPS):
        for degree in range(1, SECTIONS + 1):
            stage += 1
            final = stage == FINE_REACH

            def body(plane, at, size, cache, current=current, old=other_field, degree=degree, final=final):
                values = neighbours(current, weights, plane, at, size, 1, cache)
                for i, (total, centre) in enumerate(values):
                    value = total + weights[CENTRE, i, plane, pl.ds(at, size), :] * centre
                    where = (i, plane + 2, pl.ds(PAD + at, size), slice(None))
                    if degree > 1:
                        value = value + back[degree] * old[where]
                    if final:
                        end[i, plane, pl.ds(at - first, size), :] = factor**FINE_STEPS * value
                    else:
                        old[where] = value

            sweep(box.depth, *box.span(margin + FINE_REACH - stage), body)
            current, other_field = other_field, current


def pair_columns(value):
    lane = lane_index(value.shape[0])
    other = jnp.where(
        lane % 2 == 0, pltpu.roll(value, LANES - 1, 1), pltpu.roll(value, 1, 1)
    )
    return value + other


def pair_rows(field, i, plane, at, size):
    row = row_index(size)
    other = jnp.where(
        row % 2 == 0,
        field[i, plane + 2, pl.ds(PAD + at + 1, size), :],
        field[i, plane + 2, pl.ds(PAD + at - 1, size), :],
    )
    return field[i, plane + 2, pl.ds(PAD + at, size), :] + other


def prepare_body(box, coeff, coarse, weight, work):
    half = box.depth // 2
    for k in range(4):
        clear_edges(work.at[k], 0, box.height)

        def columns(plane, at, size, cache, k=k):
            for i in range(box.tiles):
                low = coeff[k, i, 2 * plane, pl.ds(at, size), :]
                high = coeff[k, i, 2 * plane + 1, pl.ds(at, size), :]
                work[k, i, plane + 2, pl.ds(PAD + at, size), :] = pair_columns(low + high)
                if k == 0:
                    for offset, value in ((0, low), (1, high)):
                        weight[i, 2 * plane + offset, pl.ds(at, size), :] = RELAX / (
                            1.0 + 6.0 * INTERVAL * value
                        )

        sweep(half, 0, box.height, columns)

    def rows(plane, at, size, cache):
        for i in range(box.tiles):
            where = (i, plane, pl.ds(at, size), slice(None))
            c = [0.125 * pair_rows(work.at[k], i, plane, at, size) for k in range(4)]
            set_weights(coarse, where, c, INTERVAL / 4.0, INTERVAL / 4.0, i, box.tiles, 2)
            coarse[(CENTRE,) + where] = RELAX / (1.0 + 6.0 * INTERVAL / 4.0 * c[0])

    sweep(half, 0, box.height, rows)


def coarse_step_body(box, margin, source, trial, pairs, guess, residual, params, finish):
    weights, coarse, weight = params
    half = box.depth // 2
    centre_constant = fine_scheme()[0]

    def smooth(plane, at, size, cache):
        values = neighbours(source, weights, plane, at, size, 1, cache)
        for i, (total, centre) in enumerate(values):
            trial[i, plane + 2, pl.ds(PAD + at, size), :] = (1.0 - RELAX) * centre + weight[
                i, plane, pl.ds(at, size), :
            ] * (centre + total)

    first, last = box.span(margin + 5)
    clear_edges(trial, first, last)
    sweep(box.depth, first, last, smooth)

    def restrict(plane, at, size, cache):
        sums = [None] * box.tiles
        for half_plane in range(2):
            fine_plane = 2 * plane + half_plane
            values = neighbours(trial, weights, fine_plane, at, size, 1, cache)
            for i, (total, centre) in enumerate(values):
                given = source[i, fine_plane + 2, pl.ds(PAD + at, size), :]
                inner = weights[CENTRE, i, fine_plane, pl.ds(at, size), :] - (1.0 + centre_constant)
                misfit = (given + total) + inner * centre
                sums[i] = misfit if sums[i] is None else sums[i] + misfit
        for i in range(box.tiles):
            pairs[i, plane + 2, pl.ds(PAD + at, size), :] = pair_columns(sums[i])

    first, last = box.span(margin + 4)
    clear_edges(pairs, first, last)
    sweep(half, first, last, restrict)

    def first_guess(plane, at, size, cache):
        for i in range(box.tiles):
            mean = 0.125 * pair_rows(pairs, i, plane, at, size)
            residual[i, plane + 2, pl.ds(PAD + at, size), :] = mean
            guess[i, plane + 2, pl.ds(PAD + at, size), :] = (
                coarse[CENTRE, i, plane, pl.ds(at, size), :] * mean
            )

    clear_edges(guess, first, last)
    sweep(half, first, last, first_guess)

    def correct(plane, at, size, cache):
        values = neighbours(guess, coarse, plane, at, size, 2, cache)
        for i, (total, centre) in enumerate(values):
            rest = residual[i, plane + 2, pl.ds(PAD + at, size), :] + total
            fix = (1.0 - RELAX) * centre + coarse[CENTRE, i, plane, pl.ds(at, size), :] * rest
            for half_plane in range(2):
                where = (i, 2 * plane + half_plane + 2, pl.ds(PAD + at, size), slice(None))
                trial[where] = trial[where] + fix

    sweep(half, *box.span(margin + 2), correct)

    def smooth_again(plane, at, size, cache):
        values = neighbours(trial, weights, plane, at, size, 1, cache)
        for i, (total, centre) in enumerate(values):
            given = source[i, plane + 2, pl.ds(PAD + at, size), :]
            value = (1.0 - RELAX) * centre + weight[i, plane, pl.ds(at, size), :] * (given + total)
            finish(plane, i, at, size, value)

    sweep(box.depth, *box.span(margin), smooth_again)


def coarse_scratch(box):
    half = box.depth // 2
    return [box.scratch(), box.scratch(half), box.scratch(half), box.scratch(half)]


def pair_body(box, own_end, other_end, starts, *rest):
    params, out, first_out, leaving = rest[:3], rest[3], rest[4], rest[5]
    source, trial, pairs, guess, residual = rest[6:]
    core = lax.axis_index("tm") % 2
    first, last = box.span(COARSE_REACH)
    clear_edges(source, first, last)

    def put(first_end, second_end):
        source[:, 2 : 2 + box.depth, PAD + first : PAD + last, :] = (
            first_end[...] - starts[1, :, :, first:last, :]
        )
        inner = slice(box.side - first, box.side - first + box.rows)
        out[...] = second_end[:, :, inner, :]
        first_out[...] = first_end[:, :, inner, :]

    @pl.when(core == 0)
    def _():
        put(own_end, other_end)

    @pl.when(core == 1)
    def _():
        put(other_end, own_end)

    def finish(plane, i, at, size, value):
        where = (i, plane, pl.ds(at - box.side, size), slice(None))
        out[where] = value + out[where]

    coarse_step_body(box, 0, source, trial, pairs, guess, residual, params, finish)
    half = box.depth // 2
    leaving[...] = out[:, pl.ds(core * half, half)]


def last_body(box, own_depth, turn, pieces, first_end, joined, *rest):
    arrived, rest = rest[:pieces], rest[pieces:]
    starts, params, result, leaving = rest[0], rest[1:4], rest[4], rest[5]
    source, second, trial, pairs, guess, residual, total = rest[6:]
    place = lax.axis_index("tm")
    core = place % 2
    active = place // 2 == turn
    side, rows = box.side, box.rows
    half = box.depth // 2
    clear_edges(source, 0, box.height)
    clear_edges(second, *box.span(COARSE_REACH))
    each = pieces // 2
    places = row_places(box, [arrived[at].shape[-2] for at in range(1, each, 2)])

    @pl.when(jnp.logical_not(active))
    def _():
        source[:, 2 : 2 + box.depth, PAD : PAD + box.height, :] = jnp.zeros(
            (box.tiles, box.depth, box.height, LANES), jnp.float32
        )

    @pl.when(active)
    def _():
        for part, rank in ((0, core), (1, 1 - core)):
            moves = [(arrived[part * each], side, None)]
            for step, pair in enumerate(places):
                at = part * each + 1 + 2 * step
                for ref, (where, valid) in zip(arrived[at : at + 2], pair):
                    moves.append((ref, where, valid))
            base = rank * half
            for ref, at, valid in moves:
                size = ref.shape[-2]
                for plane in range(half):
                    for i in range(box.tiles):
                        value = ref[i, plane]
                        if valid is not None:
                            value = jnp.where(valid, value, 0.0)
                        source[i, base + plane + 2, pl.ds(PAD + at, size), :] = (
                            value - starts[0, i, base + plane, pl.ds(at, size), :]
                        )

    def finish_once(plane, i, at, size, value):
        second[i, plane + 2, pl.ds(PAD + at, size), :] = value

    coarse_step_body(
        box, COARSE_REACH, source, trial, pairs, guess, residual, params, finish_once
    )

    def finish_twice(plane, i, at, size, value):
        where = (i, plane, pl.ds(at - box.side, size), slice(None))
        total[where] = value + joined[where]

    coarse_step_body(box, 0, second, trial, pairs, guess, residual, params, finish_twice)
    base = lax.axis_index("slab") * own_depth

    @pl.when(core == 0)
    def _():
        for i in range(box.tiles):
            result[0, :, :, i * LANES : (i + 1) * LANES] = (
                first_end[i, pl.ds(base, own_depth)]
                + second[i, pl.ds(base + 2, own_depth), PAD + side : PAD + side + rows, :]
            )

    @pl.when(core == 1)
    def _():
        for i in range(box.tiles):
            result[0, :, :, i * LANES : (i + 1) * LANES] = total[i, pl.ds(base, own_depth)]

    leaving[...] = total[:, pl.ds(core * half, half)]


def run(body, outs, scratch, *args, aliases={}):
    return pl.pallas_call(
        body,
        out_shape=[jax.ShapeDtypeStruct(shape, jnp.float32) for shape in outs],
        in_specs=[pl.BlockSpec(memory_space=pltpu.VMEM)] * len(args),
        out_specs=[pl.BlockSpec(memory_space=pltpu.VMEM)] * len(outs),
        scratch_shapes=scratch,
        input_output_aliases=aliases,
        compiler_params=pltpu.CompilerParams(vmem_limit_bytes=20 * 1024 * 1024),
    )(*args)


def slab_blocks(block):
    count = lax.axis_size("slab")
    if count == 1:
        return [block]
    if count == 2:
        return [block, lax.ppermute(block, "slab", [(0, 1), (1, 0)])]
    gathered = lax.all_gather(block, "slab", axis=0)
    return [gathered[i] for i in range(count)]


def row_swaps(hop, away):
    windows, count = lax.axis_size("tm"), lax.axis_size("coarse")
    rounds = []
    for first in (0, 1):
        pairs = []
        for place in range(count):
            other = place + 1 if place % 2 == first else place - 1
            for t in range(windows):
                inside = 0 <= other < count
                target = (hop(t), other) if inside else (away(t), place)
                pairs.append((t * count + place, target[0] * count + target[1]))
        rounds.append(pairs)
    return rounds


def row_pieces(block, width, rounds):
    rows = block.shape[-2]
    axis = block.ndim - 2
    both = ("tm", "coarse")
    odd = lax.axis_index("coarse") % 2 == 1
    pieces = []
    up, down = block, block
    left = width
    while left > 0:
        size = min(rows, left)
        if size == rows and up is down:
            send_one = send_two = block
        else:
            high = lax.slice_in_dim(up, up.shape[axis] - size, None, axis=axis)
            low = lax.slice_in_dim(down, 0, size, axis=axis)
            send_one, send_two = jnp.where(odd, low, high), jnp.where(odd, high, low)
        got_one = lax.ppermute(send_one, both, rounds[0])
        got_two = lax.ppermute(send_two, both, rounds[1])
        pieces += [got_one, got_two]
        left -= size
        if left > 0:
            up, down = jnp.where(odd, got_one, got_two), jnp.where(odd, got_two, got_one)
    return pieces


def core_swapped(block):
    count = lax.axis_size("tm")
    assert count % 2 == 0
    return lax.ppermute(block, "tm", [(i, i ^ 1) for i in range(count)])


def per_device(states, diffusivity, velocity):
    windows = lax.axis_size("tm")
    place = lax.axis_index("tm")
    own_depth, rows, columns = diffusivity.shape
    side = round_up(FINE_REACH + COARSE_REACH, 8)
    depth = own_depth * lax.axis_size("slab")
    box = Box(depth, rows, side, columns)
    tiles, height, half = box.tiles, box.height, depth // 2

    second = place % 2 == 1
    slot = lax.broadcasted_iota(jnp.int32, (3, 1, 1, 1), 0)
    parcel = jnp.where(
        (slot == 0) != second, velocity, jnp.where(slot == 1, diffusivity[None], states)
    )
    rounds = row_swaps(lambda t: t, lambda t: t ^ 1)
    blocks = slab_blocks(parcel)
    swapped = [core_swapped(block) for block in blocks]
    near = row_pieces(blocks[0], side, rounds)
    near_swapped = [core_swapped(piece) for piece in near]
    count = len(blocks)
    shapes = [(n, tiles, depth, height, LANES) for n in (2, 4, 7)]
    placed = run(
        functools.partial(early_body, box, own_depth, count),
        shapes,
        [],
        *blocks,
        *near,
        *swapped,
        *near_swapped,
    )
    far = []
    for block in blocks[1:]:
        far += row_pieces(block, side, rounds)
    far += [core_swapped(piece) for piece in far]
    first, last = box.span(COARSE_REACH)
    end, starts, coeff, weights = run(
        functools.partial(fine_body, box, COARSE_REACH, own_depth, count),
        [(tiles, depth, last - first, LANES)] + shapes,
        [box.scratch(), box.scratch()],
        *far,
        *placed,
        aliases={len(far) + n: 1 + n for n in range(3)},
    )
    params = run(
        functools.partial(prepare_body, box),
        [(7, tiles, half, height, LANES), (tiles, depth, height, LANES)],
        [pltpu.VMEM((4, *box.scratch(half).shape), jnp.float32)],
        coeff,
    )
    params = [weights, *params]
    joined, first_end, leaving = run(
        functools.partial(pair_body, box),
        [(tiles, depth, rows, LANES)] * 2 + [(tiles, half, rows, LANES)],
        [box.scratch()] + coarse_scratch(box),
        end,
        core_swapped(end),
        starts,
        *params,
    )
    ends = jnp.where(place % 2 == 1, joined, first_end)
    ends = jnp.concatenate([ends[i] for i in range(tiles)], axis=-1)
    base = lax.axis_index("slab") * own_depth
    result = lax.dynamic_slice_in_dim(ends, base, own_depth, 0)[None]
    hop = lambda t: (t + 2) % windows
    rounds = row_swaps(hop, hop)
    for turn in range(1, windows // 2):
        centre = lax.ppermute(leaving, "tm", [(t, hop(t)) for t in range(windows)])
        if rows >= 2 * COARSE_REACH:
            arrived = [centre, *row_pieces(leaving, min(rows, side), rounds)]
        else:
            near = row_swaps(lambda t: t, lambda t: t ^ 1)
            arrived = [centre, *row_pieces(centre, side, near)]
        arrived += [core_swapped(piece) for piece in arrived]
        out, leaving = run(
            functools.partial(last_body, box, own_depth, turn, len(arrived)),
            [(1, own_depth, rows, columns), (tiles, half, rows, LANES)],
            [box.scratch()] * 2
            + coarse_scratch(box)
            + [pltpu.VMEM((tiles, depth, rows, LANES), jnp.float32)],
            first_end,
            joined,
            *arrived,
            starts,
            *params,
        )
        result = out if turn == 1 else jnp.where(place // 2 >= turn, out, result)
    return result


def solution(mesh):
    return jax.shard_map(
        per_device,
        mesh=mesh,
        in_specs=(
            P("tm", "slab", "coarse", None),
            P("slab", "coarse", None),
            P(None, "slab", "coarse", None),
        ),
        out_specs=P("tm", "slab", "coarse", None),
        check_vma=False,
    )
```

time: 36.8 us -> 35.9 us (0.976)
  Pallas kernels: 8.17 us -> 7.59 us
  waiting for transfers between devices: 11.3 us -> 10.9 us
    pallas_call x4 -> x5, Pallas kernels: 8.17 us -> 7.59 us  [run(): pl.pallas_call(body, out_shape=[jax.ShapeDtypeStruct(shape, jnp.float32)...]
    ppermute x10, waiting for transfers between devices: 3.43 us -> 3.03 us  [core_swapped(): return lax.ppermute(block, 'tm', [(i, i ^ 1) for i in range(count)])]
  transfers between devices with their start and end apart: 18 -> 18, of which waited for: 9 -> 8; matrix products, arithmetic and copies ran while one was open for 0% -> 0% of each run, Pallas kernels for 2% -> 3%
where the time goes in v5:
time: 35.9 us; the launch traced here: 35.7 us
  starting transfers between devices  16.1 us (45%)
  waiting for transfers between devices  10.9 us (30%)
  Pallas kernels  7.59 us (21%)
  other arithmetic  1.06 us (3%)
    ppermute x3, starting transfers between devices, row_pieces(): got_one = lax.ppermute(send_one, both, rounds[0])  8.22 us
    pallas_call x5, Pallas kernels, run(): pl.pallas_call(body, out_shape=[jax.ShapeDtypeStruct(shape, jnp.float32)...  7.59 us
    ppermute x3, waiting for transfers between devices, row_pieces(): got_one = lax.ppermute(send_one, both, rounds[0])  4.89 us
    ppermute x1, starting transfers between devices, slab_blocks(): return [block, lax.ppermute(block, 'slab', [(0, 1), (1, 0)])]  3.04 us
    ppermute x10, waiting for transfers between devices, core_swapped(): return lax.ppermute(block, 'tm', [(i, i ^ 1) for i in range(count)])  3.03 us
    ppermute x3, starting transfers between devices, row_pieces(): got_two = lax.ppermute(send_two, both, rounds[1])  2.09 us
    ppermute x1, waiting for transfers between devices, slab_blocks(): return [block, lax.ppermute(block, 'slab', [(0, 1), (1, 0)])]  1.74 us
    ppermute x1, starting transfers between devices, per_device(): centre = lax.ppermute(leaving, 'tm', [(t, hop(t)) for t in range(windows)])  1.52 us
  transfers between devices with their start and end apart: 18, of which 8 were waited for; matrix products, arithmetic and copies ran while one was open for 0% of the time, Pallas kernels for 3%

profile of v5, /device:TPU:0, one launch (start us, length us, event | category | flops | bytes accessed | tf_op | source)
XLA Modules:
  0.0 35.7 jit_solution(6519986727139147161)
XLA Ops:
  0.0 1.1 %select_select_fusion.refs_0_ = f32[3,4,16,256]{3,2,1,0:T(8,128)S(1)} fusion(f32[3,4,16,256]{3,2,1,0:T(8,128)} %param.5, f32[4,16,256]{2,1,0:T(8,128)} %bitcast.1, f32[4,16,256]{2,1,0:T(8,128)} %param.4, pred[3]{0:T(512)(128)(4,1)S(1)} %get-tuple-element.32, pred[3]{0:T(512)(128)(4,1)S(1)} %get-tuple-element.31), kind=kLoop, calls=%fused_computation | loop fusion | flops 98304 | bytes 524294 | tf_op jit(solution)/shard_map/jit(_where)/select_n | solution.py:578
  1.1 3.0 %collective-permute-start = (f32[3,4,16,256]{3,2,1,0:T(8,128)S(1)}, f32[3,4,16,256]{3,2,1,0:T(8,128)S(1)}, u32[]{:S(2)}, u32[]{:S(2)}) collective-permute-start(f32[3,4,16,256]{3,2,1,0:T(8,128)S(1)} %select_select_fusion.refs_0_), channel_id=1, source_target_pairs={{0,4},{4,0},{1,5},{5,1},{2,6},{6,2},{3,7},{7,3},{8,12},{12,8},{9,1... | collective-permute-start | bytes 589832 | tf_op jit(solution)/shard_map/ppermute | solution.py:516
  4.1 0.5 %collective-permute-start.6 = (f32[3,4,16,256]{3,2,1,0:T(8,128)S(1)}, f32[3,4,16,256]{3,2,1,0:T(8,128)S(1)}, u32[]{:S(2)}, u32[]{:S(2)}) collective-permute-start(f32[3,4,16,256]{3,2,1,0:T(8,128)S(1)} %select_select_fusion.refs_0_), channel_id=1, source_target_pairs={{0,8},{8,0},{16,24},{24,16},{1,2},{9,10},{17,18},{25,26},{2,1},{10... | collective-permute-start | bytes 589832 | tf_op jit(solution)/shard_map/ppermute | solution.py:553
  4.6 2.6 %collective-permute-start.5 = (f32[3,4,16,256]{3,2,1,0:T(8,128)S(1)}, f32[3,4,16,256]{3,2,1,0:T(8,128)S(1)}, u32[]{:S(2)}, u32[]{:S(2)}) collective-permute-start(f32[3,4,16,256]{3,2,1,0:T(8,128)S(1)} %select_select_fusion.refs_0_), channel_id=1, source_target_pairs={{0,1},{8,9},{16,17},{24,25},{1,0},{9,8},{17,16},{25,24},{2,3},{10,... | collective-permute-start | bytes 589832 | tf_op jit(solution)/shard_map/ppermute | solution.py:552
  7.3 1.7 %collective-permute-done.refs_1_ = f32[3,4,16,256]{3,2,1,0:T(8,128)S(1)} collective-permute-done((f32[3,4,16,256]{3,2,1,0:T(8,128)S(1)}, f32[3,4,16,256]{3,2,1,0:T(8,128)S(1)}, u32[]{:S(2)}, u32[]{:S(2)}) %collective-permute-start) | collective-permute-done | bytes 196640 | tf_op jit(solution)/shard_map/ppermute | solution.py:516
  9.0 3.4 %collective-permute-start.1 = (f32[3,4,16,256]{3,2,1,0:T(8,128)S(1)}, f32[3,4,16,256]{3,2,1,0:T(8,128)S(1)}, u32[]{:S(2)}, u32[]{:S(2)}) collective-permute-start(f32[3,4,16,256]{3,2,1,0:T(8,128)S(1)} %collective-permute-done.refs_1_), channel_id=1, source_target_pairs={{0,1},{8,9},{16,17},{24,25},{1,0},{9,8},{17,16},{25,24},{2,3},{10,... | collective-permute-start | bytes 589832 | tf_op jit(solution)/shard_map/ppermute | solution.py:552
  12.4 0.0 collective-permute-done.7.refs_4_
  12.4 0.0 collective-permute-start.8
  12.4 0.0 collective-permute-done.6.refs_3_
  12.4 0.5 %collective-permute-start.10 = (f32[3,4,16,256]{3,2,1,0:T(8,128)S(1)}, f32[3,4,16,256]{3,2,1,0:T(8,128)S(1)}, u32[]{:S(2)}, u32[]{:S(2)}) collective-permute-start(f32[3,4,16,256]{3,2,1,0:T(8,128)S(1)} %collective-permute-done.6.refs_3_), channel_id=1, source_target_pairs={{0,8},{8,0},{16,24},{24,16},{1,9},{9,1},{17,25},{25,17},{2,10},{10... | collective-permute-start | bytes 589832 | tf_op jit(solution)/shard_map/ppermute | solution.py:564
  12.9 0.1 collective-permute-done.5.refs_2_
  13.0 0.0 collective-permute-start.9
  13.0 0.5 %collective-permute-start.4 = (f32[3,4,16,256]{3,2,1,0:T(8,128)S(1)}, f32[3,4,16,256]{3,2,1,0:T(8,128)S(1)}, u32[]{:S(2)}, u32[]{:S(2)}) collective-permute-start(f32[3,4,16,256]{3,2,1,0:T(8,128)S(1)} %collective-permute-done.2.refs_1_), channel_id=1, source_target_pairs={{0,8},{8,0},{16,24},{24,16},{1,9},{9,1},{17,25},{25,17},{2,10},{10... | collective-permute-start | bytes 589832 | tf_op jit(solution)/shard_map/ppermute | solution.py:564
  13.5 3.3 %collective-permute-done.1.refs_0_ = f32[3,4,16,256]{3,2,1,0:T(8,128)S(1)} collective-permute-done((f32[3,4,16,256]{3,2,1,0:T(8,128)S(1)}, f32[3,4,16,256]{3,2,1,0:T(8,128)S(1)}, u32[]{:S(2)}, u32[]{:S(2)}) %collective-permute-start.1) | collective-permute-done | bytes 196640 | tf_op jit(solution)/shard_map/ppermute | solution.py:552
  16.8 0.0 collective-permute-done.10.refs_7_
  16.8 0.0 collective-permute-done.9.refs_6_
  16.8 0.0 collective-permute-done.8.refs_5_
  16.8 0.4 %shard_map.37 = (f32[2,2,8,48,128]{4,3,2,1,0:T(8,128)S(1)}, f32[4,2,8,48,128]{4,3,2,1,0:T(8,128)S(1)}, f32[7,2,8,48,128]{4,3,2,1,0:T(8,128)S(1)}) custom-call(f32[3,4,16,256]{3,2,1,0:T(8,128)S(1)} %select_select_fusion.refs_0_, f32[3,4,16,256]{3,2,1,0:T(8,128)S(1)} %collective-permute-done.refs_1_, f32[3,4,16,256]{3,2,1,0:T(8,128)S(1)} %collective-permute-done.5.refs_2_, ...), custom_call_target="tpu_custom_call" | custom-call | tf_op jit(solution)/shard_map/pallas_call | solution.py:500
  17.2 1.0 %collective-permute-done.3.refs_2_ = f32[3,4,16,256]{3,2,1,0:T(8,128)S(1)} collective-permute-done((f32[3,4,16,256]{3,2,1,0:T(8,128)S(1)}, f32[3,4,16,256]{3,2,1,0:T(8,128)S(1)}, u32[]{:S(2)}, u32[]{:S(2)}) %collective-permute-start.3) | collective-permute-done | bytes 196640 | tf_op jit(solution)/shard_map/ppermute | solution.py:564
  18.2 1.9 %shard_map.38 = (f32[2,8,32,128]{3,2,1,0:T(8,128)S(1)}, f32[2,2,8,48,128]{4,3,2,1,0:T(8,128)S(1)}, f32[4,2,8,48,128]{4,3,2,1,0:T(8,128)S(1)}, f32[7,2,8,48,128]{4,3,2,1,0:T(8,128)S(1)}) custom-call(f32[3,4,16,256]{3,2,1,0:T(8,128)S(1)} %collective-permute-done.1.refs_0_, ...), custom_call_target="tpu_custom_call", output_to_operand_aliasing={{1}: (4, {}), {2}: (5, {}), {3}: (6, {})} | custom-call | tf_op jit(solution)/shard_map/pallas_call | solution.py:500
  20.1 0.2 collective-permute-start.11
  20.3 0.6 %shard_map.39 = (f32[7,2,4,48,128]{4,3,2,1,0:T(8,128)S(1)}, f32[2,8,48,128]{3,2,1,0:T(8,128)S(1)}) custom-call(f32[4,2,8,48,128]{4,3,2,1,0:T(8,128)S(1)} %get-tuple-element.24.coeff), custom_call_target="tpu_custom_call" | custom-call | tf_op jit(solution)/shard_map/pallas_call | solution.py:500
  21.0 0.7 %collective-permute-done.11.other_end = f32[2,8,32,128]{3,2,1,0:T(8,128)S(1)} collective-permute-done((f32[2,8,32,128]{3,2,1,0:T(8,128)S(1)}, f32[2,8,32,128]{3,2,1,0:T(8,128)S(1)}, u32[]{:S(2)}, u32[]{:S(2)}) %collective-permute-start.11) | collective-permute-done | bytes 262176 | tf_op jit(solution)/shard_map/ppermute | solution.py:564
  21.7 1.2 %shard_map.40 = (f32[2,8,16,128]{3,2,1,0:T(8,128)S(1)}, f32[2,8,16,128]{3,2,1,0:T(8,128)S(1)}, f32[2,4,16,128]{3,2,1,0:T(8,128)S(1)}) custom-call(f32[2,8,32,128]{3,2,1,0:T(8,128)S(1)} %get-tuple-element.21.own_end, f32[2,8,32,128]{3,2,1,0:T(8,128)S(1)} %collective-permute-done.11.other_end, f32[2,2,8,48,128]{4,3,2,1,0:T(8,128)S(1)} %get-tuple-element.22.starts.rest_6_, ...), custom_call_target="tpu_custom_call" | custom-call | tf_op jit(solution)/shard_map/pallas_call | solution.py:500
  22.9 1.6 %collective-permute-start.14 = (f32[2,4,16,128]{3,2,1,0:T(8,128)S(1)}, f32[2,4,16,128]{3,2,1,0:T(8,128)S(1)}, u32[]{:S(2)}, u32[]{:S(2)}) collective-permute-start(f32[2,4,16,128]{3,2,1,0:T(8,128)S(1)} %get-tuple-element.29), channel_id=1, source_target_pairs={{0,16},{8,24},{16,0},{24,8},{1,18},{9,26},{17,2},{25,10},{2,17},{1... | collective-permute-start | bytes 196616 | tf_op jit(solution)/shard_map/ppermute | solution.py:553
  24.5 2.2 %collective-permute-start.13 = (f32[2,4,16,128]{3,2,1,0:T(8,128)S(1)}, f32[2,4,16,128]{3,2,1,0:T(8,128)S(1)}, u32[]{:S(2)}, u32[]{:S(2)}) collective-permute-start(f32[2,4,16,128]{3,2,1,0:T(8,128)S(1)} %get-tuple-element.29), channel_id=1, source_target_pairs={{0,17},{8,25},{16,1},{24,9},{1,16},{9,24},{17,0},{25,8},{2,19},{10... | collective-permute-start | bytes 196616 | tf_op jit(solution)/shard_map/ppermute | solution.py:552
  26.7 1.5 %collective-permute-start.12 = (f32[2,4,16,128]{3,2,1,0:T(8,128)S(1)}, f32[2,4,16,128]{3,2,1,0:T(8,128)S(1)}, u32[]{:S(2)}, u32[]{:S(2)}) collective-permute-start(f32[2,4,16,128]{3,2,1,0:T(8,128)S(1)} %get-tuple-element.29), channel_id=1, source_target_pairs={{0,16},{8,24},{16,0},{24,8},{1,17},{9,25},{17,1},{25,9},{2,18},{10... | collective-permute-start | bytes 196616 | tf_op jit(solution)/shard_map/ppermute | solution.py:633
  28.2 1.6 %collective-permute-done.13.rest_1_ = f32[2,4,16,128]{3,2,1,0:T(8,128)S(1)} collective-permute-done((f32[2,4,16,128]{3,2,1,0:T(8,128)S(1)}, f32[2,4,16,128]{3,2,1,0:T(8,128)S(1)}, u32[]{:S(2)}, u32[]{:S(2)}) %collective-permute-start.13) | collective-permute-done | bytes 65568 | tf_op jit(solution)/shard_map/ppermute | solution.py:552
  29.8 1.2 %collective-permute-done.12.rest_0_ = f32[2,4,16,128]{3,2,1,0:T(8,128)S(1)} collective-permute-done((f32[2,4,16,128]{3,2,1,0:T(8,128)S(1)}, f32[2,4,16,128]{3,2,1,0:T(8,128)S(1)}, u32[]{:S(2)}, u32[]{:S(2)}) %collective-permute-start.12) | collective-permute-done | bytes 65568 | tf_op jit(solution)/shard_map/ppermute | solution.py:633
  31.0 0.0 collective-permute-done.16.rest_4_
  31.0 1.2 %collective-permute-done.15.rest_3_ = f32[2,4,16,128]{3,2,1,0:T(8,128)S(1)} collective-permute-done((f32[2,4,16,128]{3,2,1,0:T(8,128)S(1)}, f32[2,4,16,128]{3,2,1,0:T(8,128)S(1)}, u32[]{:S(2)}, u32[]{:S(2)}) %collective-permute-start.15) | collective-permute-done | bytes 65568 | tf_op jit(solution)/shard_map/ppermute | solution.py:564
  32.2 3.5 %shard_map.41 = (f32[1,4,16,256]{3,2,1,0:T(8,128)}, f32[2,4,16,128]{3,2,1,0:T(8,128)}) custom-call(f32[2,8,16,128]{3,2,1,0:T(8,128)S(1)} %get-tuple-element.27.first_end, f32[2,8,16,128]{3,2,1,0:T(8,128)S(1)} %get-tuple-element.28.joined, f32[2,4,16,128]{3,2,1,0:T(8,128)S(1)} %collective-permute-done.12.rest_0_, ...), custom_call_target="tpu_custom_call" | custom-call | tf_op jit(solution)/shard_map/pallas_call | solution.py:500
  (11 shorter events, 0.0 us)
Async XLA Ops:
  1.1 7.9 %collective-permute-start = (f32[3,4,16,256]{3,2,1,0:T(8,128)S(1)}, f32[3,4,16,256]{3,2,1,0:T(8,128)S(1)}, u32[]{:S(2)}, u32[]{:S(2)}) collective-permute-start(f32[3,4,16,256]{3,2,1,0:T(8,128)S(1)} %select_select_fusion.refs_0_), channel_id=1, source_target_pairs={{0,4},{4,0},{1,5},{5,1},{2,6},{6,2},{3,7},{7,3},{8,12},{12,8},{9,1... | collective-permute-start | bytes 589832 | tf_op jit(solution)/shard_map/ppermute | solution.py:516
  4.1 8.3 %collective-permute-start.7 = (f32[3,4,16,256]{3,2,1,0:T(8,128)S(1)}, f32[3,4,16,256]{3,2,1,0:T(8,128)S(1)}, u32[]{:S(2)}, u32[]{:S(2)}) collective-permute-start(f32[3,4,16,256]{3,2,1,0:T(8,128)S(1)} %select_select_fusion.refs_0_), channel_id=1, source_target_pairs={{0,8},{8,0},{16,24},{24,16},{1,9},{9,1},{17,25},{25,17},{2,10},{10... | collective-permute-start | bytes 589832 | tf_op jit(solution)/shard_map/ppermute | solution.py:564
  4.1 8.3 %collective-permute-start.6 = (f32[3,4,16,256]{3,2,1,0:T(8,128)S(1)}, f32[3,4,16,256]{3,2,1,0:T(8,128)S(1)}, u32[]{:S(2)}, u32[]{:S(2)}) collective-permute-start(f32[3,4,16,256]{3,2,1,0:T(8,128)S(1)} %select_select_fusion.refs_0_), channel_id=1, source_target_pairs={{0,8},{8,0},{16,24},{24,16},{1,2},{9,10},{17,18},{25,26},{2,1},{10... | collective-permute-start | bytes 589832 | tf_op jit(solution)/shard_map/ppermute | solution.py:553
  4.6 8.4 %collective-permute-start.5 = (f32[3,4,16,256]{3,2,1,0:T(8,128)S(1)}, f32[3,4,16,256]{3,2,1,0:T(8,128)S(1)}, u32[]{:S(2)}, u32[]{:S(2)}) collective-permute-start(f32[3,4,16,256]{3,2,1,0:T(8,128)S(1)} %select_select_fusion.refs_0_), channel_id=1, source_target_pairs={{0,1},{8,9},{16,17},{24,25},{1,0},{9,8},{17,16},{25,24},{2,3},{10,... | collective-permute-start | bytes 589832 | tf_op jit(solution)/shard_map/ppermute | solution.py:552
  9.0 4.0 %collective-permute-start.2 = (f32[3,4,16,256]{3,2,1,0:T(8,128)S(1)}, f32[3,4,16,256]{3,2,1,0:T(8,128)S(1)}, u32[]{:S(2)}, u32[]{:S(2)}) collective-permute-start(f32[3,4,16,256]{3,2,1,0:T(8,128)S(1)} %collective-permute-done.refs_1_), channel_id=1, source_target_pairs={{0,8},{8,0},{16,24},{24,16},{1,2},{9,10},{17,18},{25,26},{2,1},{10... | collective-permute-start | bytes 589832 | tf_op jit(solution)/shard_map/ppermute | solution.py:553
  9.0 7.8 %collective-permute-start.1 = (f32[3,4,16,256]{3,2,1,0:T(8,128)S(1)}, f32[3,4,16,256]{3,2,1,0:T(8,128)S(1)}, u32[]{:S(2)}, u32[]{:S(2)}) collective-permute-start(f32[3,4,16,256]{3,2,1,0:T(8,128)S(1)} %collective-permute-done.refs_1_), channel_id=1, source_target_pairs={{0,1},{8,9},{16,17},{24,25},{1,0},{9,8},{17,16},{25,24},{2,3},{10,... | collective-permute-start | bytes 589832 | tf_op jit(solution)/shard_map/ppermute | solution.py:552
  12.4 4.4 %collective-permute-start.8 = (f32[3,4,16,256]{3,2,1,0:T(8,128)S(1)}, f32[3,4,16,256]{3,2,1,0:T(8,128)S(1)}, u32[]{:S(2)}, u32[]{:S(2)}) collective-permute-start(f32[3,4,16,256]{3,2,1,0:T(8,128)S(1)} %collective-permute-done.refs_1_), channel_id=1, source_target_pairs={{0,8},{8,0},{16,24},{24,16},{1,9},{9,1},{17,25},{25,17},{2,10},{10... | collective-permute-start | bytes 589832 | tf_op jit(solution)/shard_map/ppermute | solution.py:564
  12.4 4.4 %collective-permute-start.10 = (f32[3,4,16,256]{3,2,1,0:T(8,128)S(1)}, f32[3,4,16,256]{3,2,1,0:T(8,128)S(1)}, u32[]{:S(2)}, u32[]{:S(2)}) collective-permute-start(f32[3,4,16,256]{3,2,1,0:T(8,128)S(1)} %collective-permute-done.6.refs_3_), channel_id=1, source_target_pairs={{0,8},{8,0},{16,24},{24,16},{1,9},{9,1},{17,25},{25,17},{2,10},{10... | collective-permute-start | bytes 589832 | tf_op jit(solution)/shard_map/ppermute | solution.py:564
  13.0 3.8 %collective-permute-start.9 = (f32[3,4,16,256]{3,2,1,0:T(8,128)S(1)}, f32[3,4,16,256]{3,2,1,0:T(8,128)S(1)}, u32[]{:S(2)}, u32[]{:S(2)}) collective-permute-start(f32[3,4,16,256]{3,2,1,0:T(8,128)S(1)} %collective-permute-done.5.refs_2_), channel_id=1, source_target_pairs={{0,8},{8,0},{16,24},{24,16},{1,9},{9,1},{17,25},{25,17},{2,10},{10... | collective-permute-start | bytes 589832 | tf_op jit(solution)/shard_map/ppermute | solution.py:564
  13.0 4.2 %collective-permute-start.4 = (f32[3,4,16,256]{3,2,1,0:T(8,128)S(1)}, f32[3,4,16,256]{3,2,1,0:T(8,128)S(1)}, u32[]{:S(2)}, u32[]{:S(2)}) collective-permute-start(f32[3,4,16,256]{3,2,1,0:T(8,128)S(1)} %collective-permute-done.2.refs_1_), channel_id=1, source_target_pairs={{0,8},{8,0},{16,24},{24,16},{1,9},{9,1},{17,25},{25,17},{2,10},{10... | collective-permute-start | bytes 589832 | tf_op jit(solution)/shard_map/ppermute | solution.py:564
  16.8 1.4 %collective-permute-start.3 = (f32[3,4,16,256]{3,2,1,0:T(8,128)S(1)}, f32[3,4,16,256]{3,2,1,0:T(8,128)S(1)}, u32[]{:S(2)}, u32[]{:S(2)}) collective-permute-start(f32[3,4,16,256]{3,2,1,0:T(8,128)S(1)} %collective-permute-done.1.refs_0_), channel_id=1, source_target_pairs={{0,8},{8,0},{16,24},{24,16},{1,9},{9,1},{17,25},{25,17},{2,10},{10... | collective-permute-start | bytes 589832 | tf_op jit(solution)/shard_map/ppermute | solution.py:564
  20.1 1.6 %collective-permute-start.11 = (f32[2,8,32,128]{3,2,1,0:T(8,128)S(1)}, f32[2,8,32,128]{3,2,1,0:T(8,128)S(1)}, u32[]{:S(2)}, u32[]{:S(2)}) collective-permute-start(f32[2,8,32,128]{3,2,1,0:T(8,128)S(1)} %get-tuple-element.21.own_end), channel_id=1, source_target_pairs={{0,8},{8,0},{16,24},{24,16},{1,9},{9,1},{17,25},{25,17},{2,10},{10... | collective-permute-start | bytes 786440 | tf_op jit(solution)/shard_map/ppermute | solution.py:564
  22.9 5.3 %collective-permute-start.14 = (f32[2,4,16,128]{3,2,1,0:T(8,128)S(1)}, f32[2,4,16,128]{3,2,1,0:T(8,128)S(1)}, u32[]{:S(2)}, u32[]{:S(2)}) collective-permute-start(f32[2,4,16,128]{3,2,1,0:T(8,128)S(1)} %get-tuple-element.29), channel_id=1, source_target_pairs={{0,16},{8,24},{16,0},{24,8},{1,18},{9,26},{17,2},{25,10},{2,17},{1... | collective-permute-start | bytes 196616 | tf_op jit(solution)/shard_map/ppermute | solution.py:553
  24.5 5.3 %collective-permute-start.13 = (f32[2,4,16,128]{3,2,1,0:T(8,128)S(1)}, f32[2,4,16,128]{3,2,1,0:T(8,128)S(1)}, u32[]{:S(2)}, u32[]{:S(2)}) collective-permute-start(f32[2,4,16,128]{3,2,1,0:T(8,128)S(1)} %get-tuple-element.29), channel_id=1, source_target_pairs={{0,17},{8,25},{16,1},{24,9},{1,16},{9,24},{17,0},{25,8},{2,19},{10... | collective-permute-start | bytes 196616 | tf_op jit(solution)/shard_map/ppermute | solution.py:552
  26.7 4.3 %collective-permute-start.12 = (f32[2,4,16,128]{3,2,1,0:T(8,128)S(1)}, f32[2,4,16,128]{3,2,1,0:T(8,128)S(1)}, u32[]{:S(2)}, u32[]{:S(2)}) collective-permute-start(f32[2,4,16,128]{3,2,1,0:T(8,128)S(1)} %get-tuple-element.29), channel_id=1, source_target_pairs={{0,16},{8,24},{16,0},{24,8},{1,17},{9,25},{17,1},{25,9},{2,18},{10... | collective-permute-start | bytes 196616 | tf_op jit(solution)/shard_map/ppermute | solution.py:633
  28.2 2.8 %collective-permute-start.17 = (f32[2,4,16,128]{3,2,1,0:T(8,128)S(1)}, f32[2,4,16,128]{3,2,1,0:T(8,128)S(1)}, u32[]{:S(2)}, u32[]{:S(2)}) collective-permute-start(f32[2,4,16,128]{3,2,1,0:T(8,128)S(1)} %collective-permute-done.14.rest_2_), channel_id=1, source_target_pairs={{0,8},{8,0},{16,24},{24,16},{1,9},{9,1},{17,25},{25,17},{2,10},{10... | collective-permute-start | bytes 196616 | tf_op jit(solution)/shard_map/ppermute | solution.py:564
  29.8 1.3 %collective-permute-start.16 = (f32[2,4,16,128]{3,2,1,0:T(8,128)S(1)}, f32[2,4,16,128]{3,2,1,0:T(8,128)S(1)}, u32[]{:S(2)}, u32[]{:S(2)}) collective-permute-start(f32[2,4,16,128]{3,2,1,0:T(8,128)S(1)} %collective-permute-done.13.rest_1_), channel_id=1, source_target_pairs={{0,8},{8,0},{16,24},{24,16},{1,9},{9,1},{17,25},{25,17},{2,10},{10... | collective-permute-start | bytes 196616 | tf_op jit(solution)/shard_map/ppermute | solution.py:564
  31.0 1.3 %collective-permute-start.15 = (f32[2,4,16,128]{3,2,1,0:T(8,128)S(1)}, f32[2,4,16,128]{3,2,1,0:T(8,128)S(1)}, u32[]{:S(2)}, u32[]{:S(2)}) collective-permute-start(f32[2,4,16,128]{3,2,1,0:T(8,128)S(1)} %collective-permute-done.12.rest_0_), channel_id=1, source_target_pairs={{0,8},{8,0},{16,24},{24,16},{1,9},{9,1},{17,25},{25,17},{2,10},{10... | collective-permute-start | bytes 196616 | tf_op jit(solution)/shard_map/ppermute | solution.py:564

commit v6 on v5

--- a/solution.py
+++ b/solution.py
@@ -59,10 +59,10 @@
         )
 
     def span(self, margin):
-        first = (self.side - margin) // 8 * 8
-        last = round_up(self.side + self.rows + margin, 8)
-        assert first >= 0 and last <= self.height
-        return first, last
+        size = round_up(self.rows + 2 * margin, 8)
+        first = self.side - (size - self.rows) // 2
+        assert first >= 0 and first % 2 == 0
+        return first, first + size
 
 
 CHUNK = 16
@@ -351,7 +351,7 @@
                 misfit = (given + total) + inner * centre
                 sums[i] = misfit if sums[i] is None else sums[i] + misfit
         for i in range(box.tiles):
-            pairs[i, plane + 2, pl.ds(PAD + at, size), :] = pair_columns(sums[i])
+            pairs[i, plane + 2, pl.ds(PAD + at, size), :] = sums[i]
 
     first, last = box.span(margin + 4)
     clear_edges(pairs, first, last)
@@ -359,7 +359,7 @@
 
     def first_guess(plane, at, size, cache):
         for i in range(box.tiles):
-            mean = 0.125 * pair_rows(pairs, i, plane, at, size)
+            mean = 0.125 * pair_columns(pair_rows(pairs, i, plane, at, size))
             residual[i, plane + 2, pl.ds(PAD + at, size), :] = mean
             guess[i, plane + 2, pl.ds(PAD + at, size), :] = (
                 coarse[CENTRE, i, plane, pl.ds(at, size), :] * mean

time: 35.9 us -> 34 us (0.947)
  Pallas kernels: 7.59 us -> 5.77 us
    pallas_call x5, Pallas kernels: 7.59 us -> 5.77 us  [run(): pl.pallas_call(body, out_shape=[jax.ShapeDtypeStruct(shape, jnp.float32)...]
  transfers between devices with their start and end apart: 18 -> 18, of which waited for: 8 -> 9; matrix products, arithmetic and copies ran while one was open for 0% -> 0% of each run, Pallas kernels for 3% -> 3%
where the time goes in v6:
time: 34 us; the launch traced here: 33.9 us
  starting transfers between devices  16.1 us (47%)
  waiting for transfers between devices  10.9 us (32%)
  Pallas kernels  5.77 us (17%)
  other arithmetic  1.06 us (3%)
    ppermute x3, starting transfers between devices, row_pieces(): got_one = lax.ppermute(send_one, both, rounds[0])  8.22 us
    pallas_call x5, Pallas kernels, run(): pl.pallas_call(body, out_shape=[jax.ShapeDtypeStruct(shape, jnp.float32)...  5.77 us
    ppermute x3, waiting for transfers between devices, row_pieces(): got_one = lax.ppermute(send_one, both, rounds[0])  4.89 us
    ppermute x10, waiting for transfers between devices, core_swapped(): return lax.ppermute(block, 'tm', [(i, i ^ 1) for i in range(count)])  3.04 us
    ppermute x1, starting transfers between devices, slab_blocks(): return [block, lax.ppermute(block, 'slab', [(0, 1), (1, 0)])]  3.04 us
    ppermute x3, starting transfers between devices, row_pieces(): got_two = lax.ppermute(send_two, both, rounds[1])  2.09 us
    ppermute x1, waiting for transfers between devices, slab_blocks(): return [block, lax.ppermute(block, 'slab', [(0, 1), (1, 0)])]  1.74 us
    ppermute x1, starting transfers between devices, per_device(): centre = lax.ppermute(leaving, 'tm', [(t, hop(t)) for t in range(windows)])  1.52 us
  transfers between devices with their start and end apart: 18, of which 9 were waited for; matrix products, arithmetic and copies ran while one was open for 0% of the time, Pallas kernels for 3%

profile of v6, /device:TPU:0, one launch (start us, length us, event | category | flops | bytes accessed | tf_op | source)
XLA Modules:
  0.0 33.9 jit_solution(2078387637266478813)
XLA Ops:
  0.0 1.1 %select_select_fusion.refs_0_ = f32[3,4,16,256]{3,2,1,0:T(8,128)S(1)} fusion(f32[3,4,16,256]{3,2,1,0:T(8,128)} %param.5, f32[4,16,256]{2,1,0:T(8,128)} %bitcast.1, f32[4,16,256]{2,1,0:T(8,128)} %param.4, pred[3]{0:T(512)(128)(4,1)S(1)} %get-tuple-element.32, pred[3]{0:T(512)(128)(4,1)S(1)} %get-tuple-element.31), kind=kLoop, calls=%fused_computation | loop fusion | flops 98304 | bytes 524294 | tf_op jit(solution)/shard_map/jit(_where)/select_n | solution.py:578
  1.1 3.0 %collective-permute-start = (f32[3,4,16,256]{3,2,1,0:T(8,128)S(1)}, f32[3,4,16,256]{3,2,1,0:T(8,128)S(1)}, u32[]{:S(2)}, u32[]{:S(2)}) collective-permute-start(f32[3,4,16,256]{3,2,1,0:T(8,128)S(1)} %select_select_fusion.refs_0_), channel_id=1, source_target_pairs={{0,4},{4,0},{1,5},{5,1},{2,6},{6,2},{3,7},{7,3},{8,12},{12,8},{9,1... | collective-permute-start | bytes 589832 | tf_op jit(solution)/shard_map/ppermute | solution.py:516
  4.1 0.0 collective-permute-start.7
  4.1 0.5 %collective-permute-start.6 = (f32[3,4,16,256]{3,2,1,0:T(8,128)S(1)}, f32[3,4,16,256]{3,2,1,0:T(8,128)S(1)}, u32[]{:S(2)}, u32[]{:S(2)}) collective-permute-start(f32[3,4,16,256]{3,2,1,0:T(8,128)S(1)} %select_select_fusion.refs_0_), channel_id=1, source_target_pairs={{0,8},{8,0},{16,24},{24,16},{1,2},{9,10},{17,18},{25,26},{2,1},{10... | collective-permute-start | bytes 589832 | tf_op jit(solution)/shard_map/ppermute | solution.py:553
  4.6 2.6 %collective-permute-start.5 = (f32[3,4,16,256]{3,2,1,0:T(8,128)S(1)}, f32[3,4,16,256]{3,2,1,0:T(8,128)S(1)}, u32[]{:S(2)}, u32[]{:S(2)}) collective-permute-start(f32[3,4,16,256]{3,2,1,0:T(8,128)S(1)} %select_select_fusion.refs_0_), channel_id=1, source_target_pairs={{0,1},{8,9},{16,17},{24,25},{1,0},{9,8},{17,16},{25,24},{2,3},{10,... | collective-permute-start | bytes 589832 | tf_op jit(solution)/shard_map/ppermute | solution.py:552
  7.3 1.7 %collective-permute-done.refs_1_ = f32[3,4,16,256]{3,2,1,0:T(8,128)S(1)} collective-permute-done((f32[3,4,16,256]{3,2,1,0:T(8,128)S(1)}, f32[3,4,16,256]{3,2,1,0:T(8,128)S(1)}, u32[]{:S(2)}, u32[]{:S(2)}) %collective-permute-start) | collective-permute-done | bytes 196640 | tf_op jit(solution)/shard_map/ppermute | solution.py:516
  9.0 0.0 collective-permute-start.2
  9.0 3.4 %collective-permute-start.1 = (f32[3,4,16,256]{3,2,1,0:T(8,128)S(1)}, f32[3,4,16,256]{3,2,1,0:T(8,128)S(1)}, u32[]{:S(2)}, u32[]{:S(2)}) collective-permute-start(f32[3,4,16,256]{3,2,1,0:T(8,128)S(1)} %collective-permute-done.refs_1_), channel_id=1, source_target_pairs={{0,1},{8,9},{16,17},{24,25},{1,0},{9,8},{17,16},{25,24},{2,3},{10,... | collective-permute-start | bytes 589832 | tf_op jit(solution)/shard_map/ppermute | solution.py:552
  12.4 0.5 %collective-permute-start.10 = (f32[3,4,16,256]{3,2,1,0:T(8,128)S(1)}, f32[3,4,16,256]{3,2,1,0:T(8,128)S(1)}, u32[]{:S(2)}, u32[]{:S(2)}) collective-permute-start(f32[3,4,16,256]{3,2,1,0:T(8,128)S(1)} %collective-permute-done.6.refs_3_), channel_id=1, source_target_pairs={{0,8},{8,0},{16,24},{24,16},{1,9},{9,1},{17,25},{25,17},{2,10},{10... | collective-permute-start | bytes 589832 | tf_op jit(solution)/shard_map/ppermute | solution.py:564
  12.9 0.1 collective-permute-done.5.refs_2_
  13.0 0.0 collective-permute-start.9
  13.0 0.0 collective-permute-done.2.refs_1_
  13.0 0.5 %collective-permute-start.4 = (f32[3,4,16,256]{3,2,1,0:T(8,128)S(1)}, f32[3,4,16,256]{3,2,1,0:T(8,128)S(1)}, u32[]{:S(2)}, u32[]{:S(2)}) collective-permute-start(f32[3,4,16,256]{3,2,1,0:T(8,128)S(1)} %collective-permute-done.2.refs_1_), channel_id=1, source_target_pairs={{0,8},{8,0},{16,24},{24,16},{1,9},{9,1},{17,25},{25,17},{2,10},{10... | collective-permute-start | bytes 589832 | tf_op jit(solution)/shard_map/ppermute | solution.py:564
  13.5 3.3 %collective-permute-done.1.refs_0_ = f32[3,4,16,256]{3,2,1,0:T(8,128)S(1)} collective-permute-done((f32[3,4,16,256]{3,2,1,0:T(8,128)S(1)}, f32[3,4,16,256]{3,2,1,0:T(8,128)S(1)}, u32[]{:S(2)}, u32[]{:S(2)}) %collective-permute-start.1) | collective-permute-done | bytes 196640 | tf_op jit(solution)/shard_map/ppermute | solution.py:552
  16.8 0.0 collective-permute-done.8.refs_5_
  16.8 0.4 %shard_map.37 = (f32[2,2,8,48,128]{4,3,2,1,0:T(8,128)S(1)}, f32[4,2,8,48,128]{4,3,2,1,0:T(8,128)S(1)}, f32[7,2,8,48,128]{4,3,2,1,0:T(8,128)S(1)}) custom-call(f32[3,4,16,256]{3,2,1,0:T(8,128)S(1)} %select_select_fusion.refs_0_, f32[3,4,16,256]{3,2,1,0:T(8,128)S(1)} %collective-permute-done.refs_1_, f32[3,4,16,256]{3,2,1,0:T(8,128)S(1)} %collective-permute-done.5.refs_2_, ...), custom_call_target="tpu_custom_call" | custom-call | tf_op jit(solution)/shard_map/pallas_call | solution.py:500
  17.2 1.0 %collective-permute-done.3.refs_2_ = f32[3,4,16,256]{3,2,1,0:T(8,128)S(1)} collective-permute-done((f32[3,4,16,256]{3,2,1,0:T(8,128)S(1)}, f32[3,4,16,256]{3,2,1,0:T(8,128)S(1)}, u32[]{:S(2)}, u32[]{:S(2)}) %collective-permute-start.3) | collective-permute-done | bytes 196640 | tf_op jit(solution)/shard_map/ppermute | solution.py:564
  18.2 1.7 %shard_map.38 = (f32[2,8,32,128]{3,2,1,0:T(8,128)S(1)}, f32[2,2,8,48,128]{4,3,2,1,0:T(8,128)S(1)}, f32[4,2,8,48,128]{4,3,2,1,0:T(8,128)S(1)}, f32[7,2,8,48,128]{4,3,2,1,0:T(8,128)S(1)}) custom-call(f32[3,4,16,256]{3,2,1,0:T(8,128)S(1)} %collective-permute-done.1.refs_0_, ...), custom_call_target="tpu_custom_call", output_to_operand_aliasing={{1}: (4, {}), {2}: (5, {}), {3}: (6, {})} | custom-call | tf_op jit(solution)/shard_map/pallas_call | solution.py:500
  19.9 0.2 collective-permute-start.11
  20.1 0.6 %shard_map.39 = (f32[7,2,4,48,128]{4,3,2,1,0:T(8,128)S(1)}, f32[2,8,48,128]{3,2,1,0:T(8,128)S(1)}) custom-call(f32[4,2,8,48,128]{4,3,2,1,0:T(8,128)S(1)} %get-tuple-element.24.coeff), custom_call_target="tpu_custom_call" | custom-call | tf_op jit(solution)/shard_map/pallas_call | solution.py:500
  20.8 0.7 %collective-permute-done.11.other_end = f32[2,8,32,128]{3,2,1,0:T(8,128)S(1)} collective-permute-done((f32[2,8,32,128]{3,2,1,0:T(8,128)S(1)}, f32[2,8,32,128]{3,2,1,0:T(8,128)S(1)}, u32[]{:S(2)}, u32[]{:S(2)}) %collective-permute-start.11) | collective-permute-done | bytes 262176 | tf_op jit(solution)/shard_map/ppermute | solution.py:564
  21.5 0.8 %shard_map.40 = (f32[2,8,16,128]{3,2,1,0:T(8,128)S(1)}, f32[2,8,16,128]{3,2,1,0:T(8,128)S(1)}, f32[2,4,16,128]{3,2,1,0:T(8,128)S(1)}) custom-call(f32[2,8,32,128]{3,2,1,0:T(8,128)S(1)} %get-tuple-element.21.own_end, f32[2,8,32,128]{3,2,1,0:T(8,128)S(1)} %collective-permute-done.11.other_end, f32[2,2,8,48,128]{4,3,2,1,0:T(8,128)S(1)} %get-tuple-element.22.starts.rest_6_, ...), custom_call_target="tpu_custom_call" | custom-call | tf_op jit(solution)/shard_map/pallas_call | solution.py:500
  22.3 1.6 %collective-permute-start.14 = (f32[2,4,16,128]{3,2,1,0:T(8,128)S(1)}, f32[2,4,16,128]{3,2,1,0:T(8,128)S(1)}, u32[]{:S(2)}, u32[]{:S(2)}) collective-permute-start(f32[2,4,16,128]{3,2,1,0:T(8,128)S(1)} %get-tuple-element.29), channel_id=1, source_target_pairs={{0,16},{8,24},{16,0},{24,8},{1,18},{9,26},{17,2},{25,10},{2,17},{1... | collective-permute-start | bytes 196616 | tf_op jit(solution)/shard_map/ppermute | solution.py:553
  23.9 2.2 %collective-permute-start.13 = (f32[2,4,16,128]{3,2,1,0:T(8,128)S(1)}, f32[2,4,16,128]{3,2,1,0:T(8,128)S(1)}, u32[]{:S(2)}, u32[]{:S(2)}) collective-permute-start(f32[2,4,16,128]{3,2,1,0:T(8,128)S(1)} %get-tuple-element.29), channel_id=1, source_target_pairs={{0,17},{8,25},{16,1},{24,9},{1,16},{9,24},{17,0},{25,8},{2,19},{10... | collective-permute-start | bytes 196616 | tf_op jit(solution)/shard_map/ppermute | solution.py:552
  26.1 1.5 %collective-permute-start.12 = (f32[2,4,16,128]{3,2,1,0:T(8,128)S(1)}, f32[2,4,16,128]{3,2,1,0:T(8,128)S(1)}, u32[]{:S(2)}, u32[]{:S(2)}) collective-permute-start(f32[2,4,16,128]{3,2,1,0:T(8,128)S(1)} %get-tuple-element.29), channel_id=1, source_target_pairs={{0,16},{8,24},{16,0},{24,8},{1,17},{9,25},{17,1},{25,9},{2,18},{10... | collective-permute-start | bytes 196616 | tf_op jit(solution)/shard_map/ppermute | solution.py:633
  27.6 0.0 collective-permute-done.14.rest_2_
  27.6 0.0 collective-permute-start.17
  27.6 1.6 %collective-permute-done.13.rest_1_ = f32[2,4,16,128]{3,2,1,0:T(8,128)S(1)} collective-permute-done((f32[2,4,16,128]{3,2,1,0:T(8,128)S(1)}, f32[2,4,16,128]{3,2,1,0:T(8,128)S(1)}, u32[]{:S(2)}, u32[]{:S(2)}) %collective-permute-start.13) | collective-permute-done | bytes 65568 | tf_op jit(solution)/shard_map/ppermute | solution.py:552
  29.2 1.2 %collective-permute-done.12.rest_0_ = f32[2,4,16,128]{3,2,1,0:T(8,128)S(1)} collective-permute-done((f32[2,4,16,128]{3,2,1,0:T(8,128)S(1)}, f32[2,4,16,128]{3,2,1,0:T(8,128)S(1)}, u32[]{:S(2)}, u32[]{:S(2)}) %collective-permute-start.12) | collective-permute-done | bytes 65568 | tf_op jit(solution)/shard_map/ppermute | solution.py:633
  30.4 0.1 collective-permute-done.16.rest_4_
  30.4 1.2 %collective-permute-done.15.rest_3_ = f32[2,4,16,128]{3,2,1,0:T(8,128)S(1)} collective-permute-done((f32[2,4,16,128]{3,2,1,0:T(8,128)S(1)}, f32[2,4,16,128]{3,2,1,0:T(8,128)S(1)}, u32[]{:S(2)}, u32[]{:S(2)}) %collective-permute-start.15) | collective-permute-done | bytes 65568 | tf_op jit(solution)/shard_map/ppermute | solution.py:564
  31.6 2.3 %shard_map.41 = (f32[1,4,16,256]{3,2,1,0:T(8,128)}, f32[2,4,16,128]{3,2,1,0:T(8,128)}) custom-call(f32[2,8,16,128]{3,2,1,0:T(8,128)S(1)} %get-tuple-element.27.first_end, f32[2,8,16,128]{3,2,1,0:T(8,128)S(1)} %get-tuple-element.28.joined, f32[2,4,16,128]{3,2,1,0:T(8,128)S(1)} %collective-permute-done.12.rest_0_, ...), custom_call_target="tpu_custom_call" | custom-call | tf_op jit(solution)/shard_map/pallas_call | solution.py:500
  (11 shorter events, 0.0 us)
Async XLA Ops:
  1.1 7.9 %collective-permute-start = (f32[3,4,16,256]{3,2,1,0:T(8,128)S(1)}, f32[3,4,16,256]{3,2,1,0:T(8,128)S(1)}, u32[]{:S(2)}, u32[]{:S(2)}) collective-permute-start(f32[3,4,16,256]{3,2,1,0:T(8,128)S(1)} %select_select_fusion.refs_0_), channel_id=1, source_target_pairs={{0,4},{4,0},{1,5},{5,1},{2,6},{6,2},{3,7},{7,3},{8,12},{12,8},{9,1... | collective-permute-start | bytes 589832 | tf_op jit(solution)/shard_map/ppermute | solution.py:516
  4.1 8.3 %collective-permute-start.7 = (f32[3,4,16,256]{3,2,1,0:T(8,128)S(1)}, f32[3,4,16,256]{3,2,1,0:T(8,128)S(1)}, u32[]{:S(2)}, u32[]{:S(2)}) collective-permute-start(f32[3,4,16,256]{3,2,1,0:T(8,128)S(1)} %select_select_fusion.refs_0_), channel_id=1, source_target_pairs={{0,8},{8,0},{16,24},{24,16},{1,9},{9,1},{17,25},{25,17},{2,10},{10... | collective-permute-start | bytes 589832 | tf_op jit(solution)/shard_map/ppermute | solution.py:564
  4.1 8.3 %collective-permute-start.6 = (f32[3,4,16,256]{3,2,1,0:T(8,128)S(1)}, f32[3,4,16,256]{3,2,1,0:T(8,128)S(1)}, u32[]{:S(2)}, u32[]{:S(2)}) collective-permute-start(f32[3,4,16,256]{3,2,1,0:T(8,128)S(1)} %select_select_fusion.refs_0_), channel_id=1, source_target_pairs={{0,8},{8,0},{16,24},{24,16},{1,2},{9,10},{17,18},{25,26},{2,1},{10... | collective-permute-start | bytes 589832 | tf_op jit(solution)/shard_map/ppermute | solution.py:553
  4.6 8.4 %collective-permute-start.5 = (f32[3,4,16,256]{3,2,1,0:T(8,128)S(1)}, f32[3,4,16,256]{3,2,1,0:T(8,128)S(1)}, u32[]{:S(2)}, u32[]{:S(2)}) collective-permute-start(f32[3,4,16,256]{3,2,1,0:T(8,128)S(1)} %select_select_fusion.refs_0_), channel_id=1, source_target_pairs={{0,1},{8,9},{16,17},{24,25},{1,0},{9,8},{17,16},{25,24},{2,3},{10,... | collective-permute-start | bytes 589832 | tf_op jit(solution)/shard_map/ppermute | solution.py:552
  9.0 4.0 %collective-permute-start.2 = (f32[3,4,16,256]{3,2,1,0:T(8,128)S(1)}, f32[3,4,16,256]{3,2,1,0:T(8,128)S(1)}, u32[]{:S(2)}, u32[]{:S(2)}) collective-permute-start(f32[3,4,16,256]{3,2,1,0:T(8,128)S(1)} %collective-permute-done.refs_1_), channel_id=1, source_target_pairs={{0,8},{8,0},{16,24},{24,16},{1,2},{9,10},{17,18},{25,26},{2,1},{10... | collective-permute-start | bytes 589832 | tf_op jit(solution)/shard_map/ppermute | solution.py:553
  9.0 7.8 %collective-permute-start.1 = (f32[3,4,16,256]{3,2,1,0:T(8,128)S(1)}, f32[3,4,16,256]{3,2,1,0:T(8,128)S(1)}, u32[]{:S(2)}, u32[]{:S(2)}) collective-permute-start(f32[3,4,16,256]{3,2,1,0:T(8,128)S(1)} %collective-permute-done.refs_1_), channel_id=1, source_target_pairs={{0,1},{8,9},{16,17},{24,25},{1,0},{9,8},{17,16},{25,24},{2,3},{10,... | collective-permute-start | bytes 589832 | tf_op jit(solution)/shard_map/ppermute | solution.py:552
  12.4 4.4 %collective-permute-start.8 = (f32[3,4,16,256]{3,2,1,0:T(8,128)S(1)}, f32[3,4,16,256]{3,2,1,0:T(8,128)S(1)}, u32[]{:S(2)}, u32[]{:S(2)}) collective-permute-start(f32[3,4,16,256]{3,2,1,0:T(8,128)S(1)} %collective-permute-done.refs_1_), channel_id=1, source_target_pairs={{0,8},{8,0},{16,24},{24,16},{1,9},{9,1},{17,25},{25,17},{2,10},{10... | collective-permute-start | bytes 589832 | tf_op jit(solution)/shard_map/ppermute | solution.py:564
  12.4 4.4 %collective-permute-start.10 = (f32[3,4,16,256]{3,2,1,0:T(8,128)S(1)}, f32[3,4,16,256]{3,2,1,0:T(8,128)S(1)}, u32[]{:S(2)}, u32[]{:S(2)}) collective-permute-start(f32[3,4,16,256]{3,2,1,0:T(8,128)S(1)} %collective-permute-done.6.refs_3_), channel_id=1, source_target_pairs={{0,8},{8,0},{16,24},{24,16},{1,9},{9,1},{17,25},{25,17},{2,10},{10... | collective-permute-start | bytes 589832 | tf_op jit(solution)/shard_map/ppermute | solution.py:564
  13.0 3.8 %collective-permute-start.9 = (f32[3,4,16,256]{3,2,1,0:T(8,128)S(1)}, f32[3,4,16,256]{3,2,1,0:T(8,128)S(1)}, u32[]{:S(2)}, u32[]{:S(2)}) collective-permute-start(f32[3,4,16,256]{3,2,1,0:T(8,128)S(1)} %collective-permute-done.5.refs_2_), channel_id=1, source_target_pairs={{0,8},{8,0},{16,24},{24,16},{1,9},{9,1},{17,25},{25,17},{2,10},{10... | collective-permute-start | bytes 589832 | tf_op jit(solution)/shard_map/ppermute | solution.py:564
  13.0 4.2 %collective-permute-start.4 = (f32[3,4,16,256]{3,2,1,0:T(8,128)S(1)}, f32[3,4,16,256]{3,2,1,0:T(8,128)S(1)}, u32[]{:S(2)}, u32[]{:S(2)}) collective-permute-start(f32[3,4,16,256]{3,2,1,0:T(8,128)S(1)} %collective-permute-done.2.refs_1_), channel_id=1, source_target_pairs={{0,8},{8,0},{16,24},{24,16},{1,9},{9,1},{17,25},{25,17},{2,10},{10... | collective-permute-start | bytes 589832 | tf_op jit(solution)/shard_map/ppermute | solution.py:564
  16.8 1.4 %collective-permute-start.3 = (f32[3,4,16,256]{3,2,1,0:T(8,128)S(1)}, f32[3,4,16,256]{3,2,1,0:T(8,128)S(1)}, u32[]{:S(2)}, u32[]{:S(2)}) collective-permute-start(f32[3,4,16,256]{3,2,1,0:T(8,128)S(1)} %collective-permute-done.1.refs_0_), channel_id=1, source_target_pairs={{0,8},{8,0},{16,24},{24,16},{1,9},{9,1},{17,25},{25,17},{2,10},{10... | collective-permute-start | bytes 589832 | tf_op jit(solution)/shard_map/ppermute | solution.py:564
  19.9 1.6 %collective-permute-start.11 = (f32[2,8,32,128]{3,2,1,0:T(8,128)S(1)}, f32[2,8,32,128]{3,2,1,0:T(8,128)S(1)}, u32[]{:S(2)}, u32[]{:S(2)}) collective-permute-start(f32[2,8,32,128]{3,2,1,0:T(8,128)S(1)} %get-tuple-element.21.own_end), channel_id=1, source_target_pairs={{0,8},{8,0},{16,24},{24,16},{1,9},{9,1},{17,25},{25,17},{2,10},{10... | collective-permute-start | bytes 786440 | tf_op jit(solution)/shard_map/ppermute | solution.py:564
  22.3 5.3 %collective-permute-start.14 = (f32[2,4,16,128]{3,2,1,0:T(8,128)S(1)}, f32[2,4,16,128]{3,2,1,0:T(8,128)S(1)}, u32[]{:S(2)}, u32[]{:S(2)}) collective-permute-start(f32[2,4,16,128]{3,2,1,0:T(8,128)S(1)} %get-tuple-element.29), channel_id=1, source_target_pairs={{0,16},{8,24},{16,0},{24,8},{1,18},{9,26},{17,2},{25,10},{2,17},{1... | collective-permute-start | bytes 196616 | tf_op jit(solution)/shard_map/ppermute | solution.py:553
  23.9 5.3 %collective-permute-start.13 = (f32[2,4,16,128]{3,2,1,0:T(8,128)S(1)}, f32[2,4,16,128]{3,2,1,0:T(8,128)S(1)}, u32[]{:S(2)}, u32[]{:S(2)}) collective-permute-start(f32[2,4,16,128]{3,2,1,0:T(8,128)S(1)} %get-tuple-element.29), channel_id=1, source_target_pairs={{0,17},{8,25},{16,1},{24,9},{1,16},{9,24},{17,0},{25,8},{2,19},{10... | collective-permute-start | bytes 196616 | tf_op jit(solution)/shard_map/ppermute | solution.py:552
  26.1 4.3 %collective-permute-start.12 = (f32[2,4,16,128]{3,2,1,0:T(8,128)S(1)}, f32[2,4,16,128]{3,2,1,0:T(8,128)S(1)}, u32[]{:S(2)}, u32[]{:S(2)}) collective-permute-start(f32[2,4,16,128]{3,2,1,0:T(8,128)S(1)} %get-tuple-element.29), channel_id=1, source_target_pairs={{0,16},{8,24},{16,0},{24,8},{1,17},{9,25},{17,1},{25,9},{2,18},{10... | collective-permute-start | bytes 196616 | tf_op jit(solution)/shard_map/ppermute | solution.py:633
  27.6 2.8 %collective-permute-start.17 = (f32[2,4,16,128]{3,2,1,0:T(8,128)S(1)}, f32[2,4,16,128]{3,2,1,0:T(8,128)S(1)}, u32[]{:S(2)}, u32[]{:S(2)}) collective-permute-start(f32[2,4,16,128]{3,2,1,0:T(8,128)S(1)} %collective-permute-done.14.rest_2_), channel_id=1, source_target_pairs={{0,8},{8,0},{16,24},{24,16},{1,9},{9,1},{17,25},{25,17},{2,10},{10... | collective-permute-start | bytes 196616 | tf_op jit(solution)/shard_map/ppermute | solution.py:564
  29.2 1.3 %collective-permute-start.16 = (f32[2,4,16,128]{3,2,1,0:T(8,128)S(1)}, f32[2,4,16,128]{3,2,1,0:T(8,128)S(1)}, u32[]{:S(2)}, u32[]{:S(2)}) collective-permute-start(f32[2,4,16,128]{3,2,1,0:T(8,128)S(1)} %collective-permute-done.13.rest_1_), channel_id=1, source_target_pairs={{0,8},{8,0},{16,24},{24,16},{1,9},{9,1},{17,25},{25,17},{2,10},{10... | collective-permute-start | bytes 196616 | tf_op jit(solution)/shard_map/ppermute | solution.py:564
  30.4 1.3 %collective-permute-start.15 = (f32[2,4,16,128]{3,2,1,0:T(8,128)S(1)}, f32[2,4,16,128]{3,2,1,0:T(8,128)S(1)}, u32[]{:S(2)}, u32[]{:S(2)}) collective-permute-start(f32[2,4,16,128]{3,2,1,0:T(8,128)S(1)} %collective-permute-done.12.rest_0_), channel_id=1, source_target_pairs={{0,8},{8,0},{16,24},{24,16},{1,9},{9,1},{17,25},{25,17},{2,10},{10... | collective-permute-start | bytes 196616 | tf_op jit(solution)/shard_map/ppermute | solution.py:564

commit v7 on v6

--- a/solution.py
+++ b/solution.py
@@ -395,8 +395,8 @@
 
 
 def pair_body(box, own_end, other_end, starts, *rest):
-    params, out, first_out, leaving = rest[:3], rest[3], rest[4], rest[5]
-    source, trial, pairs, guess, residual = rest[6:]
+    params, out, first_out, leaving = rest[:3], rest[3], rest[4], rest[5:7]
+    source, trial, pairs, guess, residual = rest[7:]
     core = lax.axis_index("tm") % 2
     first, last = box.span(COARSE_REACH)
     clear_edges(source, first, last)
@@ -422,23 +422,34 @@
         out[where] = value + out[where]
 
     coarse_step_body(box, 0, source, trial, pairs, guess, residual, params, finish)
+    pack(box, out, *leaving)
+
+
+def pack(box, field, centre, edge):
+    core, place = lax.axis_index("tm") % 2, lax.axis_index("coarse")
     half = box.depth // 2
-    leaving[...] = out[:, pl.ds(core * half, half)]
-
-
-def last_body(box, own_depth, turn, pieces, first_end, joined, *rest):
-    arrived, rest = rest[:pieces], rest[pieces:]
-    starts, params, result, leaving = rest[0], rest[1:4], rest[4], rest[5]
-    source, second, trial, pairs, guess, residual, total = rest[6:]
+    centre[...] = field[:, pl.ds(core * half, half)]
+    width = edge.shape[1] // box.depth
+    up = place % 2 == core
+    for i in range(box.tiles):
+        for plane in range(box.depth):
+            edge[i, plane * width : (plane + 1) * width, :] = jnp.where(
+                up, field[i, plane, box.rows - width :, :], field[i, plane, :width, :]
+            )
+
+
+def last_body(box, own_depth, turn, first_end, joined, *rest):
+    arrived, rest = rest[:4], rest[4:]
+    starts, params, result, leaving = rest[0], rest[1:4], rest[4], rest[5:7]
+    source, second, trial, pairs, guess, residual, total = rest[7:]
     place = lax.axis_index("tm")
     core = place % 2
     active = place // 2 == turn
     side, rows = box.side, box.rows
     half = box.depth // 2
-    clear_edges(source, 0, box.height)
+    reach = 2 * COARSE_REACH
+    clear_edges(source, side - reach, side + rows + reach)
     clear_edges(second, *box.span(COARSE_REACH))
-    each = pieces // 2
-    places = row_places(box, [arrived[at].shape[-2] for at in range(1, each, 2)])
 
     @pl.when(jnp.logical_not(active))
     def _():
@@ -448,23 +459,37 @@
 
     @pl.when(active)
     def _():
-        for part, rank in ((0, core), (1, 1 - core)):
-            moves = [(arrived[part * each], side, None)]
-            for step, pair in enumerate(places):
-                at = part * each + 1 + 2 * step
-                for ref, (where, valid) in zip(arrived[at : at + 2], pair):
-                    moves.append((ref, where, valid))
+        centre, edge, other_centre, other_edge = arrived
+        for piece, rank in ((centre, core), (other_centre, 1 - core)):
             base = rank * half
-            for ref, at, valid in moves:
-                size = ref.shape[-2]
+            for i in range(box.tiles):
                 for plane in range(half):
-                    for i in range(box.tiles):
-                        value = ref[i, plane]
-                        if valid is not None:
-                            value = jnp.where(valid, value, 0.0)
-                        source[i, base + plane + 2, pl.ds(PAD + at, size), :] = (
-                            value - starts[0, i, base + plane, pl.ds(at, size), :]
+                    source[i, base + plane + 2, PAD + side : PAD + side + rows, :] = (
+                        piece[i, plane] - starts[0, i, base + plane, side : side + rows, :]
+                    )
+        width = edge.shape[1] // box.depth
+        row_place, count = lax.axis_index("coarse"), lax.axis_size("coarse")
+        below = row_place % 2 != core
+
+        def edges(low, high):
+            for ref, at, valid in (
+                (low, side - width, row_place > 0),
+                (high, side + rows, row_place < count - 1),
+            ):
+                for i in range(box.tiles):
+                    for plane in range(box.depth):
+                        value = ref[i, plane * width : (plane + 1) * width, :]
+                        source[i, plane + 2, PAD + at : PAD + at + width, :] = (
+                            jnp.where(valid, value, 0.0) - starts[0, i, plane, at : at + width, :]
                         )
+
+        @pl.when(below)
+        def _():
+            edges(edge, other_edge)
+
+        @pl.when(jnp.logical_not(below))
+        def _():
+            edges(other_edge, edge)
 
     def finish_once(plane, i, at, size, value):
         second[i, plane + 2, pl.ds(PAD + at, size), :] = value
@@ -493,7 +518,7 @@
         for i in range(box.tiles):
             result[0, :, :, i * LANES : (i + 1) * LANES] = total[i, pl.ds(base, own_depth)]
 
-    leaving[...] = total[:, pl.ds(core * half, half)]
+    pack(box, total, *leaving)
 
 
 def run(body, outs, scratch, *args, aliases={}):
@@ -614,9 +639,12 @@
         coeff,
     )
     params = [weights, *params]
-    joined, first_end, leaving = run(
+    width = 2 * COARSE_REACH
+    assert rows >= width
+    leaving_shapes = [(tiles, half, rows, LANES), (tiles, depth * width, LANES)]
+    joined, first_end, *leaving = run(
         functools.partial(pair_body, box),
-        [(tiles, depth, rows, LANES)] * 2 + [(tiles, half, rows, LANES)],
+        [(tiles, depth, rows, LANES)] * 2 + leaving_shapes,
         [box.scratch()] + coarse_scratch(box),
         end,
         core_swapped(end),
@@ -628,18 +656,21 @@
     base = lax.axis_index("slab") * own_depth
     result = lax.dynamic_slice_in_dim(ends, base, own_depth, 0)[None]
     hop = lambda t: (t + 2) % windows
-    rounds = row_swaps(hop, hop)
+    one, two = row_swaps(hop, hop)
+    across = [(t, hop(t)) for t in range(windows)]
+    count = lax.axis_size("coarse")
+    aside = [
+        pair for pairs, core in ((one, 0), (two, 1)) for pair in pairs if pair[0] // count % 2 == core
+    ]
     for turn in range(1, windows // 2):
-        centre = lax.ppermute(leaving, "tm", [(t, hop(t)) for t in range(windows)])
-        if rows >= 2 * COARSE_REACH:
-            arrived = [centre, *row_pieces(leaving, min(rows, side), rounds)]
-        else:
-            near = row_swaps(lambda t: t, lambda t: t ^ 1)
-            arrived = [centre, *row_pieces(centre, side, near)]
+        arrived = [
+            lax.ppermute(leaving[0], "tm", across),
+            lax.ppermute(leaving[1], ("tm", "coarse"), aside),
+        ]
         arrived += [core_swapped(piece) for piece in arrived]
-        out, leaving = run(
-            functools.partial(last_body, box, own_depth, turn, len(arrived)),
-            [(1, own_depth, rows, columns), (tiles, half, rows, LANES)],
+        out, *leaving = run(
+            functools.partial(last_body, box, own_depth, turn),
+            [(1, own_depth, rows, columns)] + leaving_shapes,
             [box.scratch()] * 2
             + coarse_scratch(box)
             + [pltpu.VMEM((tiles, depth, rows, LANES), jnp.float32)],

time: 34 us -> 33.1 us (0.974)
  starting transfers between devices: 16.1 us -> 14.1 us
  waiting for transfers between devices: 10.9 us -> 11.9 us
    ppermute x1 -> x2, waiting for transfers between devices: 1.19 us -> 3.75 us  [the longest x1 2.41 us: per_device(): lax.ppermute(leaving[1], ('tm', 'coarse'), aside)]
    ppermute x3 -> x2, starting transfers between devices: 8.22 us -> 6.04 us  [row_pieces(): got_one = lax.ppermute(send_one, both, rounds[0])]
    ppermute x1 -> x2, starting transfers between devices: 1.52 us -> 3.27 us  [the longest x1 2.77 us: per_device(): lax.ppermute(leaving[1], ('tm', 'coarse'), aside)]
    ppermute x3 -> x2, starting transfers between devices: 2.09 us -> 0.51 us  [row_pieces(): got_two = lax.ppermute(send_two, both, rounds[1])]
    ppermute x3 -> x2, waiting for transfers between devices: 4.89 us -> 3.32 us  [row_pieces(): got_one = lax.ppermute(send_one, both, rounds[0])]
    ppermute x10 -> x9, waiting for transfers between devices: 3.04 us -> 3.04 us  [core_swapped(): return lax.ppermute(block, 'tm', [(i, i ^ 1) for i in range(count)])]
    ppermute x10 -> x9, starting transfers between devices: 1.24 us -> 1.24 us  [core_swapped(): return lax.ppermute(block, 'tm', [(i, i ^ 1) for i in range(count)])]
  transfers between devices with their start and end apart: 18 -> 16, of which waited for: 9 -> 8; matrix products, arithmetic and copies ran while one was open for 0% -> 0% of each run, Pallas kernels for 3% -> 3%
where the time goes in v7:
time: 33.1 us; the launch traced here: 33 us
  starting transfers between devices  14.1 us (43%)
  waiting for transfers between devices  11.9 us (36%)
  Pallas kernels  5.86 us (18%)
  other arithmetic  1.06 us (3%)
    ppermute x2, starting transfers between devices, row_pieces(): got_one = lax.ppermute(send_one, both, rounds[0])  6.04 us
    pallas_call x5, Pallas kernels, run(): pl.pallas_call(body, out_shape=[jax.ShapeDtypeStruct(shape, jnp.float32)...  5.86 us
    ppermute x2, waiting for transfers between devices, row_pieces(): got_one = lax.ppermute(send_one, both, rounds[0])  3.32 us
    ppermute x9, waiting for transfers between devices, core_swapped(): return lax.ppermute(block, 'tm', [(i, i ^ 1) for i in range(count)])  3.04 us
    ppermute x1, starting transfers between devices, slab_blocks(): return [block, lax.ppermute(block, 'slab', [(0, 1), (1, 0)])]  3.04 us
    ppermute x1, starting transfers between devices, per_device(): lax.ppermute(leaving[1], ('tm', 'coarse'), aside)  2.77 us
    ppermute x1, waiting for transfers between devices, per_device(): lax.ppermute(leaving[1], ('tm', 'coarse'), aside)  2.41 us
    ppermute x1, waiting for transfers between devices, slab_blocks(): return [block, lax.ppermute(block, 'slab', [(0, 1), (1, 0)])]  1.74 us
  transfers between devices with their start and end apart: 16, of which 8 were waited for; matrix products, arithmetic and copies ran while one was open for 0% of the time, Pallas kernels for 3%

profile of v7, /device:TPU:0, one launch (start us, length us, event | category | flops | bytes accessed | tf_op | source)
XLA Modules:
  0.0 33.0 jit_solution(13836257782531768033)
XLA Ops:
  0.0 1.1 %select_select_fusion.refs_0_ = f32[3,4,16,256]{3,2,1,0:T(8,128)S(1)} fusion(f32[3,4,16,256]{3,2,1,0:T(8,128)} %param.5, f32[4,16,256]{2,1,0:T(8,128)} %bitcast.1, f32[4,16,256]{2,1,0:T(8,128)} %param.4, pred[3]{0:T(512)(128)(4,1)S(1)} %get-tuple-element.34, pred[3]{0:T(512)(128)(4,1)S(1)} %get-tuple-element.33), kind=kLoop, calls=%fused_computation | loop fusion | flops 98304 | bytes 524294 | tf_op jit(solution)/shard_map/jit(_where)/select_n | solution.py:603
  1.1 3.0 %collective-permute-start = (f32[3,4,16,256]{3,2,1,0:T(8,128)S(1)}, f32[3,4,16,256]{3,2,1,0:T(8,128)S(1)}, u32[]{:S(2)}, u32[]{:S(2)}) collective-permute-start(f32[3,4,16,256]{3,2,1,0:T(8,128)S(1)} %select_select_fusion.refs_0_), channel_id=1, source_target_pairs={{0,4},{4,0},{1,5},{5,1},{2,6},{6,2},{3,7},{7,3},{8,12},{12,8},{9,1... | collective-permute-start | bytes 589832 | tf_op jit(solution)/shard_map/ppermute | solution.py:541
  4.1 0.0 collective-permute-start.7
  4.1 0.5 %collective-permute-start.6 = (f32[3,4,16,256]{3,2,1,0:T(8,128)S(1)}, f32[3,4,16,256]{3,2,1,0:T(8,128)S(1)}, u32[]{:S(2)}, u32[]{:S(2)}) collective-permute-start(f32[3,4,16,256]{3,2,1,0:T(8,128)S(1)} %select_select_fusion.refs_0_), channel_id=1, source_target_pairs={{0,8},{8,0},{16,24},{24,16},{1,2},{9,10},{17,18},{25,26},{2,1},{10... | collective-permute-start | bytes 589832 | tf_op jit(solution)/shard_map/ppermute | solution.py:578
  4.6 2.6 %collective-permute-start.5 = (f32[3,4,16,256]{3,2,1,0:T(8,128)S(1)}, f32[3,4,16,256]{3,2,1,0:T(8,128)S(1)}, u32[]{:S(2)}, u32[]{:S(2)}) collective-permute-start(f32[3,4,16,256]{3,2,1,0:T(8,128)S(1)} %select_select_fusion.refs_0_), channel_id=1, source_target_pairs={{0,1},{8,9},{16,17},{24,25},{1,0},{9,8},{17,16},{25,24},{2,3},{10,... | collective-permute-start | bytes 589832 | tf_op jit(solution)/shard_map/ppermute | solution.py:577
  7.3 1.7 %collective-permute-done.refs_1_ = f32[3,4,16,256]{3,2,1,0:T(8,128)S(1)} collective-permute-done((f32[3,4,16,256]{3,2,1,0:T(8,128)S(1)}, f32[3,4,16,256]{3,2,1,0:T(8,128)S(1)}, u32[]{:S(2)}, u32[]{:S(2)}) %collective-permute-start) | collective-permute-done | bytes 196640 | tf_op jit(solution)/shard_map/ppermute | solution.py:541
  9.0 0.0 collective-permute-start.2
  9.0 3.4 %collective-permute-start.1 = (f32[3,4,16,256]{3,2,1,0:T(8,128)S(1)}, f32[3,4,16,256]{3,2,1,0:T(8,128)S(1)}, u32[]{:S(2)}, u32[]{:S(2)}) collective-permute-start(f32[3,4,16,256]{3,2,1,0:T(8,128)S(1)} %collective-permute-done.refs_1_), channel_id=1, source_target_pairs={{0,1},{8,9},{16,17},{24,25},{1,0},{9,8},{17,16},{25,24},{2,3},{10,... | collective-permute-start | bytes 589832 | tf_op jit(solution)/shard_map/ppermute | solution.py:577
  12.4 0.0 collective-permute-start.8
  12.4 0.0 collective-permute-done.6.refs_3_
  12.4 0.5 %collective-permute-start.10 = (f32[3,4,16,256]{3,2,1,0:T(8,128)S(1)}, f32[3,4,16,256]{3,2,1,0:T(8,128)S(1)}, u32[]{:S(2)}, u32[]{:S(2)}) collective-permute-start(f32[3,4,16,256]{3,2,1,0:T(8,128)S(1)} %collective-permute-done.6.refs_3_), channel_id=1, source_target_pairs={{0,8},{8,0},{16,24},{24,16},{1,9},{9,1},{17,25},{25,17},{2,10},{10... | collective-permute-start | bytes 589832 | tf_op jit(solution)/shard_map/ppermute | solution.py:589
  12.9 0.1 collective-permute-done.5.refs_2_
  13.0 0.0 collective-permute-start.9
  13.0 0.5 %collective-permute-start.4 = (f32[3,4,16,256]{3,2,1,0:T(8,128)S(1)}, f32[3,4,16,256]{3,2,1,0:T(8,128)S(1)}, u32[]{:S(2)}, u32[]{:S(2)}) collective-permute-start(f32[3,4,16,256]{3,2,1,0:T(8,128)S(1)} %collective-permute-done.2.refs_1_), channel_id=1, source_target_pairs={{0,8},{8,0},{16,24},{24,16},{1,9},{9,1},{17,25},{25,17},{2,10},{10... | collective-permute-start | bytes 589832 | tf_op jit(solution)/shard_map/ppermute | solution.py:589
  13.5 3.3 %collective-permute-done.1.refs_0_ = f32[3,4,16,256]{3,2,1,0:T(8,128)S(1)} collective-permute-done((f32[3,4,16,256]{3,2,1,0:T(8,128)S(1)}, f32[3,4,16,256]{3,2,1,0:T(8,128)S(1)}, u32[]{:S(2)}, u32[]{:S(2)}) %collective-permute-start.1) | collective-permute-done | bytes 196640 | tf_op jit(solution)/shard_map/ppermute | solution.py:577
  16.8 0.0 collective-permute-done.9.refs_6_
  16.8 0.0 collective-permute-done.8.refs_5_
  16.8 0.4 %shard_map.37 = (f32[2,2,8,48,128]{4,3,2,1,0:T(8,128)S(1)}, f32[4,2,8,48,128]{4,3,2,1,0:T(8,128)S(1)}, f32[7,2,8,48,128]{4,3,2,1,0:T(8,128)S(1)}) custom-call(f32[3,4,16,256]{3,2,1,0:T(8,128)S(1)} %select_select_fusion.refs_0_, f32[3,4,16,256]{3,2,1,0:T(8,128)S(1)} %collective-permute-done.refs_1_, f32[3,4,16,256]{3,2,1,0:T(8,128)S(1)} %collective-permute-done.5.refs_2_, ...), custom_call_target="tpu_custom_call" | custom-call | tf_op jit(solution)/shard_map/pallas_call | solution.py:525
  17.2 0.0 collective-permute-done.4.refs_3_
  17.2 1.0 %collective-permute-done.3.refs_2_ = f32[3,4,16,256]{3,2,1,0:T(8,128)S(1)} collective-permute-done((f32[3,4,16,256]{3,2,1,0:T(8,128)S(1)}, f32[3,4,16,256]{3,2,1,0:T(8,128)S(1)}, u32[]{:S(2)}, u32[]{:S(2)}) %collective-permute-start.3) | collective-permute-done | bytes 196640 | tf_op jit(solution)/shard_map/ppermute | solution.py:589
  18.2 1.7 %shard_map.38 = (f32[2,8,32,128]{3,2,1,0:T(8,128)S(1)}, f32[2,2,8,48,128]{4,3,2,1,0:T(8,128)S(1)}, f32[4,2,8,48,128]{4,3,2,1,0:T(8,128)S(1)}, f32[7,2,8,48,128]{4,3,2,1,0:T(8,128)S(1)}) custom-call(f32[3,4,16,256]{3,2,1,0:T(8,128)S(1)} %collective-permute-done.1.refs_0_, ...), custom_call_target="tpu_custom_call", output_to_operand_aliasing={{1}: (4, {}), {2}: (5, {}), {3}: (6, {})} | custom-call | tf_op jit(solution)/shard_map/pallas_call | solution.py:525
  19.9 0.2 collective-permute-start.11
  20.1 0.6 %shard_map.39 = (f32[7,2,4,48,128]{4,3,2,1,0:T(8,128)S(1)}, f32[2,8,48,128]{3,2,1,0:T(8,128)S(1)}) custom-call(f32[4,2,8,48,128]{4,3,2,1,0:T(8,128)S(1)} %get-tuple-element.25.coeff), custom_call_target="tpu_custom_call" | custom-call | tf_op jit(solution)/shard_map/pallas_call | solution.py:525
  20.8 0.7 %collective-permute-done.11.other_end = f32[2,8,32,128]{3,2,1,0:T(8,128)S(1)} collective-permute-done((f32[2,8,32,128]{3,2,1,0:T(8,128)S(1)}, f32[2,8,32,128]{3,2,1,0:T(8,128)S(1)}, u32[]{:S(2)}, u32[]{:S(2)}) %collective-permute-start.11) | collective-permute-done | bytes 262176 | tf_op jit(solution)/shard_map/ppermute | solution.py:589
  21.5 0.8 %shard_map.40 = (f32[2,8,16,128]{3,2,1,0:T(8,128)S(1)}, f32[2,8,16,128]{3,2,1,0:T(8,128)S(1)}, f32[2,4,16,128]{3,2,1,0:T(8,128)S(1)}, f32[2,96,128]{2,1,0:T(8,128)S(1)}) custom-call(f32[2,8,32,128]{3,2,1,0:T(8,128)S(1)} %get-tuple-element.22.own_end, f32[2,8,32,128]{3,2,1,0:T(8,128)S(1)} %collective-permute-done.11.other_end, ...), custom_call_target="tpu_custom_call" | custom-call | tf_op jit(solution)/shard_map/pallas_call | solution.py:525
  22.3 2.8 %collective-permute-start.13 = (f32[2,96,128]{2,1,0:T(8,128)S(1)}, f32[2,96,128]{2,1,0:T(8,128)S(1)}, u32[]{:S(2)}, u32[]{:S(2)}) collective-permute-start(f32[2,96,128]{2,1,0:T(8,128)S(1)} %get-tuple-element.31), channel_id=1, source_target_pairs={{0,17},{16,1},{1,16},{17,0},{2,19},{18,3},{3,18},{19,2},{8,24},{24... | collective-permute-start | bytes 294920 | tf_op jit(solution)/shard_map/ppermute | solution.py:668
  25.1 0.5 %collective-permute-start.12 = (f32[2,4,16,128]{3,2,1,0:T(8,128)S(1)}, f32[2,4,16,128]{3,2,1,0:T(8,128)S(1)}, u32[]{:S(2)}, u32[]{:S(2)}) collective-permute-start(f32[2,4,16,128]{3,2,1,0:T(8,128)S(1)} %get-tuple-element.30), channel_id=1, source_target_pairs={{0,16},{8,24},{16,0},{24,8},{1,17},{9,25},{17,1},{25,9},{2,18},{10... | collective-permute-start | bytes 196616 | tf_op jit(solution)/shard_map/ppermute | solution.py:667
  25.6 2.4 %collective-permute-done.13.rest_1_ = f32[2,96,128]{2,1,0:T(8,128)S(1)} collective-permute-done((f32[2,96,128]{2,1,0:T(8,128)S(1)}, f32[2,96,128]{2,1,0:T(8,128)S(1)}, u32[]{:S(2)}, u32[]{:S(2)}) %collective-permute-start.13) | collective-permute-done | bytes 98336 | tf_op jit(solution)/shard_map/ppermute | solution.py:668
  28.0 1.3 %collective-permute-done.12.rest_0_ = f32[2,4,16,128]{3,2,1,0:T(8,128)S(1)} collective-permute-done((f32[2,4,16,128]{3,2,1,0:T(8,128)S(1)}, f32[2,4,16,128]{3,2,1,0:T(8,128)S(1)}, u32[]{:S(2)}, u32[]{:S(2)}) %collective-permute-start.12) | collective-permute-done | bytes 65568 | tf_op jit(solution)/shard_map/ppermute | solution.py:667
  29.4 0.0 collective-permute-start.14
  29.4 1.3 %collective-permute-done.14.rest_2_ = f32[2,4,16,128]{3,2,1,0:T(8,128)S(1)} collective-permute-done((f32[2,4,16,128]{3,2,1,0:T(8,128)S(1)}, f32[2,4,16,128]{3,2,1,0:T(8,128)S(1)}, u32[]{:S(2)}, u32[]{:S(2)}) %collective-permute-start.14) | collective-permute-done | bytes 65568 | tf_op jit(solution)/shard_map/ppermute | solution.py:589
  30.6 2.3 %shard_map.41 = (f32[1,4,16,256]{3,2,1,0:T(8,128)}, f32[2,4,16,128]{3,2,1,0:T(8,128)}, f32[2,96,128]{2,1,0:T(8,128)}) custom-call(f32[2,8,16,128]{3,2,1,0:T(8,128)S(1)} %get-tuple-element.28.first_end, f32[2,8,16,128]{3,2,1,0:T(8,128)S(1)} %get-tuple-element.29.joined, f32[2,4,16,128]{3,2,1,0:T(8,128)S(1)} %collective-permute-done.12.rest_0_, ...), custom_call_target="tpu_custom_call" | custom-call | tf_op jit(solution)/shard_map/pallas_call | solution.py:525
  (7 shorter events, 0.0 us)
Async XLA Ops:
  1.1 7.9 %collective-permute-start = (f32[3,4,16,256]{3,2,1,0:T(8,128)S(1)}, f32[3,4,16,256]{3,2,1,0:T(8,128)S(1)}, u32[]{:S(2)}, u32[]{:S(2)}) collective-permute-start(f32[3,4,16,256]{3,2,1,0:T(8,128)S(1)} %select_select_fusion.refs_0_), channel_id=1, source_target_pairs={{0,4},{4,0},{1,5},{5,1},{2,6},{6,2},{3,7},{7,3},{8,12},{12,8},{9,1... | collective-permute-start | bytes 589832 | tf_op jit(solution)/shard_map/ppermute | solution.py:541
  4.1 8.3 %collective-permute-start.7 = (f32[3,4,16,256]{3,2,1,0:T(8,128)S(1)}, f32[3,4,16,256]{3,2,1,0:T(8,128)S(1)}, u32[]{:S(2)}, u32[]{:S(2)}) collective-permute-start(f32[3,4,16,256]{3,2,1,0:T(8,128)S(1)} %select_select_fusion.refs_0_), channel_id=1, source_target_pairs={{0,8},{8,0},{16,24},{24,16},{1,9},{9,1},{17,25},{25,17},{2,10},{10... | collective-permute-start | bytes 589832 | tf_op jit(solution)/shard_map/ppermute | solution.py:589
  4.1 8.3 %collective-permute-start.6 = (f32[3,4,16,256]{3,2,1,0:T(8,128)S(1)}, f32[3,4,16,256]{3,2,1,0:T(8,128)S(1)}, u32[]{:S(2)}, u32[]{:S(2)}) collective-permute-start(f32[3,4,16,256]{3,2,1,0:T(8,128)S(1)} %select_select_fusion.refs_0_), channel_id=1, source_target_pairs={{0,8},{8,0},{16,24},{24,16},{1,2},{9,10},{17,18},{25,26},{2,1},{10... | collective-permute-start | bytes 589832 | tf_op jit(solution)/shard_map/ppermute | solution.py:578
  4.6 8.4 %collective-permute-start.5 = (f32[3,4,16,256]{3,2,1,0:T(8,128)S(1)}, f32[3,4,16,256]{3,2,1,0:T(8,128)S(1)}, u32[]{:S(2)}, u32[]{:S(2)}) collective-permute-start(f32[3,4,16,256]{3,2,1,0:T(8,128)S(1)} %select_select_fusion.refs_0_), channel_id=1, source_target_pairs={{0,1},{8,9},{16,17},{24,25},{1,0},{9,8},{17,16},{25,24},{2,3},{10,... | collective-permute-start | bytes 589832 | tf_op jit(solution)/shard_map/ppermute | solution.py:577
  9.0 4.0 %collective-permute-start.2 = (f32[3,4,16,256]{3,2,1,0:T(8,128)S(1)}, f32[3,4,16,256]{3,2,1,0:T(8,128)S(1)}, u32[]{:S(2)}, u32[]{:S(2)}) collective-permute-start(f32[3,4,16,256]{3,2,1,0:T(8,128)S(1)} %collective-permute-done.refs_1_), channel_id=1, source_target_pairs={{0,8},{8,0},{16,24},{24,16},{1,2},{9,10},{17,18},{25,26},{2,1},{10... | collective-permute-start | bytes 589832 | tf_op jit(solution)/shard_map/ppermute | solution.py:578
  9.0 7.8 %collective-permute-start.1 = (f32[3,4,16,256]{3,2,1,0:T(8,128)S(1)}, f32[3,4,16,256]{3,2,1,0:T(8,128)S(1)}, u32[]{:S(2)}, u32[]{:S(2)}) collective-permute-start(f32[3,4,16,256]{3,2,1,0:T(8,128)S(1)} %collective-permute-done.refs_1_), channel_id=1, source_target_pairs={{0,1},{8,9},{16,17},{24,25},{1,0},{9,8},{17,16},{25,24},{2,3},{10,... | collective-permute-start | bytes 589832 | tf_op jit(solution)/shard_map/ppermute | solution.py:577
  12.4 4.4 %collective-permute-start.8 = (f32[3,4,16,256]{3,2,1,0:T(8,128)S(1)}, f32[3,4,16,256]{3,2,1,0:T(8,128)S(1)}, u32[]{:S(2)}, u32[]{:S(2)}) collective-permute-start(f32[3,4,16,256]{3,2,1,0:T(8,128)S(1)} %collective-permute-done.refs_1_), channel_id=1, source_target_pairs={{0,8},{8,0},{16,24},{24,16},{1,9},{9,1},{17,25},{25,17},{2,10},{10... | collective-permute-start | bytes 589832 | tf_op jit(solution)/shard_map/ppermute | solution.py:589
  12.4 4.4 %collective-permute-start.10 = (f32[3,4,16,256]{3,2,1,0:T(8,128)S(1)}, f32[3,4,16,256]{3,2,1,0:T(8,128)S(1)}, u32[]{:S(2)}, u32[]{:S(2)}) collective-permute-start(f32[3,4,16,256]{3,2,1,0:T(8,128)S(1)} %collective-permute-done.6.refs_3_), channel_id=1, source_target_pairs={{0,8},{8,0},{16,24},{24,16},{1,9},{9,1},{17,25},{25,17},{2,10},{10... | collective-permute-start | bytes 589832 | tf_op jit(solution)/shard_map/ppermute | solution.py:589
  13.0 3.8 %collective-permute-start.9 = (f32[3,4,16,256]{3,2,1,0:T(8,128)S(1)}, f32[3,4,16,256]{3,2,1,0:T(8,128)S(1)}, u32[]{:S(2)}, u32[]{:S(2)}) collective-permute-start(f32[3,4,16,256]{3,2,1,0:T(8,128)S(1)} %collective-permute-done.5.refs_2_), channel_id=1, source_target_pairs={{0,8},{8,0},{16,24},{24,16},{1,9},{9,1},{17,25},{25,17},{2,10},{10... | collective-permute-start | bytes 589832 | tf_op jit(solution)/shard_map/ppermute | solution.py:589
  13.0 4.2 %collective-permute-start.4 = (f32[3,4,16,256]{3,2,1,0:T(8,128)S(1)}, f32[3,4,16,256]{3,2,1,0:T(8,128)S(1)}, u32[]{:S(2)}, u32[]{:S(2)}) collective-permute-start(f32[3,4,16,256]{3,2,1,0:T(8,128)S(1)} %collective-permute-done.2.refs_1_), channel_id=1, source_target_pairs={{0,8},{8,0},{16,24},{24,16},{1,9},{9,1},{17,25},{25,17},{2,10},{10... | collective-permute-start | bytes 589832 | tf_op jit(solution)/shard_map/ppermute | solution.py:589
  16.8 1.4 %collective-permute-start.3 = (f32[3,4,16,256]{3,2,1,0:T(8,128)S(1)}, f32[3,4,16,256]{3,2,1,0:T(8,128)S(1)}, u32[]{:S(2)}, u32[]{:S(2)}) collective-permute-start(f32[3,4,16,256]{3,2,1,0:T(8,128)S(1)} %collective-permute-done.1.refs_0_), channel_id=1, source_target_pairs={{0,8},{8,0},{16,24},{24,16},{1,9},{9,1},{17,25},{25,17},{2,10},{10... | collective-permute-start | bytes 589832 | tf_op jit(solution)/shard_map/ppermute | solution.py:589
  19.9 1.6 %collective-permute-start.11 = (f32[2,8,32,128]{3,2,1,0:T(8,128)S(1)}, f32[2,8,32,128]{3,2,1,0:T(8,128)S(1)}, u32[]{:S(2)}, u32[]{:S(2)}) collective-permute-start(f32[2,8,32,128]{3,2,1,0:T(8,128)S(1)} %get-tuple-element.22.own_end), channel_id=1, source_target_pairs={{0,8},{8,0},{16,24},{24,16},{1,9},{9,1},{17,25},{25,17},{2,10},{10... | collective-permute-start | bytes 786440 | tf_op jit(solution)/shard_map/ppermute | solution.py:589
  22.3 5.7 %collective-permute-start.13 = (f32[2,96,128]{2,1,0:T(8,128)S(1)}, f32[2,96,128]{2,1,0:T(8,128)S(1)}, u32[]{:S(2)}, u32[]{:S(2)}) collective-permute-start(f32[2,96,128]{2,1,0:T(8,128)S(1)} %get-tuple-element.31), channel_id=1, source_target_pairs={{0,17},{16,1},{1,16},{17,0},{2,19},{18,3},{3,18},{19,2},{8,24},{24... | collective-permute-start | bytes 294920 | tf_op jit(solution)/shard_map/ppermute | solution.py:668
  25.1 4.3 %collective-permute-start.12 = (f32[2,4,16,128]{3,2,1,0:T(8,128)S(1)}, f32[2,4,16,128]{3,2,1,0:T(8,128)S(1)}, u32[]{:S(2)}, u32[]{:S(2)}) collective-permute-start(f32[2,4,16,128]{3,2,1,0:T(8,128)S(1)} %get-tuple-element.30), channel_id=1, source_target_pairs={{0,16},{8,24},{16,0},{24,8},{1,17},{9,25},{17,1},{25,9},{2,18},{10... | collective-permute-start | bytes 196616 | tf_op jit(solution)/shard_map/ppermute | solution.py:667
  28.0 2.6 %collective-permute-start.15 = (f32[2,96,128]{2,1,0:T(8,128)S(1)}, f32[2,96,128]{2,1,0:T(8,128)S(1)}, u32[]{:S(2)}, u32[]{:S(2)}) collective-permute-start(f32[2,96,128]{2,1,0:T(8,128)S(1)} %collective-permute-done.13.rest_1_), channel_id=1, source_target_pairs={{0,8},{8,0},{16,24},{24,16},{1,9},{9,1},{17,25},{25,17},{2,10},{10... | collective-permute-start | bytes 294920 | tf_op jit(solution)/shard_map/ppermute | solution.py:589
  29.4 1.3 %collective-permute-start.14 = (f32[2,4,16,128]{3,2,1,0:T(8,128)S(1)}, f32[2,4,16,128]{3,2,1,0:T(8,128)S(1)}, u32[]{:S(2)}, u32[]{:S(2)}) collective-permute-start(f32[2,4,16,128]{3,2,1,0:T(8,128)S(1)} %collective-permute-done.12.rest_0_), channel_id=1, source_target_pairs={{0,8},{8,0},{16,24},{24,16},{1,9},{9,1},{17,25},{25,17},{2,10},{10... | collective-permute-start | bytes 196616 | tf_op jit(solution)/shard_map/ppermute | solution.py:589

commit v8 on v7

--- a/solution.py
+++ b/solution.py
@@ -235,20 +235,27 @@
     place_pieces(box, own_depth, moves, starts, coeff, weights)
 
 
+def late_moves(box, blocks, own, other, which):
+    if blocks == 1:
+        return []
+    steps = len(own) // (blocks - 1)
+    places = row_places(box, [ref.shape[-2] for ref in own[:steps]])
+    return [
+        (own[n], other[n], 1 + n // steps, blocks, *places[n % steps][which]) for n in range(len(own))
+    ]
+
+
+def late_body(box, own_depth, blocks, *refs):
+    half = (len(refs) - 6) // 2
+    moves = late_moves(box, blocks, refs[:half], refs[half : 2 * half], 1)
+    place_pieces(box, own_depth, moves, *refs[-3:])
+
+
 def fine_body(box, margin, own_depth, blocks, *refs):
     end, starts, coeff, weights, one, two = refs[-6:]
     half = (len(refs) - 9) // 2
-    own, other = refs[:half], refs[half : 2 * half]
     core = lax.axis_index("tm") % 2
-    moves = []
-    if blocks > 1:
-        each = half // (blocks - 1)
-        places = row_places(box, [ref.shape[-2] for ref in own[0:each:2]])
-        for block in range(1, blocks):
-            for step, pair in enumerate(places):
-                for which, (at, valid) in enumerate(pair):
-                    index = (block - 1) * each + 2 * step + which
-                    moves.append((own[index], other[index], block, blocks, at, valid))
+    moves = late_moves(box, blocks, refs[:half], refs[half : 2 * half], 0)
     place_pieces(box, own_depth, moves, starts, coeff, weights)
     clear_edges(one, 0, box.height)
     clear_edges(two, 0, box.height)
@@ -324,7 +331,9 @@
     sweep(half, 0, box.height, rows)
 
 
-def coarse_step_body(box, margin, source, trial, pairs, guess, residual, params, finish):
+def coarse_step_body(
+    box, margin, source, trial, pairs, guess, residual, params, finish, base=0, planes=None
+):
     weights, coarse, weight = params
     half = box.depth // 2
     centre_constant = fine_scheme()[0]
@@ -386,7 +395,14 @@
             value = (1.0 - RELAX) * centre + weight[i, plane, pl.ds(at, size), :] * (given + total)
             finish(plane, i, at, size, value)
 
-    sweep(box.depth, *box.span(margin), smooth_again)
+    if planes is None:
+        sweep(box.depth, *box.span(margin), smooth_again)
+    else:
+        sweep(
+            planes,
+            *box.span(margin),
+            lambda plane, at, size, cache: smooth_again(base + plane, at, size, None),
+        )
 
 
 def coarse_scratch(box):
@@ -438,10 +454,10 @@
             )
 
 
-def last_body(box, own_depth, turn, first_end, joined, *rest):
+def last_body(box, own_depth, turn, final, first_end, joined, *rest):
     arrived, rest = rest[:4], rest[4:]
-    starts, params, result, leaving = rest[0], rest[1:4], rest[4], rest[5:7]
-    source, second, trial, pairs, guess, residual, total = rest[7:]
+    starts, params, result, leaving = rest[0], rest[1:4], rest[4], rest[5:-7]
+    source, second, trial, pairs, guess, residual, total = rest[-7:]
     place = lax.axis_index("tm")
     core = place % 2
     active = place // 2 == turn
@@ -498,12 +514,26 @@
         box, COARSE_REACH, source, trial, pairs, guess, residual, params, finish_once
     )
 
+    base = lax.axis_index("slab") * own_depth
+    if final:
+
+        def finish_result(plane, i, at, size, value):
+            where = (i, plane, pl.ds(at - side, size), slice(None))
+            once = second[i, plane + 2, pl.ds(PAD + at, size), :]
+            result[0, plane - base, pl.ds(at - side, size), i * LANES : (i + 1) * LANES] = jnp.where(
+                core == 1, value + joined[where], once + first_end[where]
+            )
+
+        coarse_step_body(
+            box, 0, second, trial, pairs, guess, residual, params, finish_result, base, own_depth
+        )
+        return
+
     def finish_twice(plane, i, at, size, value):
         where = (i, plane, pl.ds(at - box.side, size), slice(None))
         total[where] = value + joined[where]
 
     coarse_step_body(box, 0, second, trial, pairs, guess, residual, params, finish_twice)
-    base = lax.axis_index("slab") * own_depth
 
     @pl.when(core == 0)
     def _():
@@ -622,15 +652,28 @@
     far = []
     for block in blocks[1:]:
         far += row_pieces(block, side, rounds)
-    far += [core_swapped(piece) for piece in far]
+    far = [piece for which in (1, 0) for piece in far[which::2]]
+    far_swapped = [core_swapped(piece) for piece in far]
+    cut = len(far) // 2
+    if far:
+        placed = run(
+            functools.partial(late_body, box, own_depth, count),
+            shapes,
+            [],
+            *far[:cut],
+            *far_swapped[:cut],
+            *placed,
+            aliases={2 * cut + n: n for n in range(3)},
+        )
     first, last = box.span(COARSE_REACH)
     end, starts, coeff, weights = run(
         functools.partial(fine_body, box, COARSE_REACH, own_depth, count),
         [(tiles, depth, last - first, LANES)] + shapes,
         [box.scratch(), box.scratch()],
-        *far,
+        *far[cut:],
+        *far_swapped[cut:],
         *placed,
-        aliases={len(far) + n: 1 + n for n in range(3)},
+        aliases={2 * cut + n: 1 + n for n in range(3)},
     )
     params = run(
         functools.partial(prepare_body, box),
@@ -668,9 +711,10 @@
             lax.ppermute(leaving[1], ("tm", "coarse"), aside),
         ]
         arrived += [core_swapped(piece) for piece in arrived]
+        final = turn == windows // 2 - 1
         out, *leaving = run(
-            functools.partial(last_body, box, own_depth, turn),
-            [(1, own_depth, rows, columns)] + leaving_shapes,
+            functools.partial(last_body, box, own_depth, turn, final),
+            [(1, own_depth, rows, columns)] + ([] if final else leaving_shapes),
             [box.scratch()] * 2
             + coarse_scratch(box)
             + [pltpu.VMEM((tiles, depth, rows, LANES), jnp.float32)],

time: 33.1 us -> 32.5 us (0.982)
  waiting for transfers between devices: 11.9 us -> 11.3 us
    ppermute x2, starting transfers between devices: 0.51 us -> 0.01 us  [row_pieces(): got_two = lax.ppermute(send_two, both, rounds[1])]
    ppermute x2, starting transfers between devices: 6.04 us -> 6.55 us  [row_pieces(): got_one = lax.ppermute(send_one, both, rounds[0])]
    ppermute x2, waiting for transfers between devices: 3.32 us -> 2.88 us  [row_pieces(): got_one = lax.ppermute(send_one, both, rounds[0])]
    pallas_call x5 -> x6, Pallas kernels: 5.86 us -> 5.81 us  [run(): pl.pallas_call(body, out_shape=[jax.ShapeDtypeStruct(shape, jnp.float32)...]
  transfers between devices with their start and end apart: 16 -> 16, of which waited for: 8 -> 7; matrix products, arithmetic and copies ran while one was open for 0% -> 0% of each run, Pallas kernels for 3% -> 3%
where the time goes in v8:
time: 32.5 us; the launch traced here: 32.4 us
  starting transfers between devices  14.1 us (43%)
  waiting for transfers between devices  11.3 us (35%)
  Pallas kernels  5.81 us (18%)
  other arithmetic  1.06 us (3%)
    ppermute x2, starting transfers between devices, row_pieces(): got_one = lax.ppermute(send_one, both, rounds[0])  6.55 us
    pallas_call x6, Pallas kernels, run(): pl.pallas_call(body, out_shape=[jax.ShapeDtypeStruct(shape, jnp.float32)...  5.81 us
    ppermute x1, starting transfers between devices, slab_blocks(): return [block, lax.ppermute(block, 'slab', [(0, 1), (1, 0)])]  3.04 us
    ppermute x9, waiting for transfers between devices, core_swapped(): return lax.ppermute(block, 'tm', [(i, i ^ 1) for i in range(count)])  2.92 us
    ppermute x2, waiting for transfers between devices, row_pieces(): got_one = lax.ppermute(send_one, both, rounds[0])  2.88 us
    ppermute x1, starting transfers between devices, per_device(): lax.ppermute(leaving[1], ('tm', 'coarse'), aside)  2.78 us
    ppermute x1, waiting for transfers between devices, per_device(): lax.ppermute(leaving[1], ('tm', 'coarse'), aside)  2.4 us
    ppermute x1, waiting for transfers between devices, slab_blocks(): return [block, lax.ppermute(block, 'slab', [(0, 1), (1, 0)])]  1.74 us
  transfers between devices with their start and end apart: 16, of which 7 were waited for; matrix products, arithmetic and copies ran while one was open for 0% of the time, Pallas kernels for 3%

profile of v8, /device:TPU:0, one launch (start us, length us, event | category | flops | bytes accessed | tf_op | source)
XLA Modules:
  0.0 32.4 jit_solution(8749384719266457308)
XLA Ops:
  0.0 1.1 %select_select_fusion.refs_0_ = f32[3,4,16,256]{3,2,1,0:T(8,128)S(1)} fusion(f32[3,4,16,256]{3,2,1,0:T(8,128)} %param.5, f32[4,16,256]{2,1,0:T(8,128)} %bitcast.1, f32[4,16,256]{2,1,0:T(8,128)} %param.4, pred[3]{0:T(512)(128)(4,1)S(1)} %get-tuple-element.38, pred[3]{0:T(512)(128)(4,1)S(1)} %get-tuple-element.37), kind=kLoop, calls=%fused_computation | loop fusion | flops 98304 | bytes 524294 | tf_op jit(solution)/shard_map/jit(_where)/select_n | solution.py:633
  1.1 3.0 %collective-permute-start = (f32[3,4,16,256]{3,2,1,0:T(8,128)S(1)}, f32[3,4,16,256]{3,2,1,0:T(8,128)S(1)}, u32[]{:S(2)}, u32[]{:S(2)}) collective-permute-start(f32[3,4,16,256]{3,2,1,0:T(8,128)S(1)} %select_select_fusion.refs_0_), channel_id=1, source_target_pairs={{0,4},{4,0},{1,5},{5,1},{2,6},{6,2},{3,7},{7,3},{8,12},{12,8},{9,1... | collective-permute-start | bytes 589832 | tf_op jit(solution)/shard_map/ppermute | solution.py:571
  4.1 3.1 %collective-permute-start.5 = (f32[3,4,16,256]{3,2,1,0:T(8,128)S(1)}, f32[3,4,16,256]{3,2,1,0:T(8,128)S(1)}, u32[]{:S(2)}, u32[]{:S(2)}) collective-permute-start(f32[3,4,16,256]{3,2,1,0:T(8,128)S(1)} %select_select_fusion.refs_0_), channel_id=1, source_target_pairs={{0,1},{8,9},{16,17},{24,25},{1,0},{9,8},{17,16},{25,24},{2,3},{10,... | collective-permute-start | bytes 589832 | tf_op jit(solution)/shard_map/ppermute | solution.py:607
  7.3 1.7 %collective-permute-done.refs_1_ = f32[3,4,16,256]{3,2,1,0:T(8,128)S(1)} collective-permute-done((f32[3,4,16,256]{3,2,1,0:T(8,128)S(1)}, f32[3,4,16,256]{3,2,1,0:T(8,128)S(1)}, u32[]{:S(2)}, u32[]{:S(2)}) %collective-permute-start) | collective-permute-done | bytes 196640 | tf_op jit(solution)/shard_map/ppermute | solution.py:571
  9.0 3.4 %collective-permute-start.1 = (f32[3,4,16,256]{3,2,1,0:T(8,128)S(1)}, f32[3,4,16,256]{3,2,1,0:T(8,128)S(1)}, u32[]{:S(2)}, u32[]{:S(2)}) collective-permute-start(f32[3,4,16,256]{3,2,1,0:T(8,128)S(1)} %collective-permute-done.refs_1_), channel_id=1, source_target_pairs={{0,1},{8,9},{16,17},{24,25},{1,0},{9,8},{17,16},{25,24},{2,3},{10,... | collective-permute-start | bytes 589832 | tf_op jit(solution)/shard_map/ppermute | solution.py:607
  12.4 0.0 collective-permute-done.6.refs_3_
  12.4 0.0 collective-permute-start.8
  12.4 0.0 collective-permute-done.5.refs_2_
  12.4 0.5 %collective-permute-start.10 = (f32[3,4,16,256]{3,2,1,0:T(8,128)S(1)}, f32[3,4,16,256]{3,2,1,0:T(8,128)S(1)}, u32[]{:S(2)}, u32[]{:S(2)}) collective-permute-start(f32[3,4,16,256]{3,2,1,0:T(8,128)S(1)} %collective-permute-done.6.refs_3_), channel_id=1, source_target_pairs={{0,8},{8,0},{16,24},{24,16},{1,9},{9,1},{17,25},{25,17},{2,10},{10... | collective-permute-start | bytes 589832 | tf_op jit(solution)/shard_map/ppermute | solution.py:619
  12.9 0.0 collective-permute-done.7.refs_4_
  12.9 0.1 collective-permute-start.9
  13.0 0.0 collective-permute-done.3.refs_0_
  13.0 0.4 %collective-permute-start.4 = (f32[3,4,16,256]{3,2,1,0:T(8,128)S(1)}, f32[3,4,16,256]{3,2,1,0:T(8,128)S(1)}, u32[]{:S(2)}, u32[]{:S(2)}) collective-permute-start(f32[3,4,16,256]{3,2,1,0:T(8,128)S(1)} %collective-permute-done.3.refs_0_), channel_id=1, source_target_pairs={{0,8},{8,0},{16,24},{24,16},{1,9},{9,1},{17,25},{25,17},{2,10},{10... | collective-permute-start | bytes 589832 | tf_op jit(solution)/shard_map/ppermute | solution.py:619
  13.4 2.9 %collective-permute-done.1.refs_0_ = f32[3,4,16,256]{3,2,1,0:T(8,128)S(1)} collective-permute-done((f32[3,4,16,256]{3,2,1,0:T(8,128)S(1)}, f32[3,4,16,256]{3,2,1,0:T(8,128)S(1)}, u32[]{:S(2)}, u32[]{:S(2)}) %collective-permute-start.1) | collective-permute-done | bytes 196640 | tf_op jit(solution)/shard_map/ppermute | solution.py:607
  16.3 0.0 collective-permute-start.2
  16.3 0.0 collective-permute-done.10.refs_7_
  16.3 0.0 collective-permute-done.8.refs_5_
  16.3 0.0 collective-permute-done.9.refs_6_
  16.3 0.4 %shard_map.37 = (f32[2,2,8,48,128]{4,3,2,1,0:T(8,128)S(1)}, f32[4,2,8,48,128]{4,3,2,1,0:T(8,128)S(1)}, f32[7,2,8,48,128]{4,3,2,1,0:T(8,128)S(1)}) custom-call(f32[3,4,16,256]{3,2,1,0:T(8,128)S(1)} %select_select_fusion.refs_0_, f32[3,4,16,256]{3,2,1,0:T(8,128)S(1)} %collective-permute-done.refs_1_, f32[3,4,16,256]{3,2,1,0:T(8,128)S(1)} %collective-permute-done.5.refs_2_, ...), custom_call_target="tpu_custom_call" | custom-call | tf_op jit(solution)/shard_map/pallas_call | solution.py:555
  16.7 0.1 shard_map.38
  16.9 0.9 %collective-permute-done.2.refs_1_ = f32[3,4,16,256]{3,2,1,0:T(8,128)S(1)} collective-permute-done((f32[3,4,16,256]{3,2,1,0:T(8,128)S(1)}, f32[3,4,16,256]{3,2,1,0:T(8,128)S(1)}, u32[]{:S(2)}, u32[]{:S(2)}) %collective-permute-start.2) | collective-permute-done | bytes 196640 | tf_op jit(solution)/shard_map/ppermute | solution.py:619
  17.8 1.6 %shard_map.39 = (f32[2,8,32,128]{3,2,1,0:T(8,128)S(1)}, f32[2,2,8,48,128]{4,3,2,1,0:T(8,128)S(1)}, f32[4,2,8,48,128]{4,3,2,1,0:T(8,128)S(1)}, f32[7,2,8,48,128]{4,3,2,1,0:T(8,128)S(1)}) custom-call(f32[3,4,16,256]{3,2,1,0:T(8,128)S(1)} %collective-permute-done.1.refs_0_, ...), custom_call_target="tpu_custom_call", output_to_operand_aliasing={{1}: (2, {}), {2}: (3, {}), {3}: (4, {})} | custom-call | tf_op jit(solution)/shard_map/pallas_call | solution.py:555
  19.4 0.2 collective-permute-start.11
  19.6 0.6 %shard_map.40 = (f32[7,2,4,48,128]{4,3,2,1,0:T(8,128)S(1)}, f32[2,8,48,128]{3,2,1,0:T(8,128)S(1)}) custom-call(f32[4,2,8,48,128]{4,3,2,1,0:T(8,128)S(1)} %get-tuple-element.30.coeff), custom_call_target="tpu_custom_call" | custom-call | tf_op jit(solution)/shard_map/pallas_call | solution.py:555
  20.3 0.7 %collective-permute-done.11.other_end = f32[2,8,32,128]{3,2,1,0:T(8,128)S(1)} collective-permute-done((f32[2,8,32,128]{3,2,1,0:T(8,128)S(1)}, f32[2,8,32,128]{3,2,1,0:T(8,128)S(1)}, u32[]{:S(2)}, u32[]{:S(2)}) %collective-permute-start.11) | collective-permute-done | bytes 262176 | tf_op jit(solution)/shard_map/ppermute | solution.py:619
  21.0 0.8 %shard_map.41 = (f32[2,8,16,128]{3,2,1,0:T(8,128)S(1)}, f32[2,8,16,128]{3,2,1,0:T(8,128)S(1)}, f32[2,4,16,128]{3,2,1,0:T(8,128)S(1)}, f32[2,96,128]{2,1,0:T(8,128)S(1)}) custom-call(f32[2,8,32,128]{3,2,1,0:T(8,128)S(1)} %get-tuple-element.27.own_end, f32[2,8,32,128]{3,2,1,0:T(8,128)S(1)} %collective-permute-done.11.other_end, ...), custom_call_target="tpu_custom_call" | custom-call | tf_op jit(solution)/shard_map/pallas_call | solution.py:555
  21.8 2.8 %collective-permute-start.13 = (f32[2,96,128]{2,1,0:T(8,128)S(1)}, f32[2,96,128]{2,1,0:T(8,128)S(1)}, u32[]{:S(2)}, u32[]{:S(2)}) collective-permute-start(f32[2,96,128]{2,1,0:T(8,128)S(1)} %get-tuple-element.36), channel_id=1, source_target_pairs={{0,17},{16,1},{1,16},{17,0},{2,19},{18,3},{3,18},{19,2},{8,24},{24... | collective-permute-start | bytes 294920 | tf_op jit(solution)/shard_map/ppermute | solution.py:711
  24.6 0.5 %collective-permute-start.12 = (f32[2,4,16,128]{3,2,1,0:T(8,128)S(1)}, f32[2,4,16,128]{3,2,1,0:T(8,128)S(1)}, u32[]{:S(2)}, u32[]{:S(2)}) collective-permute-start(f32[2,4,16,128]{3,2,1,0:T(8,128)S(1)} %get-tuple-element.35), channel_id=1, source_target_pairs={{0,16},{8,24},{16,0},{24,8},{1,17},{9,25},{17,1},{25,9},{2,18},{10... | collective-permute-start | bytes 196616 | tf_op jit(solution)/shard_map/ppermute | solution.py:710
  25.1 2.4 %collective-permute-done.13.rest_1_ = f32[2,96,128]{2,1,0:T(8,128)S(1)} collective-permute-done((f32[2,96,128]{2,1,0:T(8,128)S(1)}, f32[2,96,128]{2,1,0:T(8,128)S(1)}, u32[]{:S(2)}, u32[]{:S(2)}) %collective-permute-start.13) | collective-permute-done | bytes 98336 | tf_op jit(solution)/shard_map/ppermute | solution.py:711
  27.5 1.4 %collective-permute-done.12.rest_0_ = f32[2,4,16,128]{3,2,1,0:T(8,128)S(1)} collective-permute-done((f32[2,4,16,128]{3,2,1,0:T(8,128)S(1)}, f32[2,4,16,128]{3,2,1,0:T(8,128)S(1)}, u32[]{:S(2)}, u32[]{:S(2)}) %collective-permute-start.12) | collective-permute-done | bytes 65568 | tf_op jit(solution)/shard_map/ppermute | solution.py:710
  28.9 1.3 %collective-permute-done.14.rest_2_ = f32[2,4,16,128]{3,2,1,0:T(8,128)S(1)} collective-permute-done((f32[2,4,16,128]{3,2,1,0:T(8,128)S(1)}, f32[2,4,16,128]{3,2,1,0:T(8,128)S(1)}, u32[]{:S(2)}, u32[]{:S(2)}) %collective-permute-start.14) | collective-permute-done | bytes 65568 | tf_op jit(solution)/shard_map/ppermute | solution.py:619
  30.1 2.2 %shard_map.42 = f32[1,4,16,256]{3,2,1,0:T(8,128)} custom-call(f32[2,8,16,128]{3,2,1,0:T(8,128)S(1)} %get-tuple-element.33.first_end, f32[2,8,16,128]{3,2,1,0:T(8,128)S(1)} %get-tuple-element.34.joined, f32[2,4,16,128]{3,2,1,0:T(8,128)S(1)} %collective-permute-done.12.rest_0_, f32[2,96,128]{2,1,0:T(8,128)S(1)} %collective-permute-done.13.rest_1_, ...), custom_call_target="tpu_custom_call" | custom-call | tf_op jit(solution)/shard_map/pallas_call | solution.py:555
  (8 shorter events, 0.0 us)
Async XLA Ops:
  1.1 7.9 %collective-permute-start = (f32[3,4,16,256]{3,2,1,0:T(8,128)S(1)}, f32[3,4,16,256]{3,2,1,0:T(8,128)S(1)}, u32[]{:S(2)}, u32[]{:S(2)}) collective-permute-start(f32[3,4,16,256]{3,2,1,0:T(8,128)S(1)} %select_select_fusion.refs_0_), channel_id=1, source_target_pairs={{0,4},{4,0},{1,5},{5,1},{2,6},{6,2},{3,7},{7,3},{8,12},{12,8},{9,1... | collective-permute-start | bytes 589832 | tf_op jit(solution)/shard_map/ppermute | solution.py:571
  4.1 8.3 %collective-permute-start.6 = (f32[3,4,16,256]{3,2,1,0:T(8,128)S(1)}, f32[3,4,16,256]{3,2,1,0:T(8,128)S(1)}, u32[]{:S(2)}, u32[]{:S(2)}) collective-permute-start(f32[3,4,16,256]{3,2,1,0:T(8,128)S(1)} %select_select_fusion.refs_0_), channel_id=1, source_target_pairs={{0,8},{8,0},{16,24},{24,16},{1,2},{9,10},{17,18},{25,26},{2,1},{10... | collective-permute-start | bytes 589832 | tf_op jit(solution)/shard_map/ppermute | solution.py:608
  4.1 8.3 %collective-permute-start.5 = (f32[3,4,16,256]{3,2,1,0:T(8,128)S(1)}, f32[3,4,16,256]{3,2,1,0:T(8,128)S(1)}, u32[]{:S(2)}, u32[]{:S(2)}) collective-permute-start(f32[3,4,16,256]{3,2,1,0:T(8,128)S(1)} %select_select_fusion.refs_0_), channel_id=1, source_target_pairs={{0,1},{8,9},{16,17},{24,25},{1,0},{9,8},{17,16},{25,24},{2,3},{10,... | collective-permute-start | bytes 589832 | tf_op jit(solution)/shard_map/ppermute | solution.py:607
  7.3 5.7 %collective-permute-start.7 = (f32[3,4,16,256]{3,2,1,0:T(8,128)S(1)}, f32[3,4,16,256]{3,2,1,0:T(8,128)S(1)}, u32[]{:S(2)}, u32[]{:S(2)}) collective-permute-start(f32[3,4,16,256]{3,2,1,0:T(8,128)S(1)} %select_select_fusion.refs_0_), channel_id=1, source_target_pairs={{0,8},{8,0},{16,24},{24,16},{1,9},{9,1},{17,25},{25,17},{2,10},{10... | collective-permute-start | bytes 589832 | tf_op jit(solution)/shard_map/ppermute | solution.py:619
  9.0 4.0 %collective-permute-start.3 = (f32[3,4,16,256]{3,2,1,0:T(8,128)S(1)}, f32[3,4,16,256]{3,2,1,0:T(8,128)S(1)}, u32[]{:S(2)}, u32[]{:S(2)}) collective-permute-start(f32[3,4,16,256]{3,2,1,0:T(8,128)S(1)} %collective-permute-done.refs_1_), channel_id=1, source_target_pairs={{0,8},{8,0},{16,24},{24,16},{1,2},{9,10},{17,18},{25,26},{2,1},{10... | collective-permute-start | bytes 589832 | tf_op jit(solution)/shard_map/ppermute | solution.py:608
  9.0 7.3 %collective-permute-start.1 = (f32[3,4,16,256]{3,2,1,0:T(8,128)S(1)}, f32[3,4,16,256]{3,2,1,0:T(8,128)S(1)}, u32[]{:S(2)}, u32[]{:S(2)}) collective-permute-start(f32[3,4,16,256]{3,2,1,0:T(8,128)S(1)} %collective-permute-done.refs_1_), channel_id=1, source_target_pairs={{0,1},{8,9},{16,17},{24,25},{1,0},{9,8},{17,16},{25,24},{2,3},{10,... | collective-permute-start | bytes 589832 | tf_op jit(solution)/shard_map/ppermute | solution.py:607
  12.4 3.9 %collective-permute-start.8 = (f32[3,4,16,256]{3,2,1,0:T(8,128)S(1)}, f32[3,4,16,256]{3,2,1,0:T(8,128)S(1)}, u32[]{:S(2)}, u32[]{:S(2)}) collective-permute-start(f32[3,4,16,256]{3,2,1,0:T(8,128)S(1)} %collective-permute-done.refs_1_), channel_id=1, source_target_pairs={{0,8},{8,0},{16,24},{24,16},{1,9},{9,1},{17,25},{25,17},{2,10},{10... | collective-permute-start | bytes 589832 | tf_op jit(solution)/shard_map/ppermute | solution.py:619
  12.4 3.9 %collective-permute-start.10 = (f32[3,4,16,256]{3,2,1,0:T(8,128)S(1)}, f32[3,4,16,256]{3,2,1,0:T(8,128)S(1)}, u32[]{:S(2)}, u32[]{:S(2)}) collective-permute-start(f32[3,4,16,256]{3,2,1,0:T(8,128)S(1)} %collective-permute-done.6.refs_3_), channel_id=1, source_target_pairs={{0,8},{8,0},{16,24},{24,16},{1,9},{9,1},{17,25},{25,17},{2,10},{10... | collective-permute-start | bytes 589832 | tf_op jit(solution)/shard_map/ppermute | solution.py:619
  12.9 3.4 %collective-permute-start.9 = (f32[3,4,16,256]{3,2,1,0:T(8,128)S(1)}, f32[3,4,16,256]{3,2,1,0:T(8,128)S(1)}, u32[]{:S(2)}, u32[]{:S(2)}) collective-permute-start(f32[3,4,16,256]{3,2,1,0:T(8,128)S(1)} %collective-permute-done.5.refs_2_), channel_id=1, source_target_pairs={{0,8},{8,0},{16,24},{24,16},{1,9},{9,1},{17,25},{25,17},{2,10},{10... | collective-permute-start | bytes 589832 | tf_op jit(solution)/shard_map/ppermute | solution.py:619
  13.0 3.7 %collective-permute-start.4 = (f32[3,4,16,256]{3,2,1,0:T(8,128)S(1)}, f32[3,4,16,256]{3,2,1,0:T(8,128)S(1)}, u32[]{:S(2)}, u32[]{:S(2)}) collective-permute-start(f32[3,4,16,256]{3,2,1,0:T(8,128)S(1)} %collective-permute-done.3.refs_0_), channel_id=1, source_target_pairs={{0,8},{8,0},{16,24},{24,16},{1,9},{9,1},{17,25},{25,17},{2,10},{10... | collective-permute-start | bytes 589832 | tf_op jit(solution)/shard_map/ppermute | solution.py:619
  16.3 1.4 %collective-permute-start.2 = (f32[3,4,16,256]{3,2,1,0:T(8,128)S(1)}, f32[3,4,16,256]{3,2,1,0:T(8,128)S(1)}, u32[]{:S(2)}, u32[]{:S(2)}) collective-permute-start(f32[3,4,16,256]{3,2,1,0:T(8,128)S(1)} %collective-permute-done.1.refs_0_), channel_id=1, source_target_pairs={{0,8},{8,0},{16,24},{24,16},{1,9},{9,1},{17,25},{25,17},{2,10},{10... | collective-permute-start | bytes 589832 | tf_op jit(solution)/shard_map/ppermute | solution.py:619
  19.4 1.6 %collective-permute-start.11 = (f32[2,8,32,128]{3,2,1,0:T(8,128)S(1)}, f32[2,8,32,128]{3,2,1,0:T(8,128)S(1)}, u32[]{:S(2)}, u32[]{:S(2)}) collective-permute-start(f32[2,8,32,128]{3,2,1,0:T(8,128)S(1)} %get-tuple-element.27.own_end), channel_id=1, source_target_pairs={{0,8},{8,0},{16,24},{24,16},{1,9},{9,1},{17,25},{25,17},{2,10},{10... | collective-permute-start | bytes 786440 | tf_op jit(solution)/shard_map/ppermute | solution.py:619
  21.8 5.7 %collective-permute-start.13 = (f32[2,96,128]{2,1,0:T(8,128)S(1)}, f32[2,96,128]{2,1,0:T(8,128)S(1)}, u32[]{:S(2)}, u32[]{:S(2)}) collective-permute-start(f32[2,96,128]{2,1,0:T(8,128)S(1)} %get-tuple-element.36), channel_id=1, source_target_pairs={{0,17},{16,1},{1,16},{17,0},{2,19},{18,3},{3,18},{19,2},{8,24},{24... | collective-permute-start | bytes 294920 | tf_op jit(solution)/shard_map/ppermute | solution.py:711
  24.6 4.3 %collective-permute-start.12 = (f32[2,4,16,128]{3,2,1,0:T(8,128)S(1)}, f32[2,4,16,128]{3,2,1,0:T(8,128)S(1)}, u32[]{:S(2)}, u32[]{:S(2)}) collective-permute-start(f32[2,4,16,128]{3,2,1,0:T(8,128)S(1)} %get-tuple-element.35), channel_id=1, source_target_pairs={{0,16},{8,24},{16,0},{24,8},{1,17},{9,25},{17,1},{25,9},{2,18},{10... | collective-permute-start | bytes 196616 | tf_op jit(solution)/shard_map/ppermute | solution.py:710
  27.5 2.6 %collective-permute-start.15 = (f32[2,96,128]{2,1,0:T(8,128)S(1)}, f32[2,96,128]{2,1,0:T(8,128)S(1)}, u32[]{:S(2)}, u32[]{:S(2)}) collective-permute-start(f32[2,96,128]{2,1,0:T(8,128)S(1)} %collective-permute-done.13.rest_1_), channel_id=1, source_target_pairs={{0,8},{8,0},{16,24},{24,16},{1,9},{9,1},{17,25},{25,17},{2,10},{10... | collective-permute-start | bytes 294920 | tf_op jit(solution)/shard_map/ppermute | solution.py:619
  28.9 1.3 %collective-permute-start.14 = (f32[2,4,16,128]{3,2,1,0:T(8,128)S(1)}, f32[2,4,16,128]{3,2,1,0:T(8,128)S(1)}, u32[]{:S(2)}, u32[]{:S(2)}) collective-permute-start(f32[2,4,16,128]{3,2,1,0:T(8,128)S(1)} %collective-permute-done.12.rest_0_), channel_id=1, source_target_pairs={{0,8},{8,0},{16,24},{24,16},{1,9},{9,1},{17,25},{25,17},{2,10},{10... | collective-permute-start | bytes 196616 | tf_op jit(solution)/shard_map/ppermute | solution.py:619
